TPU v7x, 32 devices: a whole 2x2x4 slice. The times are simulated.
32 devices in a mesh: dp: 4 (over z), row: 2 (over x), col: 4 (over y, core).
Axes of the slice: x: 2, y: 2, z: 4, core: 2. Of those that a mesh axis runs over, the one named last changes fastest.
Arguments:
- block_input: bfloat16 [4096, 768], P(('dp', 'col'), 'row'), may hold values from -6 to 6
- span_end: int32 [4096], P('dp'), may hold values from 0 to 1023, as said below
- encoder_attention_gain: float32 [768], P('row'), may hold values from 0.25 to 1.75
- encoder_attention_bias: float32 [768], P('row'), may hold values from -1.75 to 1.75
- encoder_query_key_value: bfloat16 [768, 3, 768], P('row', None, 'col'), may hold values from -0.21875 to 0.21875
- encoder_output_weight: bfloat16 [768, 768], P('col', 'row'), may hold values from -3.5 to 3.5
- encoder_feedforward_gain: float32 [768], P('row'), may hold values from 0.25 to 1.75
- encoder_feedforward_bias: float32 [768], P('row'), may hold values from -1.75 to 1.75
- encoder_up_weight: bfloat16 [768, 3072], P('row', 'col'), may hold values from -0.21875 to 0.21875
- encoder_down_weight: bfloat16 [3072, 768], P('col', 'row'), may hold values from -0.109375 to 0.109375
- projection: bfloat16 [768, 512], P('row', 'col'), may hold values from -0.21875 to 0.21875
- decoder_attention_gain: float32 [512], P('col'), may hold values from 0.25 to 1.75
- decoder_attention_bias: float32 [512], P('col'), may hold values from -1.75 to 1.75
- decoder_query_key_value: bfloat16 [512, 3, 512], P('col', None, 'row'), may hold values from -0.25 to 0.25
- decoder_output_weight: bfloat16 [512, 512], P('row', 'col'), may hold values from -4 to 4
- decoder_feedforward_gain: float32 [512], P('col'), may hold values from 0.25 to 1.75
- decoder_feedforward_bias: float32 [512], P('col'), may hold values from -1.75 to 1.75
- decoder_up_weight: bfloat16 [512, 2048], P('col', 'row'), may hold values from -0.25 to 0.25
- decoder_down_weight: bfloat16 [2048, 512], P('row', 'col'), may hold values from -0.125 to 0.125
- output_cotangent: bfloat16 [4096, 512], P(('dp', 'row'), 'col'), may hold values from -6 to 6
Outputs:
- encoder_output: float32 [4096, 768], P(('dp', 'col'), 'row')
- decoder_output: float32 [4096, 512], P(('dp', 'row'), 'col')
- input_gradient: float32 [4096, 768], P(('dp', 'col'), 'row')
- grad_encoder_attention_gain: float32 [768], P('row')
- grad_encoder_attention_bias: float32 [768], P('row')
- grad_encoder_query_key_value: float32 [768, 3, 768], P('row', None, 'col')
- grad_encoder_output_weight: float32 [768, 768], P('col', 'row')
- grad_encoder_feedforward_gain: float32 [768], P('row')
- grad_encoder_feedforward_bias: float32 [768], P('row')
- grad_encoder_up_weight: float32 [768, 3072], P('row', 'col')
- grad_encoder_down_weight: float32 [3072, 768], P('col', 'row')
- grad_projection: float32 [768, 512], P('row', 'col')
- grad_decoder_attention_gain: float32 [512], P('col')
- grad_decoder_attention_bias: float32 [512], P('col')
- grad_decoder_query_key_value: float32 [512, 3, 512], P('col', None, 'row')
- grad_decoder_output_weight: float32 [512, 512], P('row', 'col')
- grad_decoder_feedforward_gain: float32 [512], P('col')
- grad_decoder_feedforward_bias: float32 [512], P('col')
- grad_decoder_up_weight: float32 [512, 2048], P('col', 'row')
- grad_decoder_down_weight: float32 [2048, 512], P('row', 'col')
Inputs may be any that keep to these rules, and one draw needn't show every extreme that they name: `span_end`: each aligned block of 512 positions of a sequence holds one image piece of 256 consecutive patches that starts at a place between 0 and 256 of the block; a patch's value is its piece's last position, every other token's value is its own position in its sequence.
All inputs are finite; a program needn't handle non-finite values.
Results may differ from a plain program's by a relative error of at most 0.039.
Values may be sent and summed in bfloat16 or wider, within the bound.
No kernel may reach another device: no remote copies, remote signals or barrier semaphores. Data moves between devices by JAX's collectives and lax.ppermute only.
A program may use at most 128 MiB of HBM per device.

v0:
```python
import functools
import math

import jax
import jax.numpy as jnp
from jax import lax
from jax.experimental import pallas as pl
from jax.experimental.pallas import tpu as pltpu
from jax.sharding import Mesh, PartitionSpec as P

D1 = 768
D2 = 512
HD1 = 64
HD2 = 32
EPSILON = 1e-06
BLOCK = 512
LANES = 128
LOG2E = 1.4426950408889634
SWAP = [(0, 1), (1, 0)]
BF16 = jnp.bfloat16
F32 = jnp.float32


def mm(left, right):
    return jnp.dot(left, right, preferred_element_type=F32)


def mm_nt(left, right):
    return lax.dot_general(left, right, (((1,), (1,)), ((), ())), preferred_element_type=F32)


def mm_tn(left, right):
    return lax.dot_general(left, right, (((0,), (0,)), ((), ())), preferred_element_type=F32)


def head_lanes(head, head_size, rows):
    lane = lax.broadcasted_iota(jnp.int32, (rows, LANES), 1)
    return (lane >= head * head_size) & (lane < (head + 1) * head_size)


def attention_forward_kernel(head_size, q_ref, k_ref, v_ref, limit_ref, out_ref, inv_ref, aug_ref):
    tile = pl.program_id(1)
    rows = q_ref.shape[0]
    heads = LANES // head_size
    per_block = BLOCK // rows
    scale = head_size ** (-0.5) * LOG2E

    @pl.when(tile == 0)
    def _():
        aug_ref[:, :LANES] = v_ref[...]
        aug_ref[:, LANES:] = jnp.ones_like(v_ref)

    def run(block):
        queries = q_ref[...]
        limits = limit_ref[...]
        places = block * BLOCK + lax.broadcasted_iota(jnp.int32, (rows, BLOCK), 1)
        visible = places <= limits
        result = jnp.zeros((rows, LANES), F32)
        inverses = jnp.zeros((rows, LANES), F32)
        for head in range(heads):
            own = head_lanes(head, head_size, rows)
            masked = jnp.where(own, queries, jnp.zeros_like(queries))
            total = jnp.zeros((rows, 2 * LANES), F32)
            for part in range(block + 1):
                span = slice(part * BLOCK, (part + 1) * BLOCK)
                weights = jnp.exp2(mm_nt(masked, k_ref[span, :]) * scale)
                if part == block:
                    weights = jnp.where(visible, weights, 0.0)
                total = total + mm(weights.astype(BF16), aug_ref[span, :])
            inverse = 1.0 / total[:, LANES:]
            result = jnp.where(own, total[:, :LANES] * inverse, result)
            inverses = jnp.where(own, inverse, inverses)
        out_ref[...] = result.astype(BF16)
        inv_ref[...] = inverses

    for block in range(k_ref.shape[0] // BLOCK):
        pl.when(tile // per_block == block)(functools.partial(run, block))


def attention_forward(mixed, limits, head_size):
    length, width = mixed.shape[0], mixed.shape[1] // 3
    groups = width // LANES
    rows = 256
    return pl.pallas_call(
        functools.partial(attention_forward_kernel, head_size),
        out_shape=(
            jax.ShapeDtypeStruct((length, width), BF16),
            jax.ShapeDtypeStruct((length, width), F32),
        ),
        grid=(groups, length // rows),
        in_specs=[
            pl.BlockSpec((rows, LANES), lambda g, t: (t, g)),
            pl.BlockSpec((length, LANES), lambda g, t: (0, groups + g)),
            pl.BlockSpec((length, LANES), lambda g, t: (0, 2 * groups + g)),
            pl.BlockSpec((rows, 1), lambda g, t: (t, 0)),
        ],
        out_specs=[
            pl.BlockSpec((rows, LANES), lambda g, t: (t, g)),
            pl.BlockSpec((rows, LANES), lambda g, t: (t, g)),
        ],
        scratch_shapes=[pltpu.VMEM((length, 2 * LANES), BF16)],
        compiler_params=pltpu.CompilerParams(vmem_limit_bytes=24 << 20),
        cost_estimate=pl.CostEstimate(flops=int(10.5 * COST), bytes_accessed=1, transcendentals=0),
        name="attention_forward",
    )(mixed, mixed, mixed, limits)


def attention_backward_kernel(
    head_size,
    pairs,
    q_ref,
    k_ref,
    v_ref,
    att_ref,
    inv_ref,
    grad_ref,
    limit_ref,
    dq_ref,
    dk_ref,
    dv_ref,
    vaug_ref,
    naug_ref,
    dq_acc,
    dk_acc,
    dv_acc,
):
    step = pl.program_id(1)
    length = q_ref.shape[0]
    heads = LANES // head_size
    scaling = head_size ** (-0.5)

    @pl.when(step == 0)
    def _():
        lane = lax.broadcasted_iota(jnp.int32, (length, LANES), 1)
        vaug_ref[:, :LANES] = v_ref[...]
        vaug_ref[:, LANES:] = jnp.where(lane < 2, 1.0, 0.0).astype(BF16)
        scaled = grad_ref[...] * inv_ref[...]
        terms = scaled * att_ref[...].astype(F32)
        low = scaled.astype(BF16)
        for head in range(heads):
            own = head_lanes(head, head_size, length)
            total = -jnp.sum(jnp.where(own, terms, 0.0), 1, keepdims=True)
            high = total.astype(BF16).astype(F32)
            rest = total - high
            naug_ref[head, :, :LANES] = jnp.where(own, low, jnp.zeros_like(low))
            naug_ref[head, :, LANES:] = jnp.where(
                lane == 0, high, jnp.where(lane == 1, rest, 0.0)
            ).astype(BF16)
        dq_acc[...] = jnp.zeros_like(dq_acc)
        dk_acc[...] = jnp.zeros_like(dk_acc)
        dv_acc[...] = jnp.zeros_like(dv_acc)

    def run(key_block, query_block):
        keys = slice(key_block * BLOCK, (key_block + 1) * BLOCK)
        queries = slice(query_block * BLOCK, (query_block + 1) * BLOCK)
        key_rows = k_ref[keys, :]
        query_rows = q_ref[queries, :]
        key_flipped = key_rows.astype(F32).T.astype(BF16)
        if key_block == query_block:
            places = key_block * BLOCK + lax.broadcasted_iota(jnp.int32, (BLOCK, BLOCK), 0)
            visible = places <= limit_ref[:, queries]
        dq = jnp.zeros((LANES, BLOCK), F32)
        dk = jnp.zeros((BLOCK, LANES), F32)
        dv = jnp.zeros((BLOCK, LANES), F32)
        for head in range(heads):
            own = head_lanes(head, head_size, BLOCK)
            masked = jnp.where(own, query_rows, jnp.zeros_like(query_rows))
            weights = jnp.exp2(mm_nt(key_rows, masked) * (scaling * LOG2E))
            if key_block == query_block:
                weights = jnp.where(visible, weights, 0.0)
            naug = naug_ref[head, queries, :]
            slopes = mm_nt(vaug_ref[keys, :], naug)
            scores = (weights * slopes).astype(BF16)
            dv += mm(weights.astype(BF16), naug[:, :LANES])
            dk += mm(scores, masked)
            row = lax.broadcasted_iota(jnp.int32, (LANES, BLOCK), 0)
            mine = (row >= head * head_size) & (row < (head + 1) * head_size)
            dq += mm(jnp.where(mine, key_flipped, jnp.zeros_like(key_flipped)), scores)
        dq_acc[:, queries] += dq
        dk_acc[keys, :] += dk
        dv_acc[keys, :] += dv

    for number, (key_block, query_block) in enumerate(pairs):
        pl.when(step == number)(functools.partial(run, key_block, query_block))

    @pl.when(step == len(pairs) - 1)
    def _():
        dq_ref[...] = (dq_acc[...].T * scaling).astype(BF16)
        dk_ref[...] = (dk_acc[...] * scaling).astype(BF16)
        dv_ref[...] = dv_acc[...].astype(BF16)


def attention_backward(
    mixed, attended, inverse, grad, limits_row, head_size, start=0, count=None
):
    length, width = attended.shape
    groups = width // LANES
    count = groups if count is None else count
    blocks = length // BLOCK
    pairs = [(k, q) for q in range(blocks) for k in range(q + 1)]
    whole = lambda offset: pl.BlockSpec((length, LANES), lambda g, s: (0, offset + g))
    results = pl.pallas_call(
        functools.partial(attention_backward_kernel, head_size, pairs),
        out_shape=(jax.ShapeDtypeStruct((length, count * LANES), BF16),) * 3,
        grid=(count, len(pairs)),
        in_specs=[
            whole(start),
            whole(groups + start),
            whole(2 * groups + start),
            whole(start),
            whole(start),
            whole(start),
            pl.BlockSpec((1, length), lambda g, s: (0, 0)),
        ],
        out_specs=[whole(0), whole(0), whole(0)],
        scratch_shapes=[
            pltpu.VMEM((length, 2 * LANES), BF16),
            pltpu.VMEM((LANES // head_size, length, 2 * LANES), BF16),
            pltpu.VMEM((LANES, length), F32),
            pltpu.VMEM((length, LANES), F32),
            pltpu.VMEM((length, LANES), F32),
        ],
        compiler_params=pltpu.CompilerParams(vmem_limit_bytes=32 << 20),
        cost_estimate=pl.CostEstimate(
            flops=int(count * (5.2 if head_size == HD1 else 9.6) * COST), bytes_accessed=1, transcendentals=0
        ),
        name="attention_backward",
    )(mixed, mixed, mixed, attended, inverse, grad, limits_row)
    if count == 1:
        return tuple(results)
    return tuple(r[:, g * LANES : (g + 1) * LANES] for g in range(count) for r in results)


def swap(value, axis):
    return lax.ppermute(value, axis, SWAP)


def after(value, *others):
    return lax.optimization_barrier((value, *others))[0]


def near(pack):
    return (swap(pack, "row"), swap(pack, "y"))


def across_by_row(pair, *others):
    return swap(after(pair[0], *others), "y")


def across_by_y(pair, *others):
    return swap(after(pair[1], *others), "row")


def across_both(pair, split, *others):
    first, second = after((pair[0][:split], pair[1][split:]), *others)
    return (swap(first, "y"), swap(second, "row"))


class Parts:
    def __init__(self, refs, start=0, far=None):
        own, by_row, by_y, across = refs
        self.refs = ((own, by_y), (by_row, across))
        self.start = start
        self.far = start if far is None else far

    def rows(self, by_row, by_y, base, count, offset=0):
        start = self.far if by_row and by_y else self.start
        return self.refs[by_row][by_y][pl.ds(start + base + offset, count), :]


class Pair:
    def __init__(self, refs, split):
        own, by_row, by_y, first, second = refs
        self.first = Parts((own, by_row, by_y, first))
        self.second = Parts((own, by_row, by_y, second), split, 0)


COST = 1e7
VMEM = pl.BlockSpec(memory_space=pltpu.VMEM)
SMEM = pl.BlockSpec(memory_space=pltpu.SMEM)


def call(
    kernel, name, outs, args, scratch=(), scalars=0, limit=48, cost=1, needs=(), marks=(), fetch=False
):
    count = len(args)
    arrays = count - scalars
    if needs:
        args = (*args[:scalars], after(args[scalars], *needs), *args[scalars + 1 :])
    scratch = list(scratch)
    if fetch:
        scratch += [pltpu.VMEM(a.shape, a.dtype) for a in args[scalars:]]
        scratch.append(pltpu.SemaphoreType.DMA((arrays,)))

    def body(*refs):
        given, rest = refs[:count], refs[count + len(marks) :]
        if fetch:
            local, semaphores, rest = rest[-arrays - 1 : -1], rest[-1], rest[: -arrays - 1]
            copies = [
                pltpu.make_async_copy(source, target, semaphores.at[i])
                for i, (source, target) in enumerate(zip(given[scalars:], local))
            ]
            for copy in copies:
                copy.start()
            for copy in copies:
                copy.wait()
            given = (*given[:scalars], *local)
        kernel(*given, *rest)

    place = pl.BlockSpec(memory_space=pltpu.HBM) if fetch else VMEM
    return pl.pallas_call(
        body,
        out_shape=outs,
        in_specs=[SMEM] * scalars + [place] * arrays + [VMEM] * len(marks),
        out_specs=jax.tree.map(lambda _: VMEM, outs),
        scratch_shapes=scratch,
        compiler_params=pltpu.CompilerParams(vmem_limit_bytes=limit << 20),
        cost_estimate=pl.CostEstimate(
            flops=int(cost * COST), bytes_accessed=1, transcendentals=0
        ),
        name=name,
    )(*args, *marks)


def marker_kernel(in_ref, out_ref):
    out_ref[...] = in_ref[...]


def marker(value, cost, *others):
    return call(
        marker_kernel,
        "marker",
        jax.ShapeDtypeStruct(value.shape, value.dtype),
        (value,),
        cost=cost,
        limit=4,
        needs=others,
    )


def shaped(rows, columns, kind):
    return jax.ShapeDtypeStruct((rows, columns), kind)


def store_three(ref, base, vectors):
    for tile in range(vectors[0].shape[0]):
        values = jnp.concatenate([v[tile : tile + 1, :] for v in vectors], 0)
        high = values.astype(BF16)
        rest = values - high.astype(F32)
        middle = rest.astype(BF16)
        low = (rest - middle.astype(F32)).astype(BF16)
        ref[base + 16 * tile : base + 16 * (tile + 1), :] = jnp.concatenate(
            [high, middle, low, jnp.zeros_like(high)], 0
        )


def join_three(rows):
    wide = rows.astype(F32)
    return wide[0:4] + wide[4:8] + wide[8:12]


TILE = 256


def lane_roll(values):
    return pltpu.roll(values.astype(F32), LANES // 2, 1)


HALF = LANES // 2
E_ROWS = 3 * LANES
A_LAST = 2 * E_ROWS
A_VEC = 3 * E_ROWS
A_END = A_VEC + 48
B_REST = E_ROWS
B_OUT = B_REST + E_ROWS // 2
B_END = 3 * E_ROWS
E_FEED = 18 * LANES
DA_VEC = 6 * LANES
DA_END = DA_VEC + 32
DB_PROJ = 2 * LANES
DB_END = 8 * LANES
F_COT = 8 * LANES
F_END = 12 * LANES
D_SEND = 19 * LANES + 16


def pack_mixing_kernel(w_ref, out_ref, v1, v2, v3, v4, pack_ref):
    store_three(pack_ref, A_VEC, (v1, v2, v3, v4))
    rows = w_ref.shape[1]
    pack_ref[:rows, :] = w_ref[0, :, :LANES]
    pack_ref[rows : 2 * rows, :] = w_ref[1, :, :LANES]
    pack_ref[A_LAST:A_VEC, :HALF] = w_ref[0, :, LANES:]
    pack_ref[A_LAST:A_VEC, HALF:] = w_ref[1, :, LANES:]
    pack_ref[A_END : A_END + rows, :] = w_ref[2, :, :LANES]
    rest = A_END + B_REST
    pack_ref[rest : rest + rows // 2, :HALF] = w_ref[2, : rows // 2, LANES:]
    pack_ref[rest : rest + rows // 2, HALF:] = w_ref[2, rows // 2 :, LANES:]
    heads = out_ref.shape[0]
    base = A_END + B_OUT
    for tile in range(3):
        pack_ref[base + tile * heads : base + (tile + 1) * heads, :] = out_ref[
            :, tile * LANES : (tile + 1) * LANES
        ]


def pack_encoder_kernel(up_ref, down_ref, mix_ref, first_ref, second_ref):
    for weight_ref, pack_ref in ((up_ref, first_ref), (down_ref, second_ref)):
        rows, columns = weight_ref.shape
        for tile in range(columns // LANES):
            pack_ref[tile * rows : (tile + 1) * rows, :] = weight_ref[
                :, tile * LANES : (tile + 1) * LANES
            ]
    first_ref[E_FEED:, :] = mix_ref[:DA_END, :]
    second_ref[E_FEED:, :] = mix_ref[DA_END:, :]


def pack_decoder_kernel(
    place_ref, mix_ref, out_ref, up_ref, down_ref, v1, v2, v3, v4, proj_ref, cot_ref, keep_ref, send_ref
):
    core = place_ref[0]
    rows = mix_ref.shape[1]
    units = up_ref.shape[1] // 2
    for target, half in ((keep_ref, core), (send_ref, 1 - core)):
        base = 0
        for i in range(3):
            target[base : base + rows, :] = mix_ref[i, :, pl.ds(half * LANES, LANES)]
            base += rows
        target[base : base + LANES, :] = out_ref[pl.ds(half * LANES, LANES), :]
        base += LANES
        for i in range(units // LANES):
            target[base : base + rows, :] = up_ref[:, pl.ds(half * units + i * LANES, LANES)]
            base += rows
        target[base : base + units, :] = down_ref[pl.ds(half * units, units), :]
        base += units
        target[base : base + 3 * LANES, :] = proj_ref[...]
        base += 3 * LANES
        target[base : base + 4 * LANES, :] = cot_ref[...]
        base += 4 * LANES
        store_three(target, base, (v1, v2, v3, v4))


def join_decoder_kernel(place_ref, keep_ref, got_ref, mix_ref, feed_ref):
    core = place_ref[0]
    rows = LANES
    for source, side in ((keep_ref, core), (got_ref, 1 - core)):
        base = 0
        for i in range(3):
            mix_ref[pl.ds(2 * i * rows + side * rows, rows), :] = source[base : base + rows, :]
            base += rows
        mix_ref[pl.ds(DA_END + side * rows, rows), :] = source[base : base + rows, :]
        base += rows
        for i in range(4):
            feed_ref[pl.ds(2 * i * rows + side * rows, rows), :] = source[base : base + rows, :]
            base += rows
        feed_ref[pl.ds(F_END + side * 4 * rows, 4 * rows), :] = source[base : base + 4 * rows, :]
        base += 4 * rows
        mix_ref[pl.ds(DA_END + DB_PROJ + side * 3 * rows, 3 * rows), :] = source[
            base : base + 3 * rows, :
        ]
        base += 3 * rows
        for start in (F_COT, F_END + F_COT):
            feed_ref[pl.ds(start + side * 2 * rows, 2 * rows), :] = source[base : base + 2 * rows, :]
            base += 2 * rows
        mix_ref[pl.ds(DA_VEC + side * 16, 16), :] = source[base : base + 16, :]


def join_input_kernel(place_ref, own, by_row, by_y, first, second, out_ref):
    y = place_ref[3]
    width = own.shape[1]
    split = second.shape[0]
    for right, by_y_side, sources in (
        (0, 0, (own, own)),
        (1, 0, (by_row, by_row)),
        (0, 1, (by_y, by_y)),
        (1, 1, (first, second)),
    ):
        base = (y if by_y_side == 0 else 1 - y) * 2 * split
        for number, source in enumerate(sources):
            start = 0 if source is second else number * first.shape[0]
            at = pl.ds(base + number * split, split)
            out_ref[at, right * width : (right + 1) * width] = source[start : start + split, :]


def norm_rows(values):
    width = values.shape[1]
    average = jnp.sum(values, 1, keepdims=True) / width
    variance = jnp.sum(values * values, 1, keepdims=True) / width - average * average
    inverse = lax.rsqrt(variance + EPSILON)
    return ((values - average) * inverse, inverse)


def first_norm_kernel(core_ref, own, other, vec_own, vec_other, x_ref, normed_ref, vec_ref):
    core = core_ref[0]
    for side, source in ((0, vec_own), (3, vec_other)):
        for tile in range(3):
            vec_ref[:, (side + tile) * LANES : (side + tile + 1) * LANES] = join_three(
                source[A_VEC + 16 * tile : A_VEC + 16 * (tile + 1), :]
            )
    rows = own.shape[0] // 2
    gain, bias = vec_ref[0:1, :], vec_ref[1:2, :]
    for source, place in ((own, core), (other, 1 - core)):
        for y in range(2):
            values = source[y * rows : (y + 1) * rows, :]
            target = pl.ds((2 * y + place) * rows, rows)
            x_ref[target, :] = values
            centred, _ = norm_rows(values.astype(F32))
            normed_ref[target, :] = (centred * gain + bias).astype(BF16)


def encoder_mixing_kernel(normed_ref, *refs):
    pair = Pair(refs[:5], A_END)
    first, second = pair.first, pair.second
    mixed_ref, weight_ref, out_ref = refs[5:8]
    out_ref[...] = encoder_out_rows(second)
    rows = E_ROWS
    low = lax.broadcasted_iota(jnp.int32, (rows, LANES), 1) < HALF
    for half in range(2):
        at = slice(half * rows, (half + 1) * rows)
        for kind, parts, base in ((0, first, 0), (1, first, rows), (2, second, 0)):
            for group, side in ((0, 0), (2, 1)):
                tile = (3 * kind + group) * LANES
                weight_ref[at, tile : tile + LANES] = parts.rows(half, side, base, rows)
        mine = first.rows(half, 0, A_LAST, rows).astype(F32)
        theirs = first.rows(half, 1, A_LAST, rows).astype(F32)
        weight_ref[at, LANES : 2 * LANES] = jnp.where(low, mine, lane_roll(theirs)).astype(BF16)
        weight_ref[at, 4 * LANES : 5 * LANES] = jnp.where(low, lane_roll(mine), theirs).astype(BF16)
        mine = second.rows(half, 0, B_REST, rows // 2).astype(F32)
        theirs = second.rows(half, 1, B_REST, rows // 2).astype(F32)
        mine = jnp.concatenate([mine, lane_roll(mine)], 0)
        theirs = jnp.concatenate([lane_roll(theirs), theirs], 0)
        weight_ref[at, 7 * LANES : 8 * LANES] = jnp.where(low, mine, theirs).astype(BF16)

    @pl.loop(0, normed_ref.shape[0] // TILE)
    def _(tile):
        at = pl.ds(tile * TILE, TILE)
        mixed_ref[at, :] = mm(normed_ref[at, :], weight_ref[...]).astype(BF16)


def encoder_out_rows(parts):
    heads = 3 * LANES // 2
    sides = [
        jnp.concatenate(
            [parts.rows(i, j, B_OUT + t * heads, heads) for i in range(2) for t in range(3)], 1
        )
        for j in range(2)
    ]
    return jnp.concatenate([sides[0], sides[1][LANES:], sides[1][:LANES]], 0)


def decoder_out_rows(parts):
    return jnp.concatenate(
        [
            jnp.concatenate(
                [parts.rows(i, j, t * LANES, LANES) for j in range(2) for t in range(2)], 1
            )
            for i in range(2)
        ],
        0,
    )


def attend_kernel(
    head_size, mixed_ref, limit_ref, weight_ref, attended_ref, inverse_ref, partial_ref, aug_ref
):
    length, width = attended_ref.shape
    groups, heads = width // LANES, LANES // head_size
    scale = head_size ** (-0.5) * LOG2E
    for group in range(groups):
        at = (2 * groups + group) * LANES
        aug_ref[group, :, :LANES] = mixed_ref[:, at : at + LANES]
        aug_ref[group, :, LANES:] = jnp.ones((length, LANES), BF16)

    for block in range(length // BLOCK):

        @pl.loop(0, BLOCK // TILE)
        def _(step):
            at = pl.ds(block * BLOCK + step * TILE, TILE)
            limits = limit_ref[at, :]
            places = block * BLOCK + lax.broadcasted_iota(jnp.int32, (TILE, BLOCK), 1)
            visible = places <= limits

            @pl.loop(0, groups)
            def _(group):
                queries = mixed_ref[at, pl.ds(group * LANES, LANES)]
                result = jnp.zeros((TILE, LANES), F32)
                inverses = jnp.zeros((TILE, LANES), F32)
                for head in range(heads):
                    own = head_lanes(head, head_size, TILE)
                    masked = jnp.where(own, queries, jnp.zeros_like(queries))
                    total = jnp.zeros((TILE, 2 * LANES), F32)
                    for part in range(block + 1):
                        span = slice(part * BLOCK, (part + 1) * BLOCK)
                        keys = mixed_ref[span, pl.ds((groups + group) * LANES, LANES)]
                        weights = jnp.exp2(mm_nt(masked, keys) * scale)
                        if part == block:
                            weights = jnp.where(visible, weights, 0.0)
                        total = total + mm(weights.astype(BF16), aug_ref[group, span, :])
                    inverse = 1.0 / total[:, LANES:]
                    result = jnp.where(own, total[:, :LANES] * inverse, result)
                    inverses = jnp.where(own, inverse, inverses)
                lanes = pl.ds(group * LANES, LANES)
                attended_ref[at, lanes] = result.astype(BF16)
                inverse_ref[at, lanes] = inverses

            partial_ref[at, :] = mm(attended_ref[at, :], weight_ref[...]).astype(BF16)


def gelu_pair(values):
    area = 0.5 * (1.0 + lax.erf(values * (0.5**0.5)))
    slope = area + values * jnp.exp2(values * values * (-0.5 * LOG2E)) * (0.5 / math.pi) ** 0.5
    return (values * area, slope)


class Feed:
    def __init__(self, up_parts, down_parts, decoder):
        self.up_parts = up_parts
        self.down_parts = down_parts
        self.decoder = decoder
        self.features = 2 * LANES if decoder else 3 * LANES
        self.units = 4 * LANES if decoder else 6 * LANES
        self.down = 0
        self.chunks = self.units // (2 * LANES)

    def rows(self, parts, feature, unit, base, count, offset):
        if self.decoder:
            return parts.rows(unit, feature, base, count, offset)
        return parts.rows(feature, unit, base, count, offset)

    def up_chunk(self, unit, chunk):
        f = self.features
        return jnp.concatenate(
            [
                jnp.concatenate(
                    [
                        self.rows(
                            self.up_parts, i, unit, 0, f, pl.multiple_of((2 * chunk + t) * f, f)
                        )
                        for t in range(2)
                    ],
                    1,
                )
                for i in range(2)
            ],
            0,
        )

    def down_chunk(self, unit, chunk):
        return jnp.concatenate(
            [
                self.rows(
                    self.down_parts,
                    i,
                    unit,
                    self.down + t * self.units,
                    2 * LANES,
                    pl.multiple_of(chunk * 2 * LANES, 2 * LANES),
                )
                for i in range(2)
                for t in range(self.features // LANES)
            ],
            1,
        )


def feed_forward_kernel(stream_ref, mine_ref, got_ref, vec_ref, *refs):
    middle_ref, normed_ref, active_ref, slope_ref, partial_ref, total_ref = refs[8:14]
    feed = Feed(Parts(refs[:4]), Parts(refs[4:8]), False)
    gain, bias = vec_ref[2:3, :], vec_ref[3:4, :]

    @pl.loop(0, stream_ref.shape[0] // TILE)
    def _(tile):
        at = pl.ds(tile * TILE, TILE)
        middle = stream_ref[at, :].astype(F32) + (
            mine_ref[at, :].astype(F32) + got_ref[at, :].astype(F32)
        )
        middle_ref[at, :] = middle
        centred, _ = norm_rows(middle)
        normed_ref[at, :] = (centred * gain + bias).astype(BF16)
        total_ref[...] = jnp.zeros_like(total_ref)

        @pl.loop(0, feed.chunks)
        def _(chunk):
            for unit in range(2):
                hidden = mm(normed_ref[at, :], feed.up_chunk(unit, chunk))
                active, slope = gelu_pair(hidden)
                lanes = pl.ds(unit * feed.units + chunk * 2 * LANES, 2 * LANES)
                low = active.astype(BF16)
                active_ref[at, lanes] = low
                slope_ref[at, lanes] = slope.astype(BF16)
                total_ref[...] += mm(low, feed.down_chunk(unit, chunk))

        partial_ref[at, :] = total_ref[...].astype(BF16)


def decoder_feed_kernel(
    place_ref, stream_ref, mine_ref, got_ref, vec_ref, *refs
):
    middle_ref, normed_ref, active_ref, hidden_ref, partial_ref, cot_ref, total_ref = refs[5:12]
    pair = Pair(refs[:5], F_END)
    first, second = pair.first, pair.second
    row = place_ref[2]
    for i in range(2):
        for number, parts in enumerate((first, second)):
            at = pl.ds((row if i == 0 else 1 - row) * 4 * LANES + number * 2 * LANES, 2 * LANES)
            for tile in range(4):
                cot_ref[at, tile * LANES : (tile + 1) * LANES] = parts.rows(
                    i, tile // 2, F_COT + (tile % 2) * 2 * LANES, 2 * LANES
                )
    feed = Feed(first, second, True)
    gain, bias = vec_ref[2:3, :], vec_ref[3:4, :]

    @pl.loop(0, stream_ref.shape[0] // TILE)
    def _(tile):
        at = pl.ds(tile * TILE, TILE)
        middle = stream_ref[at, :] + (mine_ref[at, :].astype(F32) + got_ref[at, :].astype(F32))
        middle_ref[at, :] = middle
        centred, _ = norm_rows(middle)
        normed_ref[at, :] = (centred * gain + bias).astype(BF16)
        total_ref[...] = jnp.zeros_like(total_ref)

        @pl.loop(0, feed.chunks)
        def _(chunk):
            for unit in range(2):
                upward = feed.up_chunk(unit, chunk)
                hidden = mm(normed_ref[at, :], upward)
                active, slope = gelu_pair(hidden)
                lanes = pl.ds(unit * feed.units + chunk * 2 * LANES, 2 * LANES)
                active_ref[at, lanes] = active.astype(BF16)
                grad = mm_nt(cot_ref[at, :], feed.down_chunk(unit, chunk))
                low = (grad * slope).astype(BF16)
                hidden_ref[at, lanes] = low
                total_ref[...] += mm_nt(low, upward)

        partial_ref[at, :] = total_ref[...].astype(BF16)


def bridge_kernel(place_ref, middle_ref, mine_ref, got_ref, *refs):
    (
        out_ref, low_ref, stream_ref, normed_ref, mixed_ref, weight_ref, vec_ref, mixing_ref,
        back_ref,
    ) = refs[8:17]
    block = place_ref[1]
    first, second = Parts(refs[:4], E_FEED), Parts(refs[4:8], E_FEED)
    back_ref[...] = decoder_out_rows(second)
    rows = E_ROWS
    for j in range(2):
        for c in range(2):
            tile = (2 * j + c) * LANES
            for i in range(2):
                weight_ref[i * rows : (i + 1) * rows, tile : tile + LANES] = second.rows(
                    i, j, DB_PROJ + c * rows, rows
                )
            vec_ref[:, tile : tile + LANES] = join_three(first.rows(0, j, DA_VEC + 16 * c, 16))
    for kind in range(3):
        for i in range(2):
            tile = (2 * kind + i) * LANES
            for j in range(2):
                mixing_ref[2 * j * LANES : 2 * (j + 1) * LANES, tile : tile + LANES] = first.rows(
                    i, j, 2 * kind * LANES, 2 * LANES
                )
    gain, bias = vec_ref[0:1, :], vec_ref[1:2, :]
    width = low_ref.shape[1]

    @pl.loop(0, middle_ref.shape[0] // TILE)
    def _(tile):
        at = pl.ds(tile * TILE, TILE)
        total = middle_ref[at, :] + (mine_ref[at, :].astype(F32) + got_ref[at, :].astype(F32))
        low = total.astype(BF16)

        @pl.when(tile == block)
        def _():
            out_ref[...] = total[:, :width]

        low_ref[at, :] = low[:, :width]
        stream = mm(low, weight_ref[...])
        stream_ref[at, :] = stream
        centred, _ = norm_rows(stream)
        normed = (centred * gain + bias).astype(BF16)
        normed_ref[at, :] = normed
        mixed_ref[at, :] = mm(normed, mixing_ref[...]).astype(BF16)


def norm_back(incoming, centred, inverse, gain):
    width = incoming.shape[1]
    scaled = incoming * gain
    first = jnp.sum(scaled, 1, keepdims=True) / width
    second = jnp.sum(scaled * centred, 1, keepdims=True) / width
    return inverse * (scaled - first - centred * second)


def store_sums(sums_ref, incoming, centred):
    sums_ref[0:1, :] = jnp.sum(incoming * centred, 0, keepdims=True)
    sums_ref[1:2, :] = jnp.sum(incoming, 0, keepdims=True)


def own_sums(place_ref, tile, sums_ref, incoming, centred):
    half = TILE // 2

    @pl.when((tile == place_ref[1]) & (place_ref[2] == 0))
    def _():
        store_sums(sums_ref, incoming[:half], centred[:half])

    @pl.when((tile == place_ref[1]) & (place_ref[2] == 1))
    def _():
        store_sums(sums_ref, incoming[half:], centred[half:])


def middle_back_kernel(
    place_ref, mine_ref, got_ref, middle_ref, grad_ref, vec_ref, weight_ref,
    total_ref, low_ref, attended_ref, sums_ref,
):
    gain = vec_ref[2:3, :]
    width = low_ref.shape[1]

    @pl.loop(0, middle_ref.shape[0] // TILE)
    def _(tile):
        at = pl.ds(tile * TILE, TILE)
        incoming = mine_ref[at, :].astype(F32) + got_ref[at, :].astype(F32)
        centred, inverse = norm_rows(middle_ref[at, :])
        total = grad_ref[at, :].astype(F32) + norm_back(incoming, centred, inverse, gain)
        total_ref[at, :] = total
        low = total.astype(BF16)
        low_ref[at, :] = low[:, :width]
        attended_ref[at, :] = mm_nt(low, weight_ref[...])
        own_sums(place_ref, tile, sums_ref, incoming, centred)


def mixed_low(refs, at):
    kinds = len(refs) // 3
    return jnp.concatenate([refs[3 * g + i][at, :] for i in range(3) for g in range(kinds)], 1)


def mixed_back_kernel(*refs):
    lows, weight_ref, partial_ref = refs[:-2], refs[-2], refs[-1]

    @pl.loop(0, partial_ref.shape[0] // TILE)
    def _(tile):
        at = pl.ds(tile * TILE, TILE)
        partial_ref[at, :] = mm_nt(mixed_low(lows, at), weight_ref[...]).astype(BF16)


def mixed_last_kernel(place_ref, *refs):
    core, y = place_ref[0], place_ref[3]
    lows, weight_ref, keep_ref, send_ref = refs[:-3], refs[-3], refs[-2], refs[-1]
    for target, side in ((keep_ref, core), (send_ref, 1 - core)):
        at = pl.ds((2 * y + side) * TILE, TILE)
        target[...] = mm_nt(mixed_low(lows, at), weight_ref[...]).astype(BF16)


def bridge_back_kernel(
    place_ref, mine_ref, got_ref, stream_ref, grad_ref, vec_ref, proj_ref,
    low_ref, encoder_ref, down_ref, sums_ref,
):
    gain = vec_ref[0:1, :]

    @pl.loop(0, stream_ref.shape[0] // TILE)
    def _(tile):
        at = pl.ds(tile * TILE, TILE)
        incoming = mine_ref[at, :].astype(F32) + got_ref[at, :].astype(F32)
        centred, inverse = norm_rows(stream_ref[at, :])
        grad = grad_ref[at, :] + norm_back(incoming, centred, inverse, gain)
        own_sums(place_ref, tile, sums_ref, incoming, centred)
        low = grad.astype(BF16)
        low_ref[at, :] = low
        encoder = mm_nt(low, proj_ref[...])
        encoder_ref[at, :] = encoder
        down_ref[at, :] = encoder.astype(BF16)


def feed_back_kernel(down_ref, slope_ref, *refs):
    hidden_ref, partial_ref, total_ref = refs[8:11]
    feed = Feed(Parts(refs[:4]), Parts(refs[4:8]), False)

    @pl.loop(0, down_ref.shape[0] // TILE)
    def _(tile):
        at = pl.ds(tile * TILE, TILE)
        total_ref[...] = jnp.zeros_like(total_ref)

        @pl.loop(0, feed.chunks)
        def _(chunk):
            for unit in range(2):
                lanes = pl.ds(unit * feed.units + chunk * 2 * LANES, 2 * LANES)
                back = mm_nt(down_ref[at, :], feed.down_chunk(unit, chunk))
                hidden = (back * slope_ref[at, lanes].astype(F32)).astype(BF16)
                hidden_ref[at, lanes] = hidden
                total_ref[...] += mm_nt(hidden, feed.up_chunk(unit, chunk))

        partial_ref[at, :] = total_ref[...].astype(BF16)


def input_back_kernel(place_ref, mine_ref, got_ref, x_ref, grad_ref, vec_ref, out_ref, sums_ref):
    at = pl.ds(place_ref[1] * TILE, TILE)
    incoming = mine_ref[...].astype(F32) + got_ref[...].astype(F32)
    centred, inverse = norm_rows(x_ref[at, :].astype(F32))
    total = grad_ref[at, :] + norm_back(incoming, centred, inverse, vec_ref[0:1, :])
    out_ref[...] = total[:, : out_ref.shape[1]]
    own_sums(place_ref, place_ref[1], sums_ref, incoming, centred)


def store_tiles(ref, base, value):
    rows = value.shape[0]
    for tile in range(value.shape[1] // LANES):
        ref[base + tile * rows : base + (tile + 1) * rows, :] = value[
            :, tile * LANES : (tile + 1) * LANES
        ].astype(BF16)


G_LAST = 3 * E_ROWS
G_REST = 4 * E_ROWS
G_OUT = G_REST + E_ROWS // 2
G_END = 6 * E_ROWS
GA_UP = 8 * LANES
GA_END = 16 * LANES
GB_OUT = 6 * LANES
GB_PROJ = 8 * LANES
GB_END = 11 * LANES


def feed_grads_kernel(active_ref, cot_ref, normed_ref, hidden_ref, pack_ref):
    units, features = 4 * LANES, 2 * LANES
    store_tiles(pack_ref, 0, mm_tn(active_ref[:, :units], cot_ref[:, :features]))
    store_tiles(pack_ref, GA_UP, mm_tn(normed_ref[:, :features], hidden_ref[:, :units]))


def mixing_grads_kernel(
    place_ref, normed_ref, q_ref, k_ref, v_ref, attended_ref, middle_ref, encoder_ref, proj_ref, pack_ref
):
    lows = jnp.concatenate([q_ref[:, :LANES], k_ref[:, :LANES], v_ref[:, :LANES]], 1)
    store_tiles(pack_ref, 0, mm_tn(normed_ref[:, : 2 * LANES], lows))
    store_tiles(pack_ref, GB_OUT, mm_tn(attended_ref[:, :LANES], middle_ref[...]))
    own = proj_ref[:, pl.ds(place_ref[0] * LANES, LANES)]
    store_tiles(pack_ref, GB_PROJ, mm_tn(encoder_ref[...], own))


def product_kernel(left_ref, right_ref, out_ref):
    rows, columns = out_ref.shape
    out_ref[...] = mm_tn(left_ref[:, :rows], right_ref[:, :columns]).astype(BF16)


def encoder_grads_kernel(
    normed_ref, q_ref, k_ref, v_ref, q2_ref, k2_ref, v2_ref, attended_ref, middle_ref, pack_ref
):
    low = lax.broadcasted_iota(jnp.int32, q2_ref.shape, 1) < HALF
    last = jnp.where(low, q2_ref[...].astype(F32), lane_roll(k2_ref[...])).astype(BF16)
    lows = jnp.concatenate([q_ref[...], k_ref[...], v_ref[...], last, v2_ref[...]], 1)
    grads = mm_tn(normed_ref[:, :E_ROWS], lows)
    store_tiles(pack_ref, 0, grads[:, : 4 * LANES])
    rest = grads[:, 4 * LANES :]
    half = E_ROWS // 2
    low = lax.broadcasted_iota(jnp.int32, (half, LANES), 1) < HALF
    pack_ref[G_REST:G_OUT, :] = jnp.where(low, rest[:half], lane_roll(rest[half:])).astype(BF16)
    grads = mm_tn(attended_ref[:, : 2 * LANES], middle_ref[...])
    store_tiles(pack_ref, G_OUT, grads[:half])


def encoder_unpack_kernel(pack_ref, mixing_ref, out_ref):
    rows, half = E_ROWS, E_ROWS // 2
    for kind in range(3):
        mixing_ref[kind, :, :LANES] = pack_ref[kind * rows : (kind + 1) * rows, :].astype(F32)
    last = pack_ref[G_LAST:G_REST, :].astype(F32)
    mixing_ref[0, :, LANES:] = last[:, :HALF]
    mixing_ref[1, :, LANES:] = last[:, HALF:]
    rest = pack_ref[G_REST:G_OUT, :].astype(F32)
    mixing_ref[2, :half, LANES:] = rest[:, :HALF]
    mixing_ref[2, half:, LANES:] = rest[:, HALF:]
    for tile in range(3):
        at = slice(G_OUT + tile * half, G_OUT + (tile + 1) * half)
        out_ref[:, tile * LANES : (tile + 1) * LANES] = pack_ref[at, :].astype(F32)


def decoder_send_kernel(place_ref, feed_ref, mix_ref, send_ref):
    other = 1 - place_ref[0]
    rows = LANES
    send_ref[: 4 * rows, :] = feed_ref[pl.ds(other * 4 * rows, 4 * rows), :]
    for tile in range(4):
        send_ref[(4 + tile) * rows : (5 + tile) * rows, :] = feed_ref[
            pl.ds(GA_UP + 2 * tile * rows + other * rows, rows), :
        ]
    for tile in range(3):
        send_ref[(8 + tile) * rows : (9 + tile) * rows, :] = mix_ref[
            pl.ds(2 * tile * rows + other * rows, rows), :
        ]
    send_ref[11 * rows : 12 * rows, :] = mix_ref[pl.ds(GB_OUT + other * rows, rows), :]


def decoder_unpack_kernel(
    place_ref, feed_ref, mix_ref, got_ref, mixing_ref, out_ref, up_ref, down_ref, proj_ref
):
    core = place_ref[0]
    rows = LANES
    units = 4 * rows
    down_ref[pl.ds(core * units, units), :] = feed_ref[pl.ds(core * units, units), :].astype(F32)
    down_ref[pl.ds((1 - core) * units, units), :] = got_ref[:units, :].astype(F32)
    for tile in range(4):
        up_ref[:, pl.ds(core * units + tile * rows, rows)] = feed_ref[
            pl.ds(GA_UP + 2 * tile * rows + core * rows, rows), :
        ].astype(F32)
        up_ref[:, pl.ds((1 - core) * units + tile * rows, rows)] = got_ref[
            (4 + tile) * rows : (5 + tile) * rows, :
        ].astype(F32)
    for tile in range(3):
        mixing_ref[tile, :, pl.ds(core * rows, rows)] = mix_ref[
            pl.ds(2 * tile * rows + core * rows, rows), :
        ].astype(F32)
        mixing_ref[tile, :, pl.ds((1 - core) * rows, rows)] = got_ref[
            (8 + tile) * rows : (9 + tile) * rows, :
        ].astype(F32)
    out_ref[pl.ds(core * rows, rows), :] = mix_ref[pl.ds(GB_OUT + core * rows, rows), :].astype(F32)
    out_ref[pl.ds((1 - core) * rows, rows), :] = got_ref[11 * rows : 12 * rows, :].astype(F32)
    proj_ref[...] = mix_ref[GB_PROJ:GB_END, :].astype(F32)


def line_first(value, size):
    if size == 4:
        return (value, lax.ppermute(value, "dp", [(0, 1), (3, 2)]))
    if size & (size - 1):
        return lax.psum(value, "dp")
    distance = 1
    while distance < size:
        got = lax.ppermute(value, "dp", [(i, i ^ distance) for i in range(size)])
        value = (value.astype(F32) + got.astype(F32)).astype(BF16)
        distance *= 2
    return value


def line_next(state, size, pairs, *others):
    if size != 4:
        return state
    mine, got = after(state, *others)
    total = (mine.astype(F32) + got.astype(F32)).astype(BF16)
    return (total, lax.ppermute(total, "dp", pairs))


def line_across(state, size, *others):
    return line_next(state, size, [(1, 2), (2, 1)], *others)


def line_back(state, size, *others):
    return line_next(state, size, [(1, 0), (2, 3)], *others)


def line_last(state, size, *others):
    if size != 4:
        return state
    mine, got = after(state, *others)
    place = lax.axis_index("dp")
    return jnp.where((place == 0) | (place == 3), got, mine)


def dp_sum(value, size):
    place = lax.axis_index("dp")
    terms = [value] + [
        lax.ppermute(value, "dp", [(i, (i + step) % size) for i in range(size)])
        for step in range(1, size)
    ]
    terms = terms[::-1]
    return jnp.sum(lax.dynamic_slice_in_dim(jnp.stack(terms + terms), size - 1 - place, size, 0), 0)


def per_device(
    data_size,
    block_input,
    span_end,
    encoder_attention_gain,
    encoder_attention_bias,
    encoder_query_key_value,
    encoder_output_weight,
    encoder_feedforward_gain,
    encoder_feedforward_bias,
    encoder_up_weight,
    encoder_down_weight,
    projection,
    decoder_attention_gain,
    decoder_attention_bias,
    decoder_query_key_value,
    decoder_output_weight,
    decoder_feedforward_gain,
    decoder_feedforward_bias,
    decoder_up_weight,
    decoder_down_weight,
    output_cotangent,
):
    row = lax.axis_index("row").astype(jnp.int32)
    y = lax.axis_index("y").astype(jnp.int32)
    core = lax.axis_index("core").astype(jnp.int32)
    length = span_end.shape[0]
    own_rows, width = block_input.shape
    block = 2 * y + core
    place = jnp.stack([core, block, row, y])
    limits = span_end.reshape(length, 1)
    limits_row = span_end.reshape(1, length)
    full = 2 * width
    low_full = 4 * LANES
    units = 2 * encoder_up_weight.shape[1]
    d_units = decoder_up_weight.shape[1]
    features = 2 * LANES

    half = own_rows // 2
    x_near = near(block_input)
    tick = jnp.zeros((8, LANES), F32)
    row_of = lambda vector: vector.reshape(-1, LANES)
    keep, send = call(
        pack_decoder_kernel,
        "pack_decoder",
        (shaped(D_SEND, LANES, BF16),) * 2,
        (
            place,
            jnp.transpose(decoder_query_key_value, (1, 0, 2)),
            decoder_output_weight,
            decoder_up_weight,
            decoder_down_weight,
            row_of(decoder_attention_gain),
            row_of(decoder_attention_bias),
            row_of(decoder_feedforward_gain),
            row_of(decoder_feedforward_bias),
            projection,
            output_cotangent,
        ),
        scalars=1,
        limit=56,
        fetch=True,
    )
    m_pack = call(
        pack_mixing_kernel,
        "pack_mixing",
        shaped(A_END + B_END, LANES, BF16),
        (
            jnp.transpose(encoder_query_key_value, (1, 0, 2)),
            encoder_output_weight,
            row_of(encoder_attention_gain),
            row_of(encoder_attention_bias),
            row_of(encoder_feedforward_gain),
            row_of(encoder_feedforward_bias),
        ),
        limit=56,
        fetch=True,
        needs=(x_near, keep),
    )
    m_near = near(m_pack)
    d_got = swap(send, "core")
    dm_pack, f_pack = call(
        join_decoder_kernel,
        "join_decoder",
        (shaped(DA_END + DB_END, LANES, BF16), shaped(2 * F_END, LANES, BF16)),
        (place, keep, d_got),
        scalars=1,
        limit=8,
    )
    up, down = call(
        pack_encoder_kernel,
        "pack_encoder",
        (shaped(E_FEED + DA_END, LANES, BF16), shaped(E_FEED + DB_END, LANES, BF16)),
        (encoder_up_weight, encoder_down_weight, dm_pack),
        limit=56,
        fetch=True,
    )
    x_far = across_both(x_near, half, up)
    m_far = across_both(m_near, A_END, x_far)
    sides = call(
        join_input_kernel,
        "join_input",
        shaped(2 * own_rows, full, BF16),
        (place, block_input, *x_near, *x_far),
        scalars=1,
        limit=56,
        fetch=True,
        needs=(m_near,),
    )
    m_parts = (m_pack, *m_near, *m_far)
    up_near, down_near = near(after(up, sides)), near(after(down, sides))
    mark = marker(tick, 5000, m_far)
    stream, normed_first, e_vec = call(
        first_norm_kernel,
        "first_norm",
        (shaped(length, full, BF16), shaped(length, full, BF16), shaped(4, full, F32)),
        (place, sides, swap(sides, "core"), m_pack, m_near[0]),
        scalars=1,
        limit=8,
        marks=(mark,),
    )
    mixed, e_mixing, e_out = call(
        encoder_mixing_kernel,
        "encoder_mixing",
        (
            shaped(length, 9 * LANES, BF16),
            shaped(full, 9 * LANES, BF16),
            shaped(E_ROWS, full, BF16),
        ),
        (normed_first, *m_parts),
        limit=12,
        cost=3,
    )
    attended, inverse, partial = call(
        functools.partial(attend_kernel, HD1),
        "encoder_attend",
        (
            shaped(length, E_ROWS, BF16),
            shaped(length, E_ROWS, F32),
            shaped(length, full, BF16),
        ),
        (mixed, limits, e_out),
        (pltpu.VMEM((3, length, 2 * LANES), BF16),),
        limit=16,
        cost=12,
    )
    got = swap(partial, "core")
    up_parts = (up, *up_near, across_by_row(up_near, attended, down_near))
    down_parts = (down, *down_near, across_by_y(down_near, attended, up_near))
    f_near = near(after(f_pack, down_near))
    mark = marker(tick, 10000, up_parts[1:], down_parts[1:])
    middle, normed_second, active, slope, partial = call(
        feed_forward_kernel,
        "feed_forward",
        (
            shaped(length, full, F32),
            shaped(length, full, BF16),
            shaped(length, units, BF16),
            shaped(length, units, BF16),
            shaped(length, full, BF16),
        ),
        (stream, partial, got, e_vec, *up_parts, *down_parts),
        (pltpu.VMEM((TILE, full), F32),),
        limit=16,
        cost=12,
        marks=(mark,),
    )
    mark = marker(tick, 10000, middle)
    (
        own_encoder_out, encoder_low, d_stream, d_normed_first, d_mixed, proj_weight, d_vec, d_mixing,
        d_out,
    ) = call(
        bridge_kernel,
        "bridge",
        (
            shaped(own_rows, width, F32),
            shaped(length, width, BF16),
            shaped(length, low_full, F32),
            shaped(length, low_full, BF16),
            shaped(length, 6 * LANES, BF16),
            shaped(full, low_full, BF16),
            shaped(4, low_full, F32),
            shaped(low_full, 6 * LANES, BF16),
            shaped(2 * LANES, low_full, BF16),
        ),
        (place, middle, partial, swap(partial, "core"), *up_parts, *down_parts),
        scalars=1,
        limit=12,
        marks=(mark,),
        cost=5.7,
    )

    d_attended, d_inverse, partial = call(
        functools.partial(attend_kernel, HD2),
        "decoder_attend",
        (
            shaped(length, 2 * LANES, BF16),
            shaped(length, 2 * LANES, F32),
            shaped(length, low_full, BF16),
        ),
        (d_mixed, limits, d_out),
        (pltpu.VMEM((2, length, 2 * LANES), BF16),),
        limit=16,
        cost=11,
    )
    f_parts = (f_pack, *f_near, *across_both(f_near, F_END, d_mixed))
    d_middle, d_normed_second, d_active, d_hidden, partial, cotangent = call(
        decoder_feed_kernel,
        "decoder_feed",
        (
            shaped(length, low_full, F32),
            shaped(length, low_full, BF16),
            shaped(length, d_units, BF16),
            shaped(length, d_units, BF16),
            shaped(length, low_full, BF16),
            shaped(length, low_full, BF16),
        ),
        (place, d_stream, partial, swap(partial, "core"), d_vec, *f_parts),
        (pltpu.VMEM((TILE, low_full), F32),),
        scalars=1,
        limit=16,
        cost=8,
    )

    got = swap(partial, "core")
    grads_a = call(
        feed_grads_kernel,
        "decoder_feed_grads",
        shaped(GA_END, LANES, BF16),
        (after(d_active, partial), cotangent, d_normed_second, d_hidden),
        limit=8,
        cost=0.8,
    )
    sum_a = line_first(grads_a, data_size)
    d_middle_grad, d_middle_low, attended_grad, d_second_sums = call(
        middle_back_kernel,
        "decoder_middle_back",
        (
            shaped(length, low_full, F32),
            shaped(length, features, BF16),
            shaped(length, 2 * LANES, F32),
            shaped(2, low_full, F32),
        ),
        (place, after(partial, grads_a), got, d_middle, cotangent, d_vec, d_out),
        scalars=1,
        limit=12,
        cost=2.6,
    )
    d_lows = attention_backward(
        d_mixed, d_attended, d_inverse, attended_grad, limits_row, HD2, 0, 1
    )
    sum_a = line_across(sum_a, data_size, d_lows)
    d_lows = d_lows + attention_backward(
        d_mixed, d_attended, d_inverse, after(attended_grad, sum_a[0]), limits_row, HD2, 1, 1
    )
    sum_a = line_back(sum_a, data_size, d_lows)
    partial = call(
        mixed_back_kernel,
        "decoder_mixed_back",
        shaped(length, low_full, BF16),
        (after(d_lows[0], sum_a[0]), *d_lows[1:], d_mixing),
        limit=12,
        cost=1.6,
    )
    got = swap(partial, "core")

    proj_low, encoder_grad, down_low, d_first_sums = call(
        bridge_back_kernel,
        "bridge_back",
        (
            shaped(length, low_full, BF16),
            shaped(length, full, F32),
            shaped(length, full, BF16),
            shaped(2, low_full, F32),
        ),
        (place, partial, got, d_stream, d_middle_grad, d_vec, proj_weight),
        scalars=1,
        limit=12,
        cost=3.9,
    )
    grads_c = call(
        product_kernel,
        "encoder_down_grads",
        shaped(units // 2, width, BF16),
        (active, down_low),
        limit=8,
        cost=1,
    )
    sum_c = line_first(grads_c, data_size)
    grads_b = call(
        mixing_grads_kernel,
        "decoder_mixing_grads",
        shaped(GB_END, LANES, BF16),
        (
            place, d_normed_first, *d_lows[:3], d_attended, d_middle_low, encoder_low,
            after(proj_low, grads_c),
        ),
        scalars=1,
        limit=8,
        cost=1.3,
    )
    sum_b = line_first(grads_b, data_size)
    hidden_low, partial = call(
        feed_back_kernel,
        "feed_back",
        (shaped(length, units, BF16), shaped(length, full, BF16)),
        (after(down_low, grads_b), slope, *up_parts, *down_parts),
        (pltpu.VMEM((TILE, full), F32),),
        limit=16,
        cost=12,
    )
    got = swap(partial, "core")
    sum_c = line_across(sum_c, data_size, partial)
    grads_e = call(
        product_kernel,
        "encoder_up_grads",
        shaped(width, units // 2, BF16),
        (normed_second, after(hidden_low, sum_c[0])),
        limit=8,
        cost=1000,
    )
    sum_e = line_first(grads_e, data_size)
    middle_grad, middle_low, attended_grad, second_sums = call(
        middle_back_kernel,
        "encoder_middle_back",
        (
            shaped(length, full, F32),
            shaped(length, width, BF16),
            shaped(length, 3 * LANES, F32),
            shaped(2, full, F32),
        ),
        (place, after(partial, grads_e), got, middle, encoder_grad, e_vec, e_out),
        scalars=1,
        limit=12,
        cost=5.5,
    )
    first = attention_backward(
        mixed, attended, inverse, attended_grad, limits_row, HD1, 0, 1
    )
    sum_c = line_back(sum_c, data_size, first)
    sum_b = line_across(sum_b, data_size, first)
    sum_e = line_across(sum_e, data_size, first)
    second = attention_backward(
        mixed,
        attended,
        inverse,
        after(attended_grad, sum_c[0], sum_b[0], sum_e[0], sum_a),
        limits_row,
        HD1,
        1,
        1,
    )
    grads_d = call(
        encoder_grads_kernel,
        "encoder_mixing_grads",
        shaped(G_END, LANES, BF16),
        (normed_first, *first, *second, attended, middle_low),
        limit=12,
        cost=1.1,
    )
    sum_d = line_first(grads_d, data_size)
    sum_e = line_back(sum_e, data_size, grads_d)
    third = attention_backward(
        mixed, attended, inverse, after(attended_grad, grads_d, sum_c, sum_e[0]), limits_row, HD1, 2, 1
    )
    sum_d = line_across(sum_d, data_size, third)
    lows = (*first, *second, after(third[0], sum_d[0]), *third[1:])
    keep, send = call(
        mixed_last_kernel,
        "encoder_mixed_back",
        (shaped(own_rows, full, BF16),) * 2,
        (place, *lows, e_mixing),
        scalars=1,
        limit=12,
        cost=1.8,
    )
    got = swap(send, "core")
    sum_b = line_back(sum_b, data_size, send)
    own_input_grad, first_sums = call(
        input_back_kernel,
        "input_back",
        (shaped(own_rows, width, F32), shaped(2, full, F32)),
        (place, after(keep, sum_b[0]), got, stream, middle_grad, e_vec),
        scalars=1,
        limit=8,
        cost=1.8,
    )

    def in_order(value, index):
        half = value.shape[1] // 2
        return jnp.where(index == 0, value, jnp.concatenate([value[:, half:], value[:, :half]], 1))

    e_sums = in_order(jnp.concatenate([first_sums, second_sums], 0), row)
    d_sums = in_order(jnp.concatenate([d_first_sums, d_second_sums], 0), y)
    sums = jnp.concatenate([e_sums, jnp.pad(d_sums, ((0, 0), (0, full - low_full)))], 0)
    sums = jnp.sum(lax.all_gather(sums, ("row", "y", "core")), 0)
    sum_d = line_back(sum_d, data_size, sums)
    sums = dp_sum(after(sums, sum_d[0]), data_size)
    e_sums = lax.dynamic_slice_in_dim(sums[:4], row * width, width, 1)
    share = decoder_attention_gain.shape[0]
    d_sums = lax.dynamic_slice_in_dim(sums[4:], block * share, share, 1)

    own, by_row = after(f_parts[:2], sum_d[0])
    out_rows, out_columns = output_cotangent.shape
    active_rows = lax.dynamic_slice_in_dim(d_active, row * out_rows, out_rows, 0)
    half = d_units // 2
    span = F_END + half
    down = jnp.concatenate(
        [jnp.concatenate([p[F_END:span], p[span : span + half]], 1) for p in (own, by_row)], 0
    )
    last = mm(active_rows, down)
    mine = lax.dynamic_slice_in_dim(last, core * out_columns, out_columns, 1)
    others = lax.dynamic_slice_in_dim(last, (1 - core) * out_columns, out_columns, 1)
    own_decoder_out = (
        lax.dynamic_slice(d_middle, (row * out_rows, core * out_columns), (out_rows, out_columns))
        + mine
        + swap(others.astype(BF16), "core").astype(F32)
    )

    grads_a = line_last(sum_a, data_size, own_input_grad)
    grads_b = line_last(sum_b, data_size, sum_d[0])
    send = call(
        decoder_send_kernel,
        "decoder_send",
        shaped(12 * LANES, LANES, BF16),
        (place, grads_a, grads_b),
        scalars=1,
        limit=8,
    )
    d_mixing_grad, d_out_grad, d_up_grad, d_down_grad, proj_grad = call(
        decoder_unpack_kernel,
        "decoder_unpack",
        (
            jax.ShapeDtypeStruct((3, LANES, 2 * LANES), F32),
            shaped(2 * LANES, LANES, F32),
            shaped(LANES, d_units, F32),
            shaped(d_units, LANES, F32),
            shaped(width, LANES, F32),
        ),
        (place, grads_a, grads_b, swap(send, "core")),
        scalars=1,
        limit=8,
        cost=1.9,
    )
    grads_c = line_last(sum_c, data_size, sum_d[0]).astype(F32)
    grads_e = line_last(sum_e, data_size, sum_d[0]).astype(F32)
    grads_d = line_last(sum_d, data_size, d_down_grad, grads_c, grads_e)
    mixing_grad, out_grad = call(
        encoder_unpack_kernel,
        "encoder_unpack",
        (
            jax.ShapeDtypeStruct((3, width, width // 2), F32),
            shaped(width // 2, width, F32),
        ),
        (grads_d,),
        limit=8,
    )
    return (
        own_encoder_out,
        own_decoder_out,
        own_input_grad,
        e_sums[0],
        e_sums[1],
        jnp.transpose(mixing_grad, (1, 0, 2)),
        out_grad,
        e_sums[2],
        e_sums[3],
        grads_e,
        grads_c,
        proj_grad,
        d_sums[0],
        d_sums[1],
        jnp.transpose(d_mixing_grad, (1, 0, 2)),
        d_out_grad,
        d_sums[2],
        d_sums[3],
        d_up_grad,
        d_down_grad,
    )


def solution(mesh):
    data, row, col = (mesh.shape[name] for name in ("dp", "row", "col"))
    split = Mesh(mesh.devices.reshape(data, row, col // 2, 2), ("dp", "row", "y", "core"))
    c = ("y", "core")
    in_specs = (
        P(("dp", *c), "row"),
        P("dp"),
        P("row"),
        P("row"),
        P("row", None, c),
        P(c, "row"),
        P("row"),
        P("row"),
        P("row", c),
        P(c, "row"),
        P("row", c),
        P(c),
        P(c),
        P(c, None, "row"),
        P("row", c),
        P(c),
        P(c),
        P(c, "row"),
        P("row", c),
        P(("dp", "row"), c),
    )
    out_specs = (
        P(("dp", *c), "row"),
        P(("dp", "row"), c),
        P(("dp", *c), "row"),
        P("row"),
        P("row"),
        P("row", None, c),
        P(c, "row"),
        P("row"),
        P("row"),
        P("row", c),
        P(c, "row"),
        P("row", c),
        P(c),
        P(c),
        P(c, None, "row"),
        P("row", c),
        P(c),
        P(c),
        P(c, "row"),
        P("row", c),
    )
    return jax.shard_map(
        functools.partial(per_device, data),
        mesh=split,
        in_specs=in_specs,
        out_specs=out_specs,
        check_vma=False,
    )
```

profile of v0, /device:TPU:0, one launch (start us, length us, event | category | flops | bytes accessed | tf_op | source)
XLA Modules:
  0.0 318.8 jit_solution(105222845560110205)
XLA Ops:
  0.7 3.0 collective-permute-start
  3.7 1.5 collective-permute-start.1
  5.8 3.2 %pack_decoder.1 = (bf16[2448,128]{1,0:T(8,128)(2,1)}, bf16[2448,128]{1,0:T(8,128)(2,1)}) custom-call(s32[4]{0:T(128)} %pad_add_fusion.refs_0_, bf16[3,128,256]{2,1,0:T(8,128)(2,1)} %bitcast.48, bf16[256,128]{1,0:T(8,128)(2,1)} %refs_2_.1, bf16[128,1024]{1,0:T(8,128)(2,1)} %refs_3_.1, bf16[1024,128]{1,0:T(8,128)(2,1)} %refs_4_.1, f32[1,128]{1,0:T(1,128)} %bitcast.53, ...), custom_call_target="tpu_custom_call" | custom-call | flops 10000000 | bytes 1 | tf_op jit(solution)/shard_map/pack_decoder/pallas_call | solution.py:311
  9.1 2.1 copy.46
  11.2 2.2 pack_mixing.1.refs_3_.refs_1_
  14.6 1.5 join_decoder.1
  16.9 2.8 pack_encoder.1
  19.7 1.6 collective-permute-start.5
  21.4 1.5 collective-permute-start.6
  22.9 7.3 %collective-permute-done.2.refs_4_.refs_2_ = bf16[2352,128]{1,0:T(8,128)(2,1)S(1)} collective-permute-done((bf16[2352,128]{1,0:T(8,128)(2,1)}, bf16[2352,128]{1,0:T(8,128)(2,1)S(1)}, u32[]{:S(2)}, u32[]{:S(2)}) %collective-permute-start.2) | collective-permute-done | bytes 602144 | tf_op jit(solution)/shard_map/ppermute | solution.py:235
  32.5 1.6 collective-permute-start.9
  34.4 2.9 join_input.1.refs_1_
  37.8 1.7 collective-permute-start.12
  39.5 1.7 collective-permute-done.9.refs_5_
  42.5 2.4 collective-permute-start.13
  46.2 1.7 first_norm.1
  48.0 3.5 %encoder_mixing.1 = (bf16[1024,1152]{1,0:T(8,128)(2,1)S(1)}, bf16[768,1152]{1,0:T(8,128)(2,1)S(1)}, bf16[384,768]{1,0:T(8,128)(2,1)S(1)}) custom-call(bf16[1024,768]{1,0:T(8,128)(2,1)S(1)} %get-tuple-element.171.refs_0_, bf16[2352,128]{1,0:T(8,128)(2,1)S(1)} %copy-done.11, bf16[2352,128]{1,0:T(8,128)(2,1)S(1)} %collective-permute-done.2.refs_4_.refs_2_, ...), custom_call_target="tpu_custom_call" | custom-call | flops 30000000 | bytes 1 | tf_op jit(solution)/shard_map/encoder_mixing/pallas_call | solution.py:311
  52.7 11.3 %encoder_attend.1 = (bf16[1024,384]{1,0:T(8,128)(2,1)S(1)}, f32[1024,384]{1,0:T(8,128)S(1)}, bf16[1024,768]{1,0:T(8,128)(2,1)S(1)}) custom-call(bf16[1024,1152]{1,0:T(8,128)(2,1)S(1)} %get-tuple-element.172.refs_0_.q_ref.k_ref.v_ref, s32[1024,1]{1,0:T(8,128)S(1)} %copy.47.refs_1_, bf16[384,768]{1,0:T(8,128)(2,1)S(1)} %get-tuple-element.173.refs_2_.refs_6_), custom_call_target="tpu_custom_call" | custom-call | flops 120000000 | bytes 1 | tf_op jit(solution)/shard_map/encoder_attend/pallas_call | solution.py:311
  64.1 12.1 %collective-permute-done.14.refs_10_.refs_8_ = bf16[3328,128]{1,0:T(8,128)(2,1)S(1)} collective-permute-done((bf16[3328,128]{1,0:T(8,128)(2,1)S(1)}, bf16[3328,128]{1,0:T(8,128)(2,1)S(1)}, u32[]{:S(2)}, u32[]{:S(2)}) %collective-permute-start.14) | collective-permute-done | bytes 852000 | tf_op jit(solution)/shard_map/ppermute | solution.py:235
  76.1 1.5 collective-permute-start.16
  77.7 1.5 collective-permute-start.15
  80.2 18.1 %collective-permute-done.15.refs_7_.refs_5_ = bf16[3104,128]{1,0:T(8,128)(2,1)S(1)} collective-permute-done((bf16[3104,128]{1,0:T(8,128)(2,1)S(1)}, bf16[3104,128]{1,0:T(8,128)(2,1)S(1)}, u32[]{:S(2)}, u32[]{:S(2)}) %collective-permute-start.15) | collective-permute-done | bytes 794656 | tf_op jit(solution)/shard_map/ppermute | solution.py:235
  98.4 13.3 %feed_forward.1 = (f32[1024,768]{1,0:T(8,128)S(1)}, bf16[1024,768]{1,0:T(8,128)(2,1)S(1)}, bf16[1024,1536]{1,0:T(8,128)(2,1)S(1)}, bf16[1024,1536]{1,0:T(8,128)(2,1)S(1)}, bf16[1024,768]{1,0:T(8,128)(2,1)S(1)}) custom-call(bf16[1024,768]{1,0:T(8,128)(2,1)S(1)} %get-tuple-element.170.refs_0_.refs_3_, bf16[1024,768]{1,0:T(8,128)(2,1)S(1)} %get-tuple-element.174.refs_1_, ...), custom_call_target="tpu_custom_call" | custom-call | flops 120000000 | bytes 1 | tf_op jit(solution)/shard_map/feed_forward/pallas_call | solution.py:311
  111.8 1.5 copy-done.15
  115.2 6.1 %bridge.1 = (f32[256,384]{1,0:T(8,128)}, bf16[1024,384]{1,0:T(8,128)(2,1)S(1)}, f32[1024,512]{1,0:T(8,128)S(1)}, bf16[1024,512]{1,0:T(8,128)(2,1)S(1)}, bf16[102...) custom-call(s32[4]{0:T(128)S(1)} %copy-done.48, ...), custom_call_target="tpu_custom_call" | custom-call | flops 57000000 | bytes 1 | tf_op jit(solution)/shard_map/bridge/pallas_call | solution.py:311
  121.3 11.0 %decoder_attend.1 = (bf16[1024,256]{1,0:T(8,128)(2,1)S(1)}, f32[1024,256]{1,0:T(8,128)S(1)}, bf16[1024,512]{1,0:T(8,128)(2,1)S(1)}) custom-call(bf16[1024,768]{1,0:T(8,128)(2,1)S(1)} %get-tuple-element.188.refs_0_.q_ref.k_ref.v_ref, s32[1024,1]{1,0:T(8,128)S(1)} %copy.47.refs_1_, bf16[256,512]{1,0:T(8,128)(2,1)S(1)} %get-tuple-element.189.refs_2_.refs_6_), custom_call_target="tpu_custom_call" | custom-call | flops 110000000 | bytes 1 | tf_op jit(solution)/shard_map/decoder_attend/pallas_call | solution.py:311
  134.6 1.6 collective-permute-start.21
  137.4 8.6 %collective-permute-done.21.refs_8_ = bf16[1536,128]{1,0:T(8,128)(2,1)S(1)} collective-permute-done((bf16[1536,128]{1,0:T(8,128)(2,1)S(1)}, bf16[1536,128]{1,0:T(8,128)(2,1)S(1)}, u32[]{:S(2)}, u32[]{:S(2)}) %collective-permute-start.21) | collective-permute-done | bytes 393248 | tf_op jit(solution)/shard_map/ppermute | solution.py:235
  147.3 9.6 %decoder_feed.1 = (f32[1024,512]{1,0:T(8,128)S(1)}, bf16[1024,512]{1,0:T(8,128)(2,1)S(1)}, bf16[1024,1024]{1,0:T(8,128)(2,1)S(1)}, bf16[1024,1024]{1,0:T(8,128)(...) custom-call(s32[4]{0:T(128)S(1)} %copy-done.48, ...), custom_call_target="tpu_custom_call" | custom-call | flops 80000000 | bytes 1 | tf_op jit(solution)/shard_map/decoder_feed/pallas_call | solution.py:311
  158.3 3.5 %collective-permute-start.24 = (bf16[2048,128]{1,0:T(8,128)(2,1)S(1)}, bf16[2048,128]{1,0:T(8,128)(2,1)S(1)}, u32[]{:S(2)}, u32[]{:S(2)}) collective-permute-start(bf16[2048,128]{1,0:T(8,128)(2,1)S(1)} %decoder_feed_grads.1), channel_id=1, source_target_pairs={{0,8},{24,16},{1,9},{25,17},{2,10},{26,18},{3,11},{27,19},{4,12},{... | collective-permute-start | bytes 1572872 | tf_op jit(solution)/shard_map/ppermute | solution.py:1015
  161.8 3.2 %decoder_middle_back.1 = (f32[1024,512]{1,0:T(8,128)S(1)}, bf16[1024,256]{1,0:T(8,128)(2,1)S(1)}, f32[1024,256]{1,0:T(8,128)S(1)}, f32[2,512]{1,0:T(2,128)S(1)}) custom-call(s32[4]{0:T(128)S(1)} %copy-done.48, bf16[1024,512]{1,0:T(8,128)(2,1)S(1)} %get-tuple-element.206.refs_1_, bf16[1024,512]{1,0:T(8,128)(2,1)S(1)} %collective-permute-done.23.refs_2_, ...), custom_call_target="tpu_custom_call" | custom-call | flops 26000000 | bytes 1 | tf_op jit(solution)/shard_map/decoder_middle_back/pallas_call | solution.py:311
  165.0 9.4 %attention_backward.5 = (bf16[1024,128]{1,0:T(8,128)(2,1)S(1)}, bf16[1024,128]{1,0:T(8,128)(2,1)S(1)}, bf16[1024,128]{1,0:T(8,128)(2,1)S(1)}) custom-call(bf16[1024,768]{1,0:T(8,128)(2,1)S(1)} %get-tuple-element.188.refs_0_.q_ref.k_ref.v_ref, bf16[1024,768]{1,0:T(8,128)(2,1)S(1)} %get-tuple-element.188.refs_0_.q_ref.k_ref.v_ref, ...), custom_call_target="tpu_custom_call" | custom-call | flops 96000000 | bytes 1 | tf_op jit(solution)/shard_map/attention_backward/pallas_call | solution.py:202
  175.3 9.6 %attention_backward.6 = (bf16[1024,128]{1,0:T(8,128)(2,1)S(1)}, bf16[1024,128]{1,0:T(8,128)(2,1)S(1)}, bf16[1024,128]{1,0:T(8,128)(2,1)S(1)}) custom-call(bf16[1024,768]{1,0:T(8,128)(2,1)S(1)} %get-tuple-element.188.refs_0_.q_ref.k_ref.v_ref, bf16[1024,768]{1,0:T(8,128)(2,1)S(1)} %get-tuple-element.188.refs_0_.q_ref.k_ref.v_ref, ...), custom_call_target="tpu_custom_call" | custom-call | flops 96000000 | bytes 1 | tf_op jit(solution)/shard_map/attention_backward/pallas_call | solution.py:202
  186.2 1.6 decoder_mixed_back.1.refs_1_
  187.9 2.6 collective-permute-done.26.refs_2_
  190.5 3.9 %bridge_back.1 = (bf16[1024,512]{1,0:T(8,128)(2,1)S(1)}, f32[1024,768]{1,0:T(8,128)S(1)}, bf16[1024,768]{1,0:T(8,128)(2,1)S(1)}, f32[2,512]{1,0:T(2,128)S(1)}) custom-call(s32[4]{0:T(128)S(1)} %copy-done.48, bf16[1024,512]{1,0:T(8,128)(2,1)S(1)} %decoder_mixed_back.1.refs_1_, bf16[1024,512]{1,0:T(8,128)(2,1)S(1)} %collective-permute-done.26.refs_2_, ...), custom_call_target="tpu_custom_call" | custom-call | flops 39000000 | bytes 1 | tf_op jit(solution)/shard_map/bridge_back/pallas_call | solution.py:311
  195.4 6.6 %collective-permute-start.27 = (bf16[768,384]{1,0:T(8,128)(2,1)S(1)}, bf16[768,384]{1,0:T(8,128)(2,1)S(1)}, u32[]{:S(2)}, u32[]{:S(2)}) collective-permute-start(bf16[768,384]{1,0:T(8,128)(2,1)S(1)} %encoder_down_grads.1), channel_id=1, source_target_pairs={{0,8},{24,16},{1,9},{25,17},{2,10},{26,18},{3,11},{27,19},{4,12},{... | collective-permute-start | bytes 1769480 | tf_op jit(solution)/shard_map/ppermute | solution.py:1015
  204.0 11.8 %feed_back.1 = (bf16[1024,1536]{1,0:T(8,128)(2,1)S(1)}, bf16[1024,768]{1,0:T(8,128)(2,1)S(1)}) custom-call(bf16[1024,768]{1,0:T(8,128)(2,1)S(1)} %get-tuple-element.230.refs_1_.refs_0_, bf16[1024,1536]{1,0:T(8,128)(2,1)S(1)} %copy-done.16, bf16[3104,128]{1,0:T(8,128)(2,1)} %get-tuple-element.176.refs_4_.refs_2_, ...), custom_call_target="tpu_custom_call" | custom-call | flops 120000000 | bytes 1 | tf_op jit(solution)/shard_map/feed_back/pallas_call | solution.py:311
  218.0 2.3 collective-permute-start.31
  221.0 4.1 %collective-permute-start.30 = (bf16[1408,128]{1,0:T(8,128)(2,1)S(1)}, bf16[1408,128]{1,0:T(8,128)(2,1)S(1)}, u32[]{:S(2)}, u32[]{:S(2)}) collective-permute-start(bf16[1408,128]{1,0:T(8,128)(2,1)S(1)} %decoder_mixing_grads.1), channel_id=1, source_target_pairs={{0,8},{24,16},{1,9},{25,17},{2,10},{26,18},{3,11},{27,19},{4,12},{... | collective-permute-start | bytes 1081352 | tf_op jit(solution)/shard_map/ppermute | solution.py:1015
  226.5 4.0 %encoder_middle_back.1 = (f32[1024,768]{1,0:T(8,128)S(1)}, bf16[1024,384]{1,0:T(8,128)(2,1)S(1)}, f32[1024,384]{1,0:T(8,128)S(1)}, f32[2,768]{1,0:T(2,128)S(1)}) custom-call(s32[4]{0:T(128)S(1)} %copy-done.48, bf16[1024,768]{1,0:T(8,128)(2,1)S(1)} %get-tuple-element.238.refs_1_, bf16[1024,768]{1,0:T(8,128)(2,1)S(1)} %collective-permute-done.28.refs_2_, ...), custom_call_target="tpu_custom_call" | custom-call | flops 55000000 | bytes 1 | tf_op jit(solution)/shard_map/encoder_middle_back/pallas_call | solution.py:311
  230.5 1.7 copy-done.12
  232.2 5.2 %attention_backward.7 = (bf16[1024,128]{1,0:T(8,128)(2,1)S(1)}, bf16[1024,128]{1,0:T(8,128)(2,1)S(1)}, bf16[1024,128]{1,0:T(8,128)(2,1)S(1)}) custom-call(bf16[1024,1152]{1,0:T(8,128)(2,1)S(1)} %copy-done.1, bf16[1024,1152]{1,0:T(8,128)(2,1)S(1)} %copy-done.1, bf16[1024,1152]{1,0:T(8,128)(2,1)S(1)} %copy-done.1, ...), custom_call_target="tpu_custom_call" | custom-call | flops 52000000 | bytes 1 | tf_op jit(solution)/shard_map/attention_backward/pallas_call | solution.py:202
  237.4 2.7 collective-permute-done.30
  241.0 1.5 collective-permute-start.35
  245.6 5.6 %attention_backward.8 = (bf16[1024,128]{1,0:T(8,128)(2,1)S(1)}, bf16[1024,128]{1,0:T(8,128)(2,1)S(1)}, bf16[1024,128]{1,0:T(8,128)(2,1)S(1)}) custom-call(bf16[1024,1152]{1,0:T(8,128)(2,1)S(1)} %copy-done.1, bf16[1024,1152]{1,0:T(8,128)(2,1)S(1)} %copy-done.1, bf16[1024,1152]{1,0:T(8,128)(2,1)S(1)} %copy-done.1, ...), custom_call_target="tpu_custom_call" | custom-call | flops 52000000 | bytes 1 | tf_op jit(solution)/shard_map/attention_backward/pallas_call | solution.py:202
  251.3 1.9 encoder_mixing_grads.1
  253.3 8.1 %collective-permute-start.33 = (bf16[2304,128]{1,0:T(8,128)(2,1)}, bf16[2304,128]{1,0:T(8,128)(2,1)}, u32[]{:S(2)}, u32[]{:S(2)}) collective-permute-start(bf16[2304,128]{1,0:T(8,128)(2,1)} %encoder_mixing_grads.1), channel_id=1, source_target_pairs={{0,8},{24,16},{1,9},{25,17},{2,10},{26,18},{3,11},{27,19},{4,12},{... | collective-permute-start | bytes 1769480 | tf_op jit(solution)/shard_map/ppermute | solution.py:1015
  262.2 1.4 add_convert_fusion.2
  263.6 1.4 copy-done.5
  265.0 5.2 %attention_backward.9 = (bf16[1024,128]{1,0:T(8,128)(2,1)S(1)}, bf16[1024,128]{1,0:T(8,128)(2,1)S(1)}, bf16[1024,128]{1,0:T(8,128)(2,1)S(1)}) custom-call(bf16[1024,1152]{1,0:T(8,128)(2,1)S(1)} %copy-done.1, bf16[1024,1152]{1,0:T(8,128)(2,1)S(1)} %copy-done.1, bf16[1024,1152]{1,0:T(8,128)(2,1)S(1)} %copy-done.1, ...), custom_call_target="tpu_custom_call" | custom-call | flops 52000000 | bytes 1 | tf_op jit(solution)/shard_map/attention_backward/pallas_call | solution.py:202
  270.3 1.4 collective-permute-done.33
  271.6 1.4 add_convert_fusion.1
  273.8 1.5 collective-permute-start.46
  275.4 1.8 encoder_mixed_back.1
  278.9 1.9 input_back.1
  280.8 9.0 %all-gather = f32[64,768]{1,0:T(8,128)S(1)} all-gather(f32[8,768]{1,0:T(8,128)S(1)} %select_maximum_fusion), channel_id=2, replica_groups=mesh['dp'=4,'row'=2,'y'=2,'core'=2] {'row','y','core'}, dimensions={0}, use_global_device_ids=true | all-gather | bytes 221184 | tf_op jit(solution)/shard_map/all_gather | solution.py:1455
  291.4 1.4 collective-permute-start.40
  292.8 4.3 %collective-permute-start.41 = (f32[8,768]{1,0:T(8,128)S(1)}, f32[8,768]{1,0:T(8,128)S(1)}, u32[]{:S(2)}, u32[]{:S(2)}) collective-permute-start(f32[8,768]{1,0:T(8,128)S(1)} %bitcast_reduce_fusion), channel_id=1, source_target_pairs={{0,16},{8,24},{16,0},{24,8},{1,17},{9,25},{17,1},{25,9},{2,18},{10... | collective-permute-start | bytes 73736 | tf_op jit(solution)/shard_map/ppermute | solution.py:1053
  297.1 1.6 collective-permute-start.42
  300.5 2.3 select_convert_fusion.1
  304.5 7.1 %collective-permute-done.40 = f32[8,768]{1,0:T(8,128)S(1)} collective-permute-done((f32[8,768]{1,0:T(8,128)S(1)}, f32[8,768]{1,0:T(8,128)S(1)}, u32[]{:S(2)}, u32[]{:S(2)}) %collective-permute-start.40) | collective-permute-done | bytes 24608 | tf_op jit(solution)/shard_map/ppermute | solution.py:1053
  312.9 1.7 convert_add_fusion
  314.6 1.9 decoder_unpack.1
  (235 shorter events, 43.5 us)
Async XLA Ops:
  0.7 10.6 %collective-permute-start = (bf16[256,384]{1,0:T(8,128)(2,1)}, bf16[256,384]{1,0:T(8,128)(2,1)S(1)}, u32[]{:S(2)}, u32[]{:S(2)}) collective-permute-start(bf16[256,384]{1,0:T(8,128)(2,1)} %refs_1_.4), channel_id=1, source_target_pairs={{0,4},{4,0},{1,5},{5,1},{2,6},{6,2},{3,7},{7,3},{8,12},{12,8},{9,1... | collective-permute-start | bytes 589832 | tf_op jit(solution)/shard_map/ppermute | solution.py:235
  3.7 7.6 %collective-permute-start.1 = (bf16[256,384]{1,0:T(8,128)(2,1)}, bf16[256,384]{1,0:T(8,128)(2,1)S(1)}, u32[]{:S(2)}, u32[]{:S(2)}) collective-permute-start(bf16[256,384]{1,0:T(8,128)(2,1)} %refs_1_.4), channel_id=1, source_target_pairs={{0,2},{2,0},{1,3},{3,1},{4,6},{6,4},{5,7},{7,5},{8,10},{10,8},{9,1... | collective-permute-start | bytes 589832 | tf_op jit(solution)/shard_map/ppermute | solution.py:235
  9.0 5.6 %collective-permute-start.4 = (bf16[2448,128]{1,0:T(8,128)(2,1)}, bf16[2448,128]{1,0:T(8,128)(2,1)S(1)}, u32[]{:S(2)}, u32[]{:S(2)}) collective-permute-start(bf16[2448,128]{1,0:T(8,128)(2,1)} %get-tuple-element.162), channel_id=1, source_target_pairs={{0,1},{1,0},{2,3},{3,2},{4,5},{5,4},{6,7},{7,6},{8,9},{9,8},{10,11... | collective-permute-start | bytes 1880072 | tf_op jit(solution)/shard_map/ppermute | solution.py:235
  13.5 16.7 %collective-permute-start.2 = (bf16[2352,128]{1,0:T(8,128)(2,1)}, bf16[2352,128]{1,0:T(8,128)(2,1)S(1)}, u32[]{:S(2)}, u32[]{:S(2)}) collective-permute-start(bf16[2352,128]{1,0:T(8,128)(2,1)} %pack_mixing.1.refs_3_.refs_1_), channel_id=1, source_target_pairs={{0,4},{4,0},{1,5},{5,1},{2,6},{6,2},{3,7},{7,3},{8,12},{12,8},{9,1... | collective-permute-start | bytes 1806344 | tf_op jit(solution)/shard_map/ppermute | solution.py:235
  14.1 16.8 %collective-permute-start.3 = (bf16[2352,128]{1,0:T(8,128)(2,1)}, bf16[2352,128]{1,0:T(8,128)(2,1)S(1)}, u32[]{:S(2)}, u32[]{:S(2)}) collective-permute-start(bf16[2352,128]{1,0:T(8,128)(2,1)} %pack_mixing.1.refs_3_.refs_1_), channel_id=1, source_target_pairs={{0,2},{2,0},{1,3},{3,1},{4,6},{6,4},{5,7},{7,5},{8,10},{10,8},{9,1... | collective-permute-start | bytes 1806344 | tf_op jit(solution)/shard_map/ppermute | solution.py:235
  16.9 17.2 %copy-start.44 = (s32[1024]{0:T(1024)S(1)}, s32[1024]{0:T(1024)}, u32[]{:S(2)}) copy-start(s32[1024]{0:T(1024)} %param.21) | copy-start | bytes 12292
  19.7 21.4 %copy-start.6 = (bf16[3328,128]{1,0:T(8,128)(2,1)S(1)}, bf16[3328,128]{1,0:T(8,128)(2,1)}, u32[]{:S(2)}) copy-start(bf16[3328,128]{1,0:T(8,128)(2,1)} %get-tuple-element.179.refs_8_.refs_6_) | copy-start | bytes 2555908
  19.7 12.3 %collective-permute-start.5 = (bf16[128,384]{1,0:T(8,128)(2,1)S(1)}, bf16[128,384]{1,0:T(8,128)(2,1)S(1)}, u32[]{:S(2)}, u32[]{:S(2)}) collective-permute-start(bf16[128,384]{1,0:T(8,128)(2,1)S(1)} %slice.96), channel_id=1, source_target_pairs={{0,2},{2,0},{1,3},{3,1},{4,6},{6,4},{5,7},{7,5},{8,10},{10,8},{9,1... | collective-permute-start | bytes 294920 | tf_op jit(solution)/shard_map/ppermute | solution.py:235
  21.4 10.7 %collective-permute-start.6 = (bf16[128,384]{1,0:T(8,128)(2,1)S(1)}, bf16[128,384]{1,0:T(8,128)(2,1)S(1)}, u32[]{:S(2)}, u32[]{:S(2)}) collective-permute-start(bf16[128,384]{1,0:T(8,128)(2,1)S(1)} %slice.97), channel_id=1, source_target_pairs={{0,4},{4,0},{1,5},{5,1},{2,6},{6,2},{3,7},{7,3},{8,12},{12,8},{9,1... | collective-permute-start | bytes 294920 | tf_op jit(solution)/shard_map/ppermute | solution.py:235
  32.1 10.4 %collective-permute-start.8 = (bf16[1200,128]{1,0:T(8,128)(2,1)}, bf16[1200,128]{1,0:T(8,128)(2,1)S(1)}, u32[]{:S(2)}, u32[]{:S(2)}) collective-permute-start(bf16[1200,128]{1,0:T(8,128)(2,1)} %slice.98), channel_id=1, source_target_pairs={{0,2},{2,0},{1,3},{3,1},{4,6},{6,4},{5,7},{7,5},{8,10},{10,8},{9,1... | collective-permute-start | bytes 921608 | tf_op jit(solution)/shard_map/ppermute | solution.py:235
  32.5 8.7 %collective-permute-start.9 = (bf16[1152,128]{1,0:T(8,128)(2,1)}, bf16[1152,128]{1,0:T(8,128)(2,1)S(1)}, u32[]{:S(2)}, u32[]{:S(2)}) collective-permute-start(bf16[1152,128]{1,0:T(8,128)(2,1)} %slice.99), channel_id=1, source_target_pairs={{0,4},{4,0},{1,5},{5,1},{2,6},{6,2},{3,7},{7,3},{8,12},{12,8},{9,1... | collective-permute-start | bytes 884744 | tf_op jit(solution)/shard_map/ppermute | solution.py:235
  37.3 7.7 %collective-permute-start.7 = (bf16[512,768]{1,0:T(8,128)(2,1)}, bf16[512,768]{1,0:T(8,128)(2,1)S(1)}, u32[]{:S(2)}, u32[]{:S(2)}) collective-permute-start(bf16[512,768]{1,0:T(8,128)(2,1)} %join_input.1.refs_1_), channel_id=1, source_target_pairs={{0,1},{1,0},{2,3},{3,2},{4,5},{5,4},{6,7},{7,6},{8,9},{9,8},{10,11... | collective-permute-start | bytes 2359304 | tf_op jit(solution)/shard_map/ppermute | solution.py:235
  37.3 26.7 %collective-permute-start.11 = (bf16[3104,128]{1,0:T(8,128)(2,1)}, bf16[3104,128]{1,0:T(8,128)(2,1)S(1)}, u32[]{:S(2)}, u32[]{:S(2)}) collective-permute-start(bf16[3104,128]{1,0:T(8,128)(2,1)} %get-tuple-element.176.refs_4_.refs_2_), channel_id=1, source_target_pairs={{0,4},{4,0},{1,5},{5,1},{2,6},{6,2},{3,7},{7,3},{8,12},{12,8},{9,1... | collective-permute-start | bytes 2383880 | tf_op jit(solution)/shard_map/ppermute | solution.py:235
  37.8 26.3 %collective-permute-start.12 = (bf16[3104,128]{1,0:T(8,128)(2,1)}, bf16[3104,128]{1,0:T(8,128)(2,1)S(1)}, u32[]{:S(2)}, u32[]{:S(2)}) collective-permute-start(bf16[3104,128]{1,0:T(8,128)(2,1)} %get-tuple-element.176.refs_4_.refs_2_), channel_id=1, source_target_pairs={{0,2},{2,0},{1,3},{3,1},{4,6},{6,4},{5,7},{7,5},{8,10},{10,8},{9,1... | collective-permute-start | bytes 2383880 | tf_op jit(solution)/shard_map/ppermute | solution.py:235
  41.1 35.0 %collective-permute-start.14 = (bf16[3328,128]{1,0:T(8,128)(2,1)S(1)}, bf16[3328,128]{1,0:T(8,128)(2,1)S(1)}, u32[]{:S(2)}, u32[]{:S(2)}) collective-permute-start(bf16[3328,128]{1,0:T(8,128)(2,1)S(1)} %copy-done.6), channel_id=1, source_target_pairs={{0,2},{2,0},{1,3},{3,1},{4,6},{6,4},{5,7},{7,5},{8,10},{10,8},{9,1... | collective-permute-start | bytes 2555912 | tf_op jit(solution)/shard_map/ppermute | solution.py:235
  42.5 35.2 %collective-permute-start.13 = (bf16[3328,128]{1,0:T(8,128)(2,1)S(1)}, bf16[3328,128]{1,0:T(8,128)(2,1)S(1)}, u32[]{:S(2)}, u32[]{:S(2)}) collective-permute-start(bf16[3328,128]{1,0:T(8,128)(2,1)S(1)} %copy-done.6), channel_id=1, source_target_pairs={{0,4},{4,0},{1,5},{5,1},{2,6},{6,2},{3,7},{7,3},{8,12},{12,8},{9,1... | collective-permute-start | bytes 2555912 | tf_op jit(solution)/shard_map/ppermute | solution.py:235
  48.0 50.4 %copy-start.7 = (bf16[1024,768]{1,0:T(8,128)(2,1)}, bf16[1024,768]{1,0:T(8,128)(2,1)S(1)}, u32[]{:S(2)}) copy-start(bf16[1024,768]{1,0:T(8,128)(2,1)S(1)} %get-tuple-element.170.refs_0_.refs_3_) | copy-start | bytes 4718596
  52.7 11.3 %copy-start = (bf16[1024,1152]{1,0:T(8,128)(2,1)}, bf16[1024,1152]{1,0:T(8,128)(2,1)S(1)}, u32[]{:S(2)}) copy-start(bf16[1024,1152]{1,0:T(8,128)(2,1)S(1)} %get-tuple-element.172.refs_0_.q_ref.k_ref.v_ref) | copy-start | bytes 7077892
  52.7 11.3 %copy-start.20 = (bf16[384,768]{1,0:T(8,128)(2,1)}, bf16[384,768]{1,0:T(8,128)(2,1)S(1)}, u32[]{:S(2)}) copy-start(bf16[384,768]{1,0:T(8,128)(2,1)S(1)} %get-tuple-element.173.refs_2_.refs_6_) | copy-start | bytes 1769476
  64.0 181.6 %copy-start.2 = (f32[1024,384]{1,0:T(8,128)}, f32[1024,384]{1,0:T(8,128)S(1)}, u32[]{:S(2)}) copy-start(f32[1024,384]{1,0:T(8,128)S(1)} %get-tuple-element.198.inv_ref) | copy-start | bytes 4718596
  76.1 22.2 %collective-permute-start.16 = (bf16[3328,128]{1,0:T(8,128)(2,1)S(1)}, bf16[3328,128]{1,0:T(8,128)(2,1)S(1)}, u32[]{:S(2)}, u32[]{:S(2)}) collective-permute-start(bf16[3328,128]{1,0:T(8,128)(2,1)S(1)} %collective-permute-done.14.refs_10_.refs_8_), channel_id=1, source_target_pairs={{0,4},{4,0},{1,5},{5,1},{2,6},{6,2},{3,7},{7,3},{8,12},{12,8},{9,1... | collective-permute-start | bytes 2555912 | tf_op jit(solution)/shard_map/ppermute | solution.py:235
  77.7 20.7 %collective-permute-start.15 = (bf16[3104,128]{1,0:T(8,128)(2,1)S(1)}, bf16[3104,128]{1,0:T(8,128)(2,1)S(1)}, u32[]{:S(2)}, u32[]{:S(2)}) collective-permute-start(bf16[3104,128]{1,0:T(8,128)(2,1)S(1)} %collective-permute-done.11.refs_5_.refs_3_), channel_id=1, source_target_pairs={{0,2},{2,0},{1,3},{3,1},{4,6},{6,4},{5,7},{7,5},{8,10},{10,8},{9,1... | collective-permute-start | bytes 2383880 | tf_op jit(solution)/shard_map/ppermute | solution.py:235
  79.2 19.1 %collective-permute-start.10 = (bf16[1024,768]{1,0:T(8,128)(2,1)S(1)}, bf16[1024,768]{1,0:T(8,128)(2,1)S(1)}, u32[]{:S(2)}, u32[]{:S(2)}) collective-permute-start(bf16[1024,768]{1,0:T(8,128)(2,1)S(1)} %get-tuple-element.174.refs_1_), channel_id=1, source_target_pairs={{0,1},{1,0},{2,3},{3,2},{4,5},{5,4},{6,7},{7,6},{8,9},{9,8},{10,11... | collective-permute-start | bytes 4718600 | tf_op jit(solution)/shard_map/ppermute | solution.py:235
  79.2 53.3 %collective-permute-start.19 = (bf16[3072,128]{1,0:T(8,128)(2,1)}, bf16[3072,128]{1,0:T(8,128)(2,1)}, u32[]{:S(2)}, u32[]{:S(2)}) collective-permute-start(bf16[3072,128]{1,0:T(8,128)(2,1)} %get-tuple-element.277.refs_5_), channel_id=1, source_target_pairs={{0,4},{4,0},{1,5},{5,1},{2,6},{6,2},{3,7},{7,3},{8,12},{12,8},{9,1... | collective-permute-start | bytes 2359304 | tf_op jit(solution)/shard_map/ppermute | solution.py:235
  79.7 53.8 %collective-permute-start.20 = (bf16[3072,128]{1,0:T(8,128)(2,1)}, bf16[3072,128]{1,0:T(8,128)(2,1)}, u32[]{:S(2)}, u32[]{:S(2)}) collective-permute-start(bf16[3072,128]{1,0:T(8,128)(2,1)} %get-tuple-element.277.refs_5_), channel_id=1, source_target_pairs={{0,2},{2,0},{1,3},{3,1},{4,6},{6,4},{5,7},{7,5},{8,10},{10,8},{9,1... | collective-permute-start | bytes 2359304 | tf_op jit(solution)/shard_map/ppermute | solution.py:235
  111.7 3.5 %collective-permute-start.17 = (bf16[1024,768]{1,0:T(8,128)(2,1)S(1)}, bf16[1024,768]{1,0:T(8,128)(2,1)S(1)}, u32[]{:S(2)}, u32[]{:S(2)}) collective-permute-start(bf16[1024,768]{1,0:T(8,128)(2,1)S(1)} %get-tuple-element.184.refs_2_), channel_id=1, source_target_pairs={{0,1},{1,0},{2,3},{3,2},{4,5},{5,4},{6,7},{7,6},{8,9},{9,8},{10,11... | collective-permute-start | bytes 4718600 | tf_op jit(solution)/shard_map/ppermute | solution.py:235
  121.3 12.2 %copy-start.36 = (bf16[1024,384]{1,0:T(8,128)(2,1)}, bf16[1024,384]{1,0:T(8,128)(2,1)S(1)}, u32[]{:S(2)}) copy-start(bf16[1024,384]{1,0:T(8,128)(2,1)S(1)} %get-tuple-element.226.refs_7_) | copy-start | bytes 2359300
  121.3 12.2 %copy-start.38 = (bf16[768,512]{1,0:T(8,128)(2,1)}, bf16[768,512]{1,0:T(8,128)(2,1)S(1)}, u32[]{:S(2)}) copy-start(bf16[768,512]{1,0:T(8,128)(2,1)S(1)} %get-tuple-element.222.refs_6_) | copy-start | bytes 2359300
  121.3 12.2 %copy-start.40 = (bf16[512,768]{1,0:T(8,128)(2,1)}, bf16[512,768]{1,0:T(8,128)(2,1)S(1)}, u32[]{:S(2)}) copy-start(bf16[512,768]{1,0:T(8,128)(2,1)S(1)} %get-tuple-element.220.refs_6_) | copy-start | bytes 2359300
  132.3 15.0 %collective-permute-start.18 = (bf16[1024,512]{1,0:T(8,128)(2,1)S(1)}, bf16[1024,512]{1,0:T(8,128)(2,1)S(1)}, u32[]{:S(2)}, u32[]{:S(2)}) collective-permute-start(bf16[1024,512]{1,0:T(8,128)(2,1)S(1)} %get-tuple-element.190.refs_2_), channel_id=1, source_target_pairs={{0,1},{1,0},{2,3},{3,2},{4,5},{5,4},{6,7},{7,6},{8,9},{9,8},{10,11... | collective-permute-start | bytes 3145736 | tf_op jit(solution)/shard_map/ppermute | solution.py:235
  134.6 11.5 %collective-permute-start.21 = (bf16[1536,128]{1,0:T(8,128)(2,1)S(1)}, bf16[1536,128]{1,0:T(8,128)(2,1)S(1)}, u32[]{:S(2)}, u32[]{:S(2)}) collective-permute-start(bf16[1536,128]{1,0:T(8,128)(2,1)S(1)} %slice.100), channel_id=1, source_target_pairs={{0,2},{2,0},{1,3},{3,1},{4,6},{6,4},{5,7},{7,5},{8,10},{10,8},{9,1... | collective-permute-start | bytes 1179656 | tf_op jit(solution)/shard_map/ppermute | solution.py:235
  136.2 11.1 %collective-permute-start.22 = (bf16[1536,128]{1,0:T(8,128)(2,1)S(1)}, bf16[1536,128]{1,0:T(8,128)(2,1)S(1)}, u32[]{:S(2)}, u32[]{:S(2)}) collective-permute-start(bf16[1536,128]{1,0:T(8,128)(2,1)S(1)} %slice.101), channel_id=1, source_target_pairs={{0,4},{4,0},{1,5},{5,1},{2,6},{6,2},{3,7},{7,3},{8,12},{12,8},{9,1... | collective-permute-start | bytes 1179656 | tf_op jit(solution)/shard_map/ppermute | solution.py:235
  157.0 4.8 %collective-permute-start.23 = (bf16[1024,512]{1,0:T(8,128)(2,1)S(1)}, bf16[1024,512]{1,0:T(8,128)(2,1)S(1)}, u32[]{:S(2)}, u32[]{:S(2)}) collective-permute-start(bf16[1024,512]{1,0:T(8,128)(2,1)S(1)} %get-tuple-element.206.refs_1_), channel_id=1, source_target_pairs={{0,1},{1,0},{2,3},{3,2},{4,5},{5,4},{6,7},{7,6},{8,9},{9,8},{10,11... | collective-permute-start | bytes 3145736 | tf_op jit(solution)/shard_map/ppermute | solution.py:235
  158.3 16.2 %collective-permute-start.24 = (bf16[2048,128]{1,0:T(8,128)(2,1)S(1)}, bf16[2048,128]{1,0:T(8,128)(2,1)S(1)}, u32[]{:S(2)}, u32[]{:S(2)}) collective-permute-start(bf16[2048,128]{1,0:T(8,128)(2,1)S(1)} %decoder_feed_grads.1), channel_id=1, source_target_pairs={{0,8},{24,16},{1,9},{25,17},{2,10},{26,18},{3,11},{27,19},{4,12},{... | collective-permute-start | bytes 1572872 | tf_op jit(solution)/shard_map/ppermute | solution.py:1015
  174.6 10.3 %collective-permute-start.25 = (bf16[2048,128]{1,0:T(8,128)(2,1)S(1)}, bf16[2048,128]{1,0:T(8,128)(2,1)S(1)}, u32[]{:S(2)}, u32[]{:S(2)}) collective-permute-start(bf16[2048,128]{1,0:T(8,128)(2,1)S(1)} %add_convert_fusion.7), channel_id=1, source_target_pairs={{8,16},{16,8},{9,17},{17,9},{10,18},{18,10},{11,19},{19,11},{12,20... | collective-permute-start | bytes 1572872 | tf_op jit(solution)/shard_map/ppermute | solution.py:1031
  185.1 40.0 %copy-start.51 = (bf16[2048,128]{1,0:T(8,128)(2,1)}, bf16[2048,128]{1,0:T(8,128)(2,1)S(1)}, u32[]{:S(2)}) copy-start(bf16[2048,128]{1,0:T(8,128)(2,1)S(1)} %add_convert_fusion.6) | copy-start | bytes 1572868
  187.8 2.7 collective-permute-start.26
  195.4 20.4 %collective-permute-start.27 = (bf16[768,384]{1,0:T(8,128)(2,1)S(1)}, bf16[768,384]{1,0:T(8,128)(2,1)S(1)}, u32[]{:S(2)}, u32[]{:S(2)}) collective-permute-start(bf16[768,384]{1,0:T(8,128)(2,1)S(1)} %encoder_down_grads.1), channel_id=1, source_target_pairs={{0,8},{24,16},{1,9},{25,17},{2,10},{26,18},{3,11},{27,19},{4,12},{... | collective-permute-start | bytes 1769480 | tf_op jit(solution)/shard_map/ppermute | solution.py:1015
  215.8 10.6 %collective-permute-start.28 = (bf16[1024,768]{1,0:T(8,128)(2,1)S(1)}, bf16[1024,768]{1,0:T(8,128)(2,1)S(1)}, u32[]{:S(2)}, u32[]{:S(2)}) collective-permute-start(bf16[1024,768]{1,0:T(8,128)(2,1)S(1)} %get-tuple-element.238.refs_1_), channel_id=1, source_target_pairs={{0,1},{1,0},{2,3},{3,2},{4,5},{5,4},{6,7},{7,6},{8,9},{9,8},{10,11... | collective-permute-start | bytes 4718600 | tf_op jit(solution)/shard_map/ppermute | solution.py:235
  218.0 19.4 %collective-permute-start.31 = (bf16[384,768]{1,0:T(8,128)(2,1)S(1)}, bf16[384,768]{1,0:T(8,128)(2,1)S(1)}, u32[]{:S(2)}, u32[]{:S(2)}) collective-permute-start(bf16[384,768]{1,0:T(8,128)(2,1)S(1)} %encoder_up_grads.1), channel_id=1, source_target_pairs={{0,8},{24,16},{1,9},{25,17},{2,10},{26,18},{3,11},{27,19},{4,12},{... | collective-permute-start | bytes 1769480 | tf_op jit(solution)/shard_map/ppermute | solution.py:1015
  220.3 19.7 %collective-permute-start.29 = (bf16[768,384]{1,0:T(8,128)(2,1)S(1)}, bf16[768,384]{1,0:T(8,128)(2,1)S(1)}, u32[]{:S(2)}, u32[]{:S(2)}) collective-permute-start(bf16[768,384]{1,0:T(8,128)(2,1)S(1)} %add_convert_fusion.5), channel_id=1, source_target_pairs={{8,16},{16,8},{9,17},{17,9},{10,18},{18,10},{11,19},{19,11},{12,20... | collective-permute-start | bytes 1769480 | tf_op jit(solution)/shard_map/ppermute | solution.py:1031
  221.0 19.0 %collective-permute-start.30 = (bf16[1408,128]{1,0:T(8,128)(2,1)S(1)}, bf16[1408,128]{1,0:T(8,128)(2,1)S(1)}, u32[]{:S(2)}, u32[]{:S(2)}) collective-permute-start(bf16[1408,128]{1,0:T(8,128)(2,1)S(1)} %decoder_mixing_grads.1), channel_id=1, source_target_pairs={{0,8},{24,16},{1,9},{25,17},{2,10},{26,18},{3,11},{27,19},{4,12},{... | collective-permute-start | bytes 1081352 | tf_op jit(solution)/shard_map/ppermute | solution.py:1015
  225.1 20.5 %collective-permute-start.32 = (bf16[2048,128]{1,0:T(8,128)(2,1)S(1)}, bf16[2048,128]{1,0:T(8,128)(2,1)S(1)}, u32[]{:S(2)}, u32[]{:S(2)}) collective-permute-start(bf16[2048,128]{1,0:T(8,128)(2,1)S(1)} %add_convert_fusion.6), channel_id=1, source_target_pairs={{8,0},{16,24},{9,1},{17,25},{10,2},{18,26},{11,3},{19,27},{12,4},{... | collective-permute-start | bytes 1572872 | tf_op jit(solution)/shard_map/ppermute | solution.py:1031
  232.2 13.5 %copy-start.4 = (f32[1024,384]{1,0:T(8,128)}, f32[1024,384]{1,0:T(8,128)S(1)}, u32[]{:S(2)}) copy-start(f32[1024,384]{1,0:T(8,128)S(1)} %get-tuple-element.257.grad_ref) | copy-start | bytes 4718596
  237.4 13.9 %copy-start.26 = (bf16[1024,128]{1,0:T(8,128)(2,1)}, bf16[1024,128]{1,0:T(8,128)(2,1)S(1)}, u32[]{:S(2)}) copy-start(bf16[1024,128]{1,0:T(8,128)(2,1)S(1)} %get-tuple-element.242.refs_2_) | copy-start | bytes 786436
  237.4 13.9 %copy-start.28 = (bf16[1024,128]{1,0:T(8,128)(2,1)}, bf16[1024,128]{1,0:T(8,128)(2,1)S(1)}, u32[]{:S(2)}) copy-start(bf16[1024,128]{1,0:T(8,128)(2,1)S(1)} %get-tuple-element.243.refs_3_) | copy-start | bytes 786436
  241.0 21.2 %collective-permute-start.35 = (bf16[384,768]{1,0:T(8,128)(2,1)}, bf16[384,768]{1,0:T(8,128)(2,1)}, u32[]{:S(2)}, u32[]{:S(2)}) collective-permute-start(bf16[384,768]{1,0:T(8,128)(2,1)} %add_convert_fusion.3), channel_id=1, source_target_pairs={{8,16},{16,8},{9,17},{17,9},{10,18},{18,10},{11,19},{19,11},{12,20... | collective-permute-start | bytes 1769480 | tf_op jit(solution)/shard_map/ppermute | solution.py:1031
  243.5 20.1 %collective-permute-start.34 = (bf16[768,384]{1,0:T(8,128)(2,1)}, bf16[768,384]{1,0:T(8,128)(2,1)}, u32[]{:S(2)}, u32[]{:S(2)}) collective-permute-start(bf16[768,384]{1,0:T(8,128)(2,1)} %add_convert_fusion.4), channel_id=1, source_target_pairs={{8,0},{16,24},{9,1},{17,25},{10,2},{18,26},{11,3},{19,27},{12,4},{... | collective-permute-start | bytes 1769480 | tf_op jit(solution)/shard_map/ppermute | solution.py:1031
  253.3 18.4 %collective-permute-start.33 = (bf16[2304,128]{1,0:T(8,128)(2,1)}, bf16[2304,128]{1,0:T(8,128)(2,1)}, u32[]{:S(2)}, u32[]{:S(2)}) collective-permute-start(bf16[2304,128]{1,0:T(8,128)(2,1)} %encoder_mixing_grads.1), channel_id=1, source_target_pairs={{0,8},{24,16},{1,9},{25,17},{2,10},{26,18},{3,11},{27,19},{4,12},{... | collective-permute-start | bytes 1769480 | tf_op jit(solution)/shard_map/ppermute | solution.py:1015
  261.4 15.8 %collective-permute-start.37 = (bf16[1408,128]{1,0:T(8,128)(2,1)}, bf16[1408,128]{1,0:T(8,128)(2,1)S(1)}, u32[]{:S(2)}, u32[]{:S(2)}) collective-permute-start(bf16[1408,128]{1,0:T(8,128)(2,1)} %add_convert_fusion.9), channel_id=1, source_target_pairs={{8,16},{16,8},{9,17},{17,9},{10,18},{18,10},{11,19},{19,11},{12,20... | collective-permute-start | bytes 1081352 | tf_op jit(solution)/shard_map/ppermute | solution.py:1031
  265.0 10.3 %copy-start.33 = (bf16[1024,128]{1,0:T(8,128)(2,1)S(1)}, bf16[1024,128]{1,0:T(8,128)(2,1)}, u32[]{:S(2)}) copy-start(bf16[1024,128]{1,0:T(8,128)(2,1)} %copy-done.32) | copy-start | bytes 786436
  265.0 10.3 %copy-start.35 = (bf16[1024,128]{1,0:T(8,128)(2,1)S(1)}, bf16[1024,128]{1,0:T(8,128)(2,1)}, u32[]{:S(2)}) copy-start(bf16[1024,128]{1,0:T(8,128)(2,1)} %copy-done.34) | copy-start | bytes 786436
  273.1 16.8 %collective-permute-start.36 = (bf16[2304,128]{1,0:T(8,128)(2,1)S(1)}, bf16[2304,128]{1,0:T(8,128)(2,1)S(1)}, u32[]{:S(2)}, u32[]{:S(2)}) collective-permute-start(bf16[2304,128]{1,0:T(8,128)(2,1)S(1)} %add_convert_fusion.1), channel_id=1, source_target_pairs={{8,16},{16,8},{9,17},{17,9},{10,18},{18,10},{11,19},{19,11},{12,20... | collective-permute-start | bytes 1769480 | tf_op jit(solution)/shard_map/ppermute | solution.py:1031
  273.8 23.3 %collective-permute-start.46 = (bf16[384,768]{1,0:T(8,128)(2,1)S(1)}, bf16[384,768]{1,0:T(8,128)(2,1)S(1)}, u32[]{:S(2)}, u32[]{:S(2)}) collective-permute-start(bf16[384,768]{1,0:T(8,128)(2,1)S(1)} %add_convert_fusion.2), channel_id=1, source_target_pairs={{8,0},{16,24},{9,1},{17,25},{10,2},{18,26},{11,3},{19,27},{12,4},{... | collective-permute-start | bytes 1769480 | tf_op jit(solution)/shard_map/ppermute | solution.py:1031
  277.1 1.8 collective-permute-start.38
  277.3 21.4 %collective-permute-start.44 = (bf16[1408,128]{1,0:T(8,128)(2,1)S(1)}, bf16[1408,128]{1,0:T(8,128)(2,1)S(1)}, u32[]{:S(2)}, u32[]{:S(2)}) collective-permute-start(bf16[1408,128]{1,0:T(8,128)(2,1)S(1)} %add_convert_fusion.8), channel_id=1, source_target_pairs={{8,0},{16,24},{9,1},{17,25},{10,2},{18,26},{11,3},{19,27},{12,4},{... | collective-permute-start | bytes 1081352 | tf_op jit(solution)/shard_map/ppermute | solution.py:1031
  278.9 10.9 %copy-start.52 = (bf16[2048,128]{1,0:T(8,128)(2,1)S(1)}, bf16[2048,128]{1,0:T(8,128)(2,1)}, u32[]{:S(2)}) copy-start(bf16[2048,128]{1,0:T(8,128)(2,1)} %copy-done.51) | copy-start | bytes 1572868
  278.9 10.9 %copy-start.55 = (bf16[2048,128]{1,0:T(8,128)(2,1)S(1)}, bf16[2048,128]{1,0:T(8,128)(2,1)}, u32[]{:S(2)}) copy-start(bf16[2048,128]{1,0:T(8,128)(2,1)} %copy-done.54) | copy-start | bytes 1572868
  290.1 26.4 %collective-permute-start.43 = (bf16[2304,128]{1,0:T(8,128)(2,1)S(1)}, bf16[2304,128]{1,0:T(8,128)(2,1)S(1)}, u32[]{:S(2)}, u32[]{:S(2)}) collective-permute-start(bf16[2304,128]{1,0:T(8,128)(2,1)S(1)} %add_convert_fusion), channel_id=1, source_target_pairs={{8,0},{16,24},{9,1},{17,25},{10,2},{18,26},{11,3},{19,27},{12,4},{... | collective-permute-start | bytes 1769480 | tf_op jit(solution)/shard_map/ppermute | solution.py:1031
  291.4 20.2 %collective-permute-start.40 = (f32[8,768]{1,0:T(8,128)S(1)}, f32[8,768]{1,0:T(8,128)S(1)}, u32[]{:S(2)}, u32[]{:S(2)}) collective-permute-start(f32[8,768]{1,0:T(8,128)S(1)} %bitcast_reduce_fusion), channel_id=1, source_target_pairs={{0,24},{8,0},{16,8},{24,16},{1,25},{9,1},{17,9},{25,17},{2,26},{10... | collective-permute-start | bytes 73736 | tf_op jit(solution)/shard_map/ppermute | solution.py:1053
  292.8 18.8 %collective-permute-start.41 = (f32[8,768]{1,0:T(8,128)S(1)}, f32[8,768]{1,0:T(8,128)S(1)}, u32[]{:S(2)}, u32[]{:S(2)}) collective-permute-start(f32[8,768]{1,0:T(8,128)S(1)} %bitcast_reduce_fusion), channel_id=1, source_target_pairs={{0,16},{8,24},{16,0},{24,8},{1,17},{9,25},{17,1},{25,9},{2,18},{10... | collective-permute-start | bytes 73736 | tf_op jit(solution)/shard_map/ppermute | solution.py:1053
  297.1 14.5 %collective-permute-start.42 = (f32[8,768]{1,0:T(8,128)S(1)}, f32[8,768]{1,0:T(8,128)S(1)}, u32[]{:S(2)}, u32[]{:S(2)}) collective-permute-start(f32[8,768]{1,0:T(8,128)S(1)} %bitcast_reduce_fusion), channel_id=1, source_target_pairs={{0,8},{8,16},{16,24},{24,0},{1,9},{9,17},{17,25},{25,1},{2,10},{10... | collective-permute-start | bytes 73736 | tf_op jit(solution)/shard_map/ppermute | solution.py:1053
  299.3 15.3 %collective-permute-start.45 = (bf16[1536,128]{1,0:T(8,128)(2,1)S(1)}, bf16[1536,128]{1,0:T(8,128)(2,1)S(1)}, u32[]{:S(2)}, u32[]{:S(2)}) collective-permute-start(bf16[1536,128]{1,0:T(8,128)(2,1)S(1)} %decoder_send.1), channel_id=1, source_target_pairs={{0,1},{1,0},{2,3},{3,2},{4,5},{5,4},{6,7},{7,6},{8,9},{9,8},{10,11... | collective-permute-start | bytes 1179656 | tf_op jit(solution)/shard_map/ppermute | solution.py:235
  311.6 1.4 collective-permute-start.39
  (43 other events, 172.3 us)
where the time goes:
time: 323 us; the launch traced here: 319 us
  Pallas kernels  141 us (44%)
  starting transfers between devices  67.1 us (21%)
  waiting for transfers between devices  64 us (20%)
  local copies, waits for them, and re-layouts  22.4 us (7%)
  other arithmetic  12.2 us (4%)
  blocking collectives  8.96 us (3%)
    pallas_call x30, Pallas kernels, call(): pl.pallas_call(body, out_shape=outs, in_specs=[SMEM] * scalars + [place]...  106 us
    ppermute x29, waiting for transfers between devices, swap(): return lax.ppermute(value, axis, SWAP)  52.8 us
    pallas_call x5, Pallas kernels, attention_backward(): pl.pallas_call(functools.partial(attention_backward_kernel, head_size, pa...  35 us
    ppermute x5, starting transfers between devices, line_first(): return (value, lax.ppermute(value, 'dp', [(0, 1), (3, 2)]))  24.6 us
    ppermute x29, starting transfers between devices, swap(): return lax.ppermute(value, axis, SWAP)  24.3 us
    unnamed x129, local copies, waits for them, and re-layouts  16.3 us
    ppermute x10, starting transfers between devices, line_next(): return (total, lax.ppermute(total, 'dp', pairs))  11 us
    all_gather x1, blocking collectives, per_device(): sums = jnp.sum(lax.all_gather(sums, ('row', 'y', 'core')), 0)  8.96 us
  transfers between devices with their start and end apart: 47, of which 13 were waited for; matrix products, arithmetic and copies ran while one was open for 6% of the time, Pallas kernels for 39%

commit v1 on v0

--- a/solution.py
+++ b/solution.py
@@ -251,6 +251,10 @@
     return swap(after(pair[1], *others), "row")
 
 
+def across_direct(pack):
+    return lax.ppermute(pack, ("row", "y"), [(i, 3 - i) for i in range(4)])
+
+
 def across_both(pair, split, *others):
     first, second = after((pair[0][:split], pair[1][split:]), *others)
     return (swap(first, "y"), swap(second, "row"))
@@ -360,6 +364,7 @@
 
 
 TILE = 256
+FEED = 512
 
 
 def lane_roll(values):
@@ -403,15 +408,13 @@
         ]
 
 
-def pack_encoder_kernel(up_ref, down_ref, mix_ref, first_ref, second_ref):
-    for weight_ref, pack_ref in ((up_ref, first_ref), (down_ref, second_ref)):
+def pack_encoder_kernel(up_ref, down_ref, pack_ref):
+    base = 0
+    for weight_ref in (up_ref, down_ref):
         rows, columns = weight_ref.shape
         for tile in range(columns // LANES):
-            pack_ref[tile * rows : (tile + 1) * rows, :] = weight_ref[
-                :, tile * LANES : (tile + 1) * LANES
-            ]
-    first_ref[E_FEED:, :] = mix_ref[:DA_END, :]
-    second_ref[E_FEED:, :] = mix_ref[DA_END:, :]
+            pack_ref[base : base + rows, :] = weight_ref[:, tile * LANES : (tile + 1) * LANES]
+            base += rows
 
 
 def pack_decoder_kernel(
@@ -530,9 +533,9 @@
         theirs = jnp.concatenate([lane_roll(theirs), theirs], 0)
         weight_ref[at, 7 * LANES : 8 * LANES] = jnp.where(low, mine, theirs).astype(BF16)
 
-    @pl.loop(0, normed_ref.shape[0] // TILE)
+    @pl.loop(0, normed_ref.shape[0] // FEED)
     def _(tile):
-        at = pl.ds(tile * TILE, TILE)
+        at = pl.ds(tile * FEED, FEED)
         mixed_ref[at, :] = mm(normed_ref[at, :], weight_ref[...]).astype(BF16)
 
 
@@ -644,6 +647,12 @@
             0,
         )
 
+    def up_both(self, chunk):
+        return jnp.concatenate([self.up_chunk(unit, chunk) for unit in range(2)], 1)
+
+    def down_both(self, chunk):
+        return jnp.concatenate([self.down_chunk(unit, chunk) for unit in range(2)], 0)
+
     def down_chunk(self, unit, chunk):
         return jnp.concatenate(
             [
@@ -663,13 +672,14 @@
 
 
 def feed_forward_kernel(stream_ref, mine_ref, got_ref, vec_ref, *refs):
-    middle_ref, normed_ref, active_ref, slope_ref, partial_ref, total_ref = refs[8:14]
-    feed = Feed(Parts(refs[:4]), Parts(refs[4:8]), False)
+    middle_ref, normed_ref, active_ref, slope_ref, partial_ref, total_ref = refs[5:11]
+    pair = Pair(refs[:5], E_FEED)
+    feed = Feed(pair.first, pair.second, False)
     gain, bias = vec_ref[2:3, :], vec_ref[3:4, :]
 
-    @pl.loop(0, stream_ref.shape[0] // TILE)
+    @pl.loop(0, stream_ref.shape[0] // FEED)
     def _(tile):
-        at = pl.ds(tile * TILE, TILE)
+        at = pl.ds(tile * FEED, FEED)
         middle = stream_ref[at, :].astype(F32) + (
             mine_ref[at, :].astype(F32) + got_ref[at, :].astype(F32)
         )
@@ -680,14 +690,16 @@
 
         @pl.loop(0, feed.chunks)
         def _(chunk):
+            hidden = mm(normed_ref[at, :], feed.up_both(chunk))
+            active, slope = gelu_pair(hidden)
+            low = active.astype(BF16)
+            slope = slope.astype(BF16)
             for unit in range(2):
-                hidden = mm(normed_ref[at, :], feed.up_chunk(unit, chunk))
-                active, slope = gelu_pair(hidden)
                 lanes = pl.ds(unit * feed.units + chunk * 2 * LANES, 2 * LANES)
-                low = active.astype(BF16)
-                active_ref[at, lanes] = low
-                slope_ref[at, lanes] = slope.astype(BF16)
-                total_ref[...] += mm(low, feed.down_chunk(unit, chunk))
+                part = slice(unit * 2 * LANES, (unit + 1) * 2 * LANES)
+                active_ref[at, lanes] = low[:, part]
+                slope_ref[at, lanes] = slope[:, part]
+            total_ref[...] += mm(low, feed.down_both(chunk))
 
         partial_ref[at, :] = total_ref[...].astype(BF16)
 
@@ -695,9 +707,8 @@
 def decoder_feed_kernel(
     place_ref, stream_ref, mine_ref, got_ref, vec_ref, *refs
 ):
-    middle_ref, normed_ref, active_ref, hidden_ref, partial_ref, cot_ref, total_ref = refs[5:12]
-    pair = Pair(refs[:5], F_END)
-    first, second = pair.first, pair.second
+    middle_ref, normed_ref, active_ref, hidden_ref, partial_ref, cot_ref, total_ref = refs[4:11]
+    first, second = Parts(refs[:4]), Parts(refs[:4], F_END)
     row = place_ref[2]
     for i in range(2):
         for number, parts in enumerate((first, second)):
@@ -709,9 +720,9 @@
     feed = Feed(first, second, True)
     gain, bias = vec_ref[2:3, :], vec_ref[3:4, :]
 
-    @pl.loop(0, stream_ref.shape[0] // TILE)
+    @pl.loop(0, stream_ref.shape[0] // FEED)
     def _(tile):
-        at = pl.ds(tile * TILE, TILE)
+        at = pl.ds(tile * FEED, FEED)
         middle = stream_ref[at, :] + (mine_ref[at, :].astype(F32) + got_ref[at, :].astype(F32))
         middle_ref[at, :] = middle
         centred, _ = norm_rows(middle)
@@ -720,16 +731,18 @@
 
         @pl.loop(0, feed.chunks)
         def _(chunk):
+            upward = feed.up_both(chunk)
+            hidden = mm(normed_ref[at, :], upward)
+            active, slope = gelu_pair(hidden)
+            active = active.astype(BF16)
+            grad = mm_nt(cot_ref[at, :], feed.down_both(chunk))
+            low = (grad * slope).astype(BF16)
             for unit in range(2):
-                upward = feed.up_chunk(unit, chunk)
-                hidden = mm(normed_ref[at, :], upward)
-                active, slope = gelu_pair(hidden)
                 lanes = pl.ds(unit * feed.units + chunk * 2 * LANES, 2 * LANES)
-                active_ref[at, lanes] = active.astype(BF16)
-                grad = mm_nt(cot_ref[at, :], feed.down_chunk(unit, chunk))
-                low = (grad * slope).astype(BF16)
-                hidden_ref[at, lanes] = low
-                total_ref[...] += mm_nt(low, upward)
+                part = slice(unit * 2 * LANES, (unit + 1) * 2 * LANES)
+                active_ref[at, lanes] = active[:, part]
+                hidden_ref[at, lanes] = low[:, part]
+            total_ref[...] += mm_nt(low, upward)
 
         partial_ref[at, :] = total_ref[...].astype(BF16)
 
@@ -738,9 +751,10 @@
     (
         out_ref, low_ref, stream_ref, normed_ref, mixed_ref, weight_ref, vec_ref, mixing_ref,
         back_ref,
-    ) = refs[8:17]
+    ) = refs[5:14]
     block = place_ref[1]
-    first, second = Parts(refs[:4], E_FEED), Parts(refs[4:8], E_FEED)
+    pair = Pair(refs[:5], DA_END)
+    first, second = pair.first, pair.second
     back_ref[...] = decoder_out_rows(second)
     rows = E_ROWS
     for j in range(2):
@@ -833,9 +847,9 @@
 def mixed_back_kernel(*refs):
     lows, weight_ref, partial_ref = refs[:-2], refs[-2], refs[-1]
 
-    @pl.loop(0, partial_ref.shape[0] // TILE)
+    @pl.loop(0, partial_ref.shape[0] // FEED)
     def _(tile):
-        at = pl.ds(tile * TILE, TILE)
+        at = pl.ds(tile * FEED, FEED)
         partial_ref[at, :] = mm_nt(mixed_low(lows, at), weight_ref[...]).astype(BF16)
 
 
@@ -868,22 +882,26 @@
 
 
 def feed_back_kernel(down_ref, slope_ref, *refs):
-    hidden_ref, partial_ref, total_ref = refs[8:11]
-    feed = Feed(Parts(refs[:4]), Parts(refs[4:8]), False)
-
-    @pl.loop(0, down_ref.shape[0] // TILE)
+    hidden_ref, partial_ref, total_ref = refs[5:8]
+    pair = Pair(refs[:5], E_FEED)
+    feed = Feed(pair.first, pair.second, False)
+
+    @pl.loop(0, down_ref.shape[0] // FEED)
     def _(tile):
-        at = pl.ds(tile * TILE, TILE)
+        at = pl.ds(tile * FEED, FEED)
         total_ref[...] = jnp.zeros_like(total_ref)
 
         @pl.loop(0, feed.chunks)
         def _(chunk):
+            back = mm_nt(down_ref[at, :], feed.down_both(chunk))
+            parts = []
             for unit in range(2):
                 lanes = pl.ds(unit * feed.units + chunk * 2 * LANES, 2 * LANES)
-                back = mm_nt(down_ref[at, :], feed.down_chunk(unit, chunk))
-                hidden = (back * slope_ref[at, lanes].astype(F32)).astype(BF16)
+                part = slice(unit * 2 * LANES, (unit + 1) * 2 * LANES)
+                hidden = (back[:, part] * slope_ref[at, lanes].astype(F32)).astype(BF16)
                 hidden_ref[at, lanes] = hidden
-                total_ref[...] += mm_nt(hidden, feed.up_chunk(unit, chunk))
+                parts.append(hidden)
+            total_ref[...] += mm_nt(jnp.concatenate(parts, 1), feed.up_both(chunk))
 
         partial_ref[at, :] = total_ref[...].astype(BF16)
 
@@ -1146,15 +1164,15 @@
         scalars=1,
         limit=8,
     )
-    up, down = call(
+    e_pack = call(
         pack_encoder_kernel,
         "pack_encoder",
-        (shaped(E_FEED + DA_END, LANES, BF16), shaped(E_FEED + DB_END, LANES, BF16)),
-        (encoder_up_weight, encoder_down_weight, dm_pack),
+        shaped(2 * E_FEED, LANES, BF16),
+        (encoder_up_weight, encoder_down_weight),
         limit=56,
         fetch=True,
     )
-    x_far = across_both(x_near, half, up)
+    x_far = across_both(x_near, half, e_pack, dm_pack)
     m_far = across_both(m_near, A_END, x_far)
     sides = call(
         join_input_kernel,
@@ -1167,7 +1185,8 @@
         needs=(m_near,),
     )
     m_parts = (m_pack, *m_near, *m_far)
-    up_near, down_near = near(after(up, sides)), near(after(down, sides))
+    e_near = near(after(e_pack, sides))
+    dm_near = near(after(dm_pack, sides))
     mark = marker(tick, 5000, m_far)
     stream, normed_first, e_vec = call(
         first_norm_kernel,
@@ -1204,10 +1223,12 @@
         cost=12,
     )
     got = swap(partial, "core")
-    up_parts = (up, *up_near, across_by_row(up_near, attended, down_near))
-    down_parts = (down, *down_near, across_by_y(down_near, attended, up_near))
-    f_near = near(after(f_pack, down_near))
-    mark = marker(tick, 10000, up_parts[1:], down_parts[1:])
+    e_far = across_both(e_near, E_FEED, attended, dm_near)
+    e_parts = (e_pack, *e_near, *e_far)
+    dm_far = across_both(dm_near, DA_END, attended)
+    f_go = after(f_pack, e_far)
+    f_parts = (f_pack, *near(f_go), across_direct(f_go))
+    mark = marker(tick, 10000, e_far)
     middle, normed_second, active, slope, partial = call(
         feed_forward_kernel,
         "feed_forward",
@@ -1218,8 +1239,8 @@
             shaped(length, units, BF16),
             shaped(length, full, BF16),
         ),
-        (stream, partial, got, e_vec, *up_parts, *down_parts),
-        (pltpu.VMEM((TILE, full), F32),),
+        (stream, partial, got, e_vec, *e_parts),
+        (pltpu.VMEM((FEED, full), F32),),
         limit=16,
         cost=12,
         marks=(mark,),
@@ -1242,7 +1263,7 @@
             shaped(low_full, 6 * LANES, BF16),
             shaped(2 * LANES, low_full, BF16),
         ),
-        (place, middle, partial, swap(partial, "core"), *up_parts, *down_parts),
+        (place, middle, partial, swap(partial, "core"), dm_pack, *dm_near, *dm_far),
         scalars=1,
         limit=12,
         marks=(mark,),
@@ -1262,7 +1283,7 @@
         limit=16,
         cost=11,
     )
-    f_parts = (f_pack, *f_near, *across_both(f_near, F_END, d_mixed))
+    mark = marker(tick, 10000, partial)
     d_middle, d_normed_second, d_active, d_hidden, partial, cotangent = call(
         decoder_feed_kernel,
         "decoder_feed",
@@ -1275,9 +1296,10 @@
             shaped(length, low_full, BF16),
         ),
         (place, d_stream, partial, swap(partial, "core"), d_vec, *f_parts),
-        (pltpu.VMEM((TILE, low_full), F32),),
+        (pltpu.VMEM((FEED, low_full), F32),),
         scalars=1,
         limit=16,
+        marks=(mark,),
         cost=8,
     )
 
@@ -1363,8 +1385,8 @@
         feed_back_kernel,
         "feed_back",
         (shaped(length, units, BF16), shaped(length, full, BF16)),
-        (after(down_low, grads_b), slope, *up_parts, *down_parts),
-        (pltpu.VMEM((TILE, full), F32),),
+        (after(down_low, grads_b), slope, *e_parts),
+        (pltpu.VMEM((FEED, full), F32),),
         limit=16,
         cost=12,
     )

time: 323 us -> 306 us (0.947)
  Pallas kernels: 141 us -> 131 us
  waiting for transfers between devices: 64 us -> 57.4 us
  local copies, waits for them, and re-layouts: 22.4 us -> 17.4 us
  starting transfers between devices: 67.1 us -> 71.6 us
    ppermute x29, waiting for transfers between devices: 52.8 us -> 36.8 us  [swap(): return lax.ppermute(value, axis, SWAP)]
    pallas_call x30 -> x31, Pallas kernels: 106 us -> 96 us  [call(): pl.pallas_call(body, out_shape=outs, in_specs=[SMEM] * scalars + [place]...]
    ppermute x0 -> x1, waiting for transfers between devices: none -> 5.83 us  [across_direct(): return lax.ppermute(pack, ('row', 'y'), [(i, 3 - i) for i in range(4)])]
    unnamed x129 -> x127, local copies, waits for them, and re-layouts: 16.3 us -> 11.8 us
    ppermute x5, waiting for transfers between devices: 4.05 us -> 7.99 us  [line_first(): return (value, lax.ppermute(value, 'dp', [(0, 1), (3, 2)]))]
    ppermute x5, starting transfers between devices: 24.6 us -> 28.2 us  [line_first(): return (value, lax.ppermute(value, 'dp', [(0, 1), (3, 2)]))]
  transfers between devices with their start and end apart: 47 -> 48, of which waited for: 13 -> 14; matrix products, arithmetic and copies ran while one was open for 6% -> 7% of each run, Pallas kernels for 39% -> 38%
where the time goes in v1:
time: 306 us; the launch traced here: 302 us
  Pallas kernels  131 us (43%)
  starting transfers between devices  71.6 us (23%)
  waiting for transfers between devices  57.4 us (19%)
  local copies, waits for them, and re-layouts  17.4 us (6%)
  other arithmetic  12.2 us (4%)
  blocking collectives  9.36 us (3%)
    pallas_call x31, Pallas kernels, call(): pl.pallas_call(body, out_shape=outs, in_specs=[SMEM] * scalars + [place]...  96 us
    ppermute x29, waiting for transfers between devices, swap(): return lax.ppermute(value, axis, SWAP)  36.8 us
    pallas_call x5, Pallas kernels, attention_backward(): pl.pallas_call(functools.partial(attention_backward_kernel, head_size, pa...  35 us
    ppermute x5, starting transfers between devices, line_first(): return (value, lax.ppermute(value, 'dp', [(0, 1), (3, 2)]))  28.2 us
    ppermute x29, starting transfers between devices, swap(): return lax.ppermute(value, axis, SWAP)  23.6 us
    unnamed x127, local copies, waits for them, and re-layouts  11.8 us
    ppermute x10, starting transfers between devices, line_next(): return (total, lax.ppermute(total, 'dp', pairs))  11 us
    all_gather x1, blocking collectives, per_device(): sums = jnp.sum(lax.all_gather(sums, ('row', 'y', 'core')), 0)  9.36 us
  transfers between devices with their start and end apart: 48, of which 14 were waited for; matrix products, arithmetic and copies ran while one was open for 7% of the time, Pallas kernels for 38%

profile of v1, /device:TPU:0, one launch (start us, length us, event | category | flops | bytes accessed | tf_op | source)
XLA Modules:
  0.0 301.6 jit_solution(470189845941286728)
XLA Ops:
  0.7 3.0 collective-permute-start
  3.7 1.5 collective-permute-start.1
  5.8 3.2 %pack_decoder.1 = (bf16[2448,128]{1,0:T(8,128)(2,1)}, bf16[2448,128]{1,0:T(8,128)(2,1)}) custom-call(s32[4]{0:T(128)} %pad_add_fusion.refs_0_, bf16[3,128,256]{2,1,0:T(8,128)(2,1)} %bitcast.48, bf16[256,128]{1,0:T(8,128)(2,1)} %refs_2_.1, bf16[128,1024]{1,0:T(8,128)(2,1)} %refs_3_.1, bf16[1024,128]{1,0:T(8,128)(2,1)} %refs_4_.1, f32[1,128]{1,0:T(1,128)} %bitcast.53, ...), custom_call_target="tpu_custom_call" | custom-call | flops 10000000 | bytes 1 | tf_op jit(solution)/shard_map/pack_decoder/pallas_call | solution.py:315
  9.1 2.1 copy.46
  11.2 2.3 pack_mixing.1.refs_3_.refs_1_
  14.6 2.5 pack_encoder.1.refs_4_.refs_2_
  17.2 1.5 join_decoder.1
  19.4 1.5 collective-permute-start.5
  20.9 1.5 collective-permute-start.6
  22.4 7.7 %collective-permute-done.2.refs_4_.refs_2_ = bf16[2352,128]{1,0:T(8,128)(2,1)S(1)} collective-permute-done((bf16[2352,128]{1,0:T(8,128)(2,1)}, bf16[2352,128]{1,0:T(8,128)(2,1)S(1)}, u32[]{:S(2)}, u32[]{:S(2)}) %collective-permute-start.2) | collective-permute-done | bytes 602144 | tf_op jit(solution)/shard_map/ppermute | solution.py:235
  32.5 1.6 collective-permute-start.9
  34.4 3.0 join_input.1.refs_1_
  38.0 1.7 collective-permute-start.14
  39.6 1.7 collective-permute-done.9.refs_5_
  41.3 2.5 collective-permute-start.11
  43.8 1.4 collective-permute-start.12
  46.5 1.7 first_norm.1
  48.3 4.4 %encoder_mixing.1 = (bf16[1024,1152]{1,0:T(8,128)(2,1)S(1)}, bf16[768,1152]{1,0:T(8,128)(2,1)S(1)}, bf16[384,768]{1,0:T(8,128)(2,1)S(1)}) custom-call(bf16[1024,768]{1,0:T(8,128)(2,1)S(1)} %get-tuple-element.169.refs_0_, bf16[2352,128]{1,0:T(8,128)(2,1)S(1)} %copy-done.13, bf16[2352,128]{1,0:T(8,128)(2,1)S(1)} %collective-permute-done.2.refs_4_.refs_2_, ...), custom_call_target="tpu_custom_call" | custom-call | flops 30000000 | bytes 1 | tf_op jit(solution)/shard_map/encoder_mixing/pallas_call | solution.py:315
  53.9 11.3 %encoder_attend.1 = (bf16[1024,384]{1,0:T(8,128)(2,1)S(1)}, f32[1024,384]{1,0:T(8,128)S(1)}, bf16[1024,768]{1,0:T(8,128)(2,1)S(1)}) custom-call(bf16[1024,1152]{1,0:T(8,128)(2,1)S(1)} %get-tuple-element.170.refs_0_.q_ref.k_ref.v_ref, s32[1024,1]{1,0:T(8,128)S(1)} %copy.47.refs_1_, bf16[384,768]{1,0:T(8,128)(2,1)S(1)} %get-tuple-element.171.refs_2_.refs_6_), custom_call_target="tpu_custom_call" | custom-call | flops 120000000 | bytes 1 | tf_op jit(solution)/shard_map/encoder_attend/pallas_call | solution.py:315
  65.3 10.9 %collective-permute-done.11.refs_5_.refs_3_ = bf16[4608,128]{1,0:T(8,128)(2,1)S(1)} collective-permute-done((bf16[4608,128]{1,0:T(8,128)(2,1)S(1)}, bf16[4608,128]{1,0:T(8,128)(2,1)S(1)}, u32[]{:S(2)}, u32[]{:S(2)}) %collective-permute-start.11) | collective-permute-done | bytes 1179680 | tf_op jit(solution)/shard_map/ppermute | solution.py:235
  76.3 1.6 collective-permute-start.15
  77.9 1.5 collective-permute-start.16
  81.8 10.7 %collective-permute-done.15.refs_7_.refs_5_ = bf16[2304,128]{1,0:T(8,128)(2,1)S(1)} collective-permute-done((bf16[2304,128]{1,0:T(8,128)(2,1)S(1)}, bf16[2304,128]{1,0:T(8,128)(2,1)S(1)}, u32[]{:S(2)}, u32[]{:S(2)}) %collective-permute-start.15) | collective-permute-done | bytes 589856 | tf_op jit(solution)/shard_map/ppermute | solution.py:235
  92.6 1.6 collective-permute-done.16.refs_8_.refs_6_
  94.2 1.5 collective-permute-start.21
  96.2 9.2 %feed_forward.1 = (f32[1024,768]{1,0:T(8,128)S(1)}, bf16[1024,768]{1,0:T(8,128)(2,1)S(1)}, bf16[1024,1536]{1,0:T(8,128)(2,1)S(1)}, bf16[1024,1536]{1,0:T(8,128)(2,1)S(1)}, bf16[1024,768]{1,0:T(8,128)(2,1)S(1)}) custom-call(bf16[1024,768]{1,0:T(8,128)(2,1)S(1)} %get-tuple-element.168.refs_0_.refs_3_, bf16[1024,768]{1,0:T(8,128)(2,1)S(1)} %get-tuple-element.172.refs_1_, ...), custom_call_target="tpu_custom_call" | custom-call | flops 120000000 | bytes 1 | tf_op jit(solution)/shard_map/feed_forward/pallas_call | solution.py:315
  106.6 1.5 collective-permute-start.23
  108.9 6.1 %bridge.1 = (f32[256,384]{1,0:T(8,128)}, bf16[1024,384]{1,0:T(8,128)(2,1)S(1)}, f32[1024,512]{1,0:T(8,128)S(1)}, bf16[1024,512]{1,0:T(8,128)(2,1)S(1)}, bf16[102...) custom-call(s32[4]{0:T(128)S(1)} %copy-done.45, ...), custom_call_target="tpu_custom_call" | custom-call | flops 57000000 | bytes 1 | tf_op jit(solution)/shard_map/bridge/pallas_call | solution.py:315
  114.9 10.9 %decoder_attend.1 = (bf16[1024,256]{1,0:T(8,128)(2,1)S(1)}, f32[1024,256]{1,0:T(8,128)S(1)}, bf16[1024,512]{1,0:T(8,128)(2,1)S(1)}) custom-call(bf16[1024,768]{1,0:T(8,128)(2,1)S(1)} %get-tuple-element.187.refs_0_.q_ref.k_ref.v_ref, s32[1024,1]{1,0:T(8,128)S(1)} %copy.47.refs_1_, bf16[256,512]{1,0:T(8,128)(2,1)S(1)} %get-tuple-element.188.refs_2_.refs_6_), custom_call_target="tpu_custom_call" | custom-call | flops 110000000 | bytes 1 | tf_op jit(solution)/shard_map/decoder_attend/pallas_call | solution.py:315
  126.1 5.8 %collective-permute-done.23.refs_8_ = bf16[3072,128]{1,0:T(8,128)(2,1)S(1)} collective-permute-done((bf16[3072,128]{1,0:T(8,128)(2,1)}, bf16[3072,128]{1,0:T(8,128)(2,1)S(1)}, u32[]{:S(2)}, u32[]{:S(2)}) %collective-permute-start.23) | collective-permute-done | bytes 786464 | tf_op jit(solution)/shard_map/ppermute | solution.py:255
  131.9 8.3 %decoder_feed.1 = (f32[1024,512]{1,0:T(8,128)S(1)}, bf16[1024,512]{1,0:T(8,128)(2,1)S(1)}, bf16[1024,1024]{1,0:T(8,128)(2,1)S(1)}, bf16[1024,1024]{1,0:T(8,128)(...) custom-call(s32[4]{0:T(128)S(1)} %copy-done.45, ...), custom_call_target="tpu_custom_call" | custom-call | flops 80000000 | bytes 1 | tf_op jit(solution)/shard_map/decoder_feed/pallas_call | solution.py:315
  141.6 3.5 %collective-permute-start.25 = (bf16[2048,128]{1,0:T(8,128)(2,1)S(1)}, bf16[2048,128]{1,0:T(8,128)(2,1)S(1)}, u32[]{:S(2)}, u32[]{:S(2)}) collective-permute-start(bf16[2048,128]{1,0:T(8,128)(2,1)S(1)} %decoder_feed_grads.1), channel_id=1, source_target_pairs={{0,8},{24,16},{1,9},{25,17},{2,10},{26,18},{3,11},{27,19},{4,12},{... | collective-permute-start | bytes 1572872 | tf_op jit(solution)/shard_map/ppermute | solution.py:1033
  145.2 2.6 decoder_middle_back.1
  147.8 9.4 %attention_backward.5 = (bf16[1024,128]{1,0:T(8,128)(2,1)S(1)}, bf16[1024,128]{1,0:T(8,128)(2,1)S(1)}, bf16[1024,128]{1,0:T(8,128)(2,1)S(1)}) custom-call(bf16[1024,768]{1,0:T(8,128)(2,1)S(1)} %get-tuple-element.187.refs_0_.q_ref.k_ref.v_ref, bf16[1024,768]{1,0:T(8,128)(2,1)S(1)} %get-tuple-element.187.refs_0_.q_ref.k_ref.v_ref, ...), custom_call_target="tpu_custom_call" | custom-call | flops 96000000 | bytes 1 | tf_op jit(solution)/shard_map/attention_backward/pallas_call | solution.py:202
  158.1 9.6 %attention_backward.6 = (bf16[1024,128]{1,0:T(8,128)(2,1)S(1)}, bf16[1024,128]{1,0:T(8,128)(2,1)S(1)}, bf16[1024,128]{1,0:T(8,128)(2,1)S(1)}) custom-call(bf16[1024,768]{1,0:T(8,128)(2,1)S(1)} %get-tuple-element.187.refs_0_.q_ref.k_ref.v_ref, bf16[1024,768]{1,0:T(8,128)(2,1)S(1)} %get-tuple-element.187.refs_0_.q_ref.k_ref.v_ref, ...), custom_call_target="tpu_custom_call" | custom-call | flops 96000000 | bytes 1 | tf_op jit(solution)/shard_map/attention_backward/pallas_call | solution.py:202
  169.2 2.6 collective-permute-done.27.refs_2_
  171.8 3.9 %bridge_back.1 = (bf16[1024,512]{1,0:T(8,128)(2,1)S(1)}, f32[1024,768]{1,0:T(8,128)S(1)}, bf16[1024,768]{1,0:T(8,128)(2,1)S(1)}, f32[2,512]{1,0:T(2,128)S(1)}) custom-call(s32[4]{0:T(128)S(1)} %copy-done.45, bf16[1024,512]{1,0:T(8,128)(2,1)S(1)} %decoder_mixed_back.1.refs_1_, bf16[1024,512]{1,0:T(8,128)(2,1)S(1)} %collective-permute-done.27.refs_2_, ...), custom_call_target="tpu_custom_call" | custom-call | flops 39000000 | bytes 1 | tf_op jit(solution)/shard_map/bridge_back/pallas_call | solution.py:315
  176.7 8.2 %collective-permute-start.28 = (bf16[768,384]{1,0:T(8,128)(2,1)S(1)}, bf16[768,384]{1,0:T(8,128)(2,1)S(1)}, u32[]{:S(2)}, u32[]{:S(2)}) collective-permute-start(bf16[768,384]{1,0:T(8,128)(2,1)S(1)} %encoder_down_grads.1), channel_id=1, source_target_pairs={{0,8},{24,16},{1,9},{25,17},{2,10},{26,18},{3,11},{27,19},{4,12},{... | collective-permute-start | bytes 1769480 | tf_op jit(solution)/shard_map/ppermute | solution.py:1033
  186.5 7.4 %feed_back.1 = (bf16[1024,1536]{1,0:T(8,128)(2,1)S(1)}, bf16[1024,768]{1,0:T(8,128)(2,1)S(1)}) custom-call(bf16[1024,768]{1,0:T(8,128)(2,1)S(1)} %get-tuple-element.228.refs_1_.refs_0_, bf16[1024,1536]{1,0:T(8,128)(2,1)S(1)} %get-tuple-element.229.refs_1_, bf16[4608,128]{1,0:T(8,128)(2,1)S(1)} %copy-done.6, ...), custom_call_target="tpu_custom_call" | custom-call | flops 120000000 | bytes 1 | tf_op jit(solution)/shard_map/feed_back/pallas_call | solution.py:315
  194.0 3.8 %collective-permute-done.28 = bf16[768,384]{1,0:T(8,128)(2,1)S(1)} collective-permute-done((bf16[768,384]{1,0:T(8,128)(2,1)S(1)}, bf16[768,384]{1,0:T(8,128)(2,1)S(1)}, u32[]{:S(2)}, u32[]{:S(2)}) %collective-permute-start.28) | collective-permute-done | bytes 589856 | tf_op jit(solution)/shard_map/ppermute | solution.py:1033
  198.7 4.4 %collective-permute-start.32 = (bf16[384,768]{1,0:T(8,128)(2,1)S(1)}, bf16[384,768]{1,0:T(8,128)(2,1)S(1)}, u32[]{:S(2)}, u32[]{:S(2)}) collective-permute-start(bf16[384,768]{1,0:T(8,128)(2,1)S(1)} %encoder_up_grads.1), channel_id=1, source_target_pairs={{0,8},{24,16},{1,9},{25,17},{2,10},{26,18},{3,11},{27,19},{4,12},{... | collective-permute-start | bytes 1769480 | tf_op jit(solution)/shard_map/ppermute | solution.py:1033
  203.9 4.0 %collective-permute-start.31 = (bf16[1408,128]{1,0:T(8,128)(2,1)S(1)}, bf16[1408,128]{1,0:T(8,128)(2,1)S(1)}, u32[]{:S(2)}, u32[]{:S(2)}) collective-permute-start(bf16[1408,128]{1,0:T(8,128)(2,1)S(1)} %decoder_mixing_grads.1), channel_id=1, source_target_pairs={{0,8},{24,16},{1,9},{25,17},{2,10},{26,18},{3,11},{27,19},{4,12},{... | collective-permute-start | bytes 1081352 | tf_op jit(solution)/shard_map/ppermute | solution.py:1033
  209.3 3.9 %encoder_middle_back.1 = (f32[1024,768]{1,0:T(8,128)S(1)}, bf16[1024,384]{1,0:T(8,128)(2,1)S(1)}, f32[1024,384]{1,0:T(8,128)S(1)}, f32[2,768]{1,0:T(2,128)S(1)}) custom-call(s32[4]{0:T(128)S(1)} %copy-done.45, bf16[1024,768]{1,0:T(8,128)(2,1)S(1)} %get-tuple-element.236.refs_1_, bf16[1024,768]{1,0:T(8,128)(2,1)S(1)} %collective-permute-done.29.refs_2_, ...), custom_call_target="tpu_custom_call" | custom-call | flops 55000000 | bytes 1 | tf_op jit(solution)/shard_map/encoder_middle_back/pallas_call | solution.py:315
  213.2 1.7 copy-done.14
  214.8 5.2 %attention_backward.7 = (bf16[1024,128]{1,0:T(8,128)(2,1)S(1)}, bf16[1024,128]{1,0:T(8,128)(2,1)S(1)}, bf16[1024,128]{1,0:T(8,128)(2,1)S(1)}) custom-call(bf16[1024,1152]{1,0:T(8,128)(2,1)S(1)} %copy-done.1, bf16[1024,1152]{1,0:T(8,128)(2,1)S(1)} %copy-done.1, bf16[1024,1152]{1,0:T(8,128)(2,1)S(1)} %copy-done.1, ...), custom_call_target="tpu_custom_call" | custom-call | flops 52000000 | bytes 1 | tf_op jit(solution)/shard_map/attention_backward/pallas_call | solution.py:202
  220.1 2.8 collective-permute-done.31
  223.8 1.5 collective-permute-start.36
  228.4 5.6 %attention_backward.8 = (bf16[1024,128]{1,0:T(8,128)(2,1)S(1)}, bf16[1024,128]{1,0:T(8,128)(2,1)S(1)}, bf16[1024,128]{1,0:T(8,128)(2,1)S(1)}) custom-call(bf16[1024,1152]{1,0:T(8,128)(2,1)S(1)} %copy-done.1, bf16[1024,1152]{1,0:T(8,128)(2,1)S(1)} %copy-done.1, bf16[1024,1152]{1,0:T(8,128)(2,1)S(1)} %copy-done.1, ...), custom_call_target="tpu_custom_call" | custom-call | flops 52000000 | bytes 1 | tf_op jit(solution)/shard_map/attention_backward/pallas_call | solution.py:202
  234.1 1.9 encoder_mixing_grads.1
  236.1 8.1 %collective-permute-start.34 = (bf16[2304,128]{1,0:T(8,128)(2,1)}, bf16[2304,128]{1,0:T(8,128)(2,1)}, u32[]{:S(2)}, u32[]{:S(2)}) collective-permute-start(bf16[2304,128]{1,0:T(8,128)(2,1)} %encoder_mixing_grads.1), channel_id=1, source_target_pairs={{0,8},{24,16},{1,9},{25,17},{2,10},{26,18},{3,11},{27,19},{4,12},{... | collective-permute-start | bytes 1769480 | tf_op jit(solution)/shard_map/ppermute | solution.py:1033
  246.4 1.4 copy-done.5
  247.8 5.2 %attention_backward.9 = (bf16[1024,128]{1,0:T(8,128)(2,1)S(1)}, bf16[1024,128]{1,0:T(8,128)(2,1)S(1)}, bf16[1024,128]{1,0:T(8,128)(2,1)S(1)}) custom-call(bf16[1024,1152]{1,0:T(8,128)(2,1)S(1)} %copy-done.1, bf16[1024,1152]{1,0:T(8,128)(2,1)S(1)} %copy-done.1, bf16[1024,1152]{1,0:T(8,128)(2,1)S(1)} %copy-done.1, ...), custom_call_target="tpu_custom_call" | custom-call | flops 52000000 | bytes 1 | tf_op jit(solution)/shard_map/attention_backward/pallas_call | solution.py:202
  253.1 1.4 collective-permute-done.34
  254.5 1.4 add_convert_fusion.1
  256.6 1.5 collective-permute-start.47
  258.2 1.8 encoder_mixed_back.1
  261.7 1.9 input_back.1
  263.7 9.4 %all-gather = f32[64,768]{1,0:T(8,128)S(1)} all-gather(f32[8,768]{1,0:T(8,128)S(1)} %select_maximum_fusion), channel_id=2, replica_groups=mesh['dp'=4,'row'=2,'y'=2,'core'=2] {'row','y','core'}, dimensions={0}, use_global_device_ids=true | all-gather | bytes 221184 | tf_op jit(solution)/shard_map/all_gather | solution.py:1477
  276.0 4.3 %collective-permute-start.42 = (f32[8,768]{1,0:T(8,128)S(1)}, f32[8,768]{1,0:T(8,128)S(1)}, u32[]{:S(2)}, u32[]{:S(2)}) collective-permute-start(f32[8,768]{1,0:T(8,128)S(1)} %bitcast_reduce_fusion), channel_id=1, source_target_pairs={{0,16},{8,24},{16,0},{24,8},{1,17},{9,25},{17,1},{25,9},{2,18},{10... | collective-permute-start | bytes 73736 | tf_op jit(solution)/shard_map/ppermute | solution.py:1071
  280.3 1.6 collective-permute-start.43
  283.7 2.3 select_convert_fusion.1
  287.7 6.7 %collective-permute-done.41 = f32[8,768]{1,0:T(8,128)S(1)} collective-permute-done((f32[8,768]{1,0:T(8,128)S(1)}, f32[8,768]{1,0:T(8,128)S(1)}, u32[]{:S(2)}, u32[]{:S(2)}) %collective-permute-start.41) | collective-permute-done | bytes 24608 | tf_op jit(solution)/shard_map/ppermute | solution.py:1071
  295.7 1.7 convert_add_fusion
  297.4 1.9 decoder_unpack.1
  (238 shorter events, 41.3 us)
Async XLA Ops:
  0.7 10.5 %collective-permute-start = (bf16[256,384]{1,0:T(8,128)(2,1)}, bf16[256,384]{1,0:T(8,128)(2,1)S(1)}, u32[]{:S(2)}, u32[]{:S(2)}) collective-permute-start(bf16[256,384]{1,0:T(8,128)(2,1)} %refs_1_.4), channel_id=1, source_target_pairs={{0,4},{4,0},{1,5},{5,1},{2,6},{6,2},{3,7},{7,3},{8,12},{12,8},{9,1... | collective-permute-start | bytes 589832 | tf_op jit(solution)/shard_map/ppermute | solution.py:235
  3.7 7.5 %collective-permute-start.1 = (bf16[256,384]{1,0:T(8,128)(2,1)}, bf16[256,384]{1,0:T(8,128)(2,1)S(1)}, u32[]{:S(2)}, u32[]{:S(2)}) collective-permute-start(bf16[256,384]{1,0:T(8,128)(2,1)} %refs_1_.4), channel_id=1, source_target_pairs={{0,2},{2,0},{1,3},{3,1},{4,6},{6,4},{5,7},{7,5},{8,10},{10,8},{9,1... | collective-permute-start | bytes 589832 | tf_op jit(solution)/shard_map/ppermute | solution.py:235
  9.0 8.2 %collective-permute-start.4 = (bf16[2448,128]{1,0:T(8,128)(2,1)}, bf16[2448,128]{1,0:T(8,128)(2,1)S(1)}, u32[]{:S(2)}, u32[]{:S(2)}) collective-permute-start(bf16[2448,128]{1,0:T(8,128)(2,1)} %get-tuple-element.161), channel_id=1, source_target_pairs={{0,1},{1,0},{2,3},{3,2},{4,5},{5,4},{6,7},{7,6},{8,9},{9,8},{10,11... | collective-permute-start | bytes 1880072 | tf_op jit(solution)/shard_map/ppermute | solution.py:235
  13.4 16.7 %collective-permute-start.2 = (bf16[2352,128]{1,0:T(8,128)(2,1)}, bf16[2352,128]{1,0:T(8,128)(2,1)S(1)}, u32[]{:S(2)}, u32[]{:S(2)}) collective-permute-start(bf16[2352,128]{1,0:T(8,128)(2,1)} %pack_mixing.1.refs_3_.refs_1_), channel_id=1, source_target_pairs={{0,4},{4,0},{1,5},{5,1},{2,6},{6,2},{3,7},{7,3},{8,12},{12,8},{9,1... | collective-permute-start | bytes 1806344 | tf_op jit(solution)/shard_map/ppermute | solution.py:235
  14.1 16.8 %collective-permute-start.3 = (bf16[2352,128]{1,0:T(8,128)(2,1)}, bf16[2352,128]{1,0:T(8,128)(2,1)S(1)}, u32[]{:S(2)}, u32[]{:S(2)}) collective-permute-start(bf16[2352,128]{1,0:T(8,128)(2,1)} %pack_mixing.1.refs_3_.refs_1_), channel_id=1, source_target_pairs={{0,2},{2,0},{1,3},{3,1},{4,6},{6,4},{5,7},{7,5},{8,10},{10,8},{9,1... | collective-permute-start | bytes 1806344 | tf_op jit(solution)/shard_map/ppermute | solution.py:235
  17.1 17.1 %copy-start.41 = (s32[1024]{0:T(1024)S(1)}, s32[1024]{0:T(1024)}, u32[]{:S(2)}) copy-start(s32[1024]{0:T(1024)} %param.21) | copy-start | bytes 12292
  19.4 21.8 %copy-start.6 = (bf16[4608,128]{1,0:T(8,128)(2,1)S(1)}, bf16[4608,128]{1,0:T(8,128)(2,1)}, u32[]{:S(2)}) copy-start(bf16[4608,128]{1,0:T(8,128)(2,1)} %pack_encoder.1.refs_4_.refs_2_) | copy-start | bytes 3538948
  19.4 12.6 %collective-permute-start.5 = (bf16[128,384]{1,0:T(8,128)(2,1)S(1)}, bf16[128,384]{1,0:T(8,128)(2,1)S(1)}, u32[]{:S(2)}, u32[]{:S(2)}) collective-permute-start(bf16[128,384]{1,0:T(8,128)(2,1)S(1)} %slice.104), channel_id=1, source_target_pairs={{0,2},{2,0},{1,3},{3,1},{4,6},{6,4},{5,7},{7,5},{8,10},{10,8},{9,1... | collective-permute-start | bytes 294920 | tf_op jit(solution)/shard_map/ppermute | solution.py:235
  20.9 11.1 %collective-permute-start.6 = (bf16[128,384]{1,0:T(8,128)(2,1)S(1)}, bf16[128,384]{1,0:T(8,128)(2,1)S(1)}, u32[]{:S(2)}, u32[]{:S(2)}) collective-permute-start(bf16[128,384]{1,0:T(8,128)(2,1)S(1)} %slice.105), channel_id=1, source_target_pairs={{0,4},{4,0},{1,5},{5,1},{2,6},{6,2},{3,7},{7,3},{8,12},{12,8},{9,1... | collective-permute-start | bytes 294920 | tf_op jit(solution)/shard_map/ppermute | solution.py:235
  32.1 11.7 %collective-permute-start.8 = (bf16[1200,128]{1,0:T(8,128)(2,1)}, bf16[1200,128]{1,0:T(8,128)(2,1)S(1)}, u32[]{:S(2)}, u32[]{:S(2)}) collective-permute-start(bf16[1200,128]{1,0:T(8,128)(2,1)} %slice.106), channel_id=1, source_target_pairs={{0,2},{2,0},{1,3},{3,1},{4,6},{6,4},{5,7},{7,5},{8,10},{10,8},{9,1... | collective-permute-start | bytes 921608 | tf_op jit(solution)/shard_map/ppermute | solution.py:235
  32.5 8.8 %collective-permute-start.9 = (bf16[1152,128]{1,0:T(8,128)(2,1)}, bf16[1152,128]{1,0:T(8,128)(2,1)}, u32[]{:S(2)}, u32[]{:S(2)}) collective-permute-start(bf16[1152,128]{1,0:T(8,128)(2,1)} %slice.107), channel_id=1, source_target_pairs={{0,4},{4,0},{1,5},{5,1},{2,6},{6,2},{3,7},{7,3},{8,12},{12,8},{9,1... | collective-permute-start | bytes 884744 | tf_op jit(solution)/shard_map/ppermute | solution.py:235
  37.4 7.8 %collective-permute-start.7 = (bf16[512,768]{1,0:T(8,128)(2,1)}, bf16[512,768]{1,0:T(8,128)(2,1)S(1)}, u32[]{:S(2)}, u32[]{:S(2)}) collective-permute-start(bf16[512,768]{1,0:T(8,128)(2,1)} %join_input.1.refs_1_), channel_id=1, source_target_pairs={{0,1},{1,0},{2,3},{3,2},{4,5},{5,4},{6,7},{7,6},{8,9},{9,8},{10,11... | collective-permute-start | bytes 2359304 | tf_op jit(solution)/shard_map/ppermute | solution.py:235
  37.5 38.8 %collective-permute-start.13 = (bf16[1824,128]{1,0:T(8,128)(2,1)S(1)}, bf16[1824,128]{1,0:T(8,128)(2,1)S(1)}, u32[]{:S(2)}, u32[]{:S(2)}) collective-permute-start(bf16[1824,128]{1,0:T(8,128)(2,1)S(1)} %copy-done.40), channel_id=1, source_target_pairs={{0,4},{4,0},{1,5},{5,1},{2,6},{6,2},{3,7},{7,3},{8,12},{12,8},{9,1... | collective-permute-start | bytes 1400840 | tf_op jit(solution)/shard_map/ppermute | solution.py:235
  38.0 38.3 %collective-permute-start.14 = (bf16[1824,128]{1,0:T(8,128)(2,1)S(1)}, bf16[1824,128]{1,0:T(8,128)(2,1)S(1)}, u32[]{:S(2)}, u32[]{:S(2)}) collective-permute-start(bf16[1824,128]{1,0:T(8,128)(2,1)S(1)} %copy-done.40), channel_id=1, source_target_pairs={{0,2},{2,0},{1,3},{3,1},{4,6},{6,4},{5,7},{7,5},{8,10},{10,8},{9,1... | collective-permute-start | bytes 1400840 | tf_op jit(solution)/shard_map/ppermute | solution.py:235
  41.3 34.9 %collective-permute-start.11 = (bf16[4608,128]{1,0:T(8,128)(2,1)S(1)}, bf16[4608,128]{1,0:T(8,128)(2,1)S(1)}, u32[]{:S(2)}, u32[]{:S(2)}) collective-permute-start(bf16[4608,128]{1,0:T(8,128)(2,1)S(1)} %copy-done.6), channel_id=1, source_target_pairs={{0,4},{4,0},{1,5},{5,1},{2,6},{6,2},{3,7},{7,3},{8,12},{12,8},{9,1... | collective-permute-start | bytes 3538952 | tf_op jit(solution)/shard_map/ppermute | solution.py:235
  43.8 32.4 %collective-permute-start.12 = (bf16[4608,128]{1,0:T(8,128)(2,1)S(1)}, bf16[4608,128]{1,0:T(8,128)(2,1)S(1)}, u32[]{:S(2)}, u32[]{:S(2)}) collective-permute-start(bf16[4608,128]{1,0:T(8,128)(2,1)S(1)} %copy-done.6), channel_id=1, source_target_pairs={{0,2},{2,0},{1,3},{3,1},{4,6},{6,4},{5,7},{7,5},{8,10},{10,8},{9,1... | collective-permute-start | bytes 3538952 | tf_op jit(solution)/shard_map/ppermute | solution.py:235
  48.3 47.9 %copy-start.9 = (bf16[1024,768]{1,0:T(8,128)(2,1)}, bf16[1024,768]{1,0:T(8,128)(2,1)S(1)}, u32[]{:S(2)}) copy-start(bf16[1024,768]{1,0:T(8,128)(2,1)S(1)} %get-tuple-element.168.refs_0_.refs_3_) | copy-start | bytes 4718596
  48.3 47.9 %copy-start.46 = (f32[4,768]{1,0:T(4,128)}, f32[4,768]{1,0:T(4,128)S(1)}, u32[]{:S(2)}) copy-start(f32[4,768]{1,0:T(4,128)S(1)} %get-tuple-element.173.refs_3_.refs_5_) | copy-start | bytes 36868
  53.9 11.3 %copy-start = (bf16[1024,1152]{1,0:T(8,128)(2,1)}, bf16[1024,1152]{1,0:T(8,128)(2,1)S(1)}, u32[]{:S(2)}) copy-start(bf16[1024,1152]{1,0:T(8,128)(2,1)S(1)} %get-tuple-element.170.refs_0_.q_ref.k_ref.v_ref) | copy-start | bytes 7077892
  53.9 11.3 %copy-start.22 = (bf16[384,768]{1,0:T(8,128)(2,1)}, bf16[384,768]{1,0:T(8,128)(2,1)S(1)}, u32[]{:S(2)}) copy-start(bf16[384,768]{1,0:T(8,128)(2,1)S(1)} %get-tuple-element.171.refs_2_.refs_6_) | copy-start | bytes 1769476
  65.3 163.1 %copy-start.2 = (f32[1024,384]{1,0:T(8,128)}, f32[1024,384]{1,0:T(8,128)S(1)}, u32[]{:S(2)}) copy-start(f32[1024,384]{1,0:T(8,128)S(1)} %get-tuple-element.196.inv_ref) | copy-start | bytes 4718596
  76.2 19.9 %copy-start.7 = (bf16[4608,128]{1,0:T(8,128)(2,1)}, bf16[4608,128]{1,0:T(8,128)(2,1)S(1)}, u32[]{:S(2)}) copy-start(bf16[4608,128]{1,0:T(8,128)(2,1)S(1)} %collective-permute-done.12.refs_6_.refs_4_) | copy-start | bytes 3538948
  76.3 16.3 %collective-permute-start.15 = (bf16[2304,128]{1,0:T(8,128)(2,1)S(1)}, bf16[2304,128]{1,0:T(8,128)(2,1)S(1)}, u32[]{:S(2)}, u32[]{:S(2)}) collective-permute-start(bf16[2304,128]{1,0:T(8,128)(2,1)S(1)} %slice.108), channel_id=1, source_target_pairs={{0,2},{2,0},{1,3},{3,1},{4,6},{6,4},{5,7},{7,5},{8,10},{10,8},{9,1... | collective-permute-start | bytes 1769480 | tf_op jit(solution)/shard_map/ppermute | solution.py:235
  77.9 16.2 %collective-permute-start.16 = (bf16[2304,128]{1,0:T(8,128)(2,1)S(1)}, bf16[2304,128]{1,0:T(8,128)(2,1)S(1)}, u32[]{:S(2)}, u32[]{:S(2)}) collective-permute-start(bf16[2304,128]{1,0:T(8,128)(2,1)S(1)} %slice.109), channel_id=1, source_target_pairs={{0,4},{4,0},{1,5},{5,1},{2,6},{6,2},{3,7},{7,3},{8,12},{12,8},{9,1... | collective-permute-start | bytes 1769480 | tf_op jit(solution)/shard_map/ppermute | solution.py:235
  80.8 27.3 %collective-permute-start.19 = (bf16[1024,128]{1,0:T(8,128)(2,1)}, bf16[1024,128]{1,0:T(8,128)(2,1)}, u32[]{:S(2)}, u32[]{:S(2)}) collective-permute-start(bf16[1024,128]{1,0:T(8,128)(2,1)} %slice.111), channel_id=1, source_target_pairs={{0,4},{4,0},{1,5},{5,1},{2,6},{6,2},{3,7},{7,3},{8,12},{12,8},{9,1... | collective-permute-start | bytes 786440 | tf_op jit(solution)/shard_map/ppermute | solution.py:235
  81.3 25.2 %collective-permute-start.18 = (bf16[800,128]{1,0:T(8,128)(2,1)}, bf16[800,128]{1,0:T(8,128)(2,1)}, u32[]{:S(2)}, u32[]{:S(2)}) collective-permute-start(bf16[800,128]{1,0:T(8,128)(2,1)} %slice.110), channel_id=1, source_target_pairs={{0,2},{2,0},{1,3},{3,1},{4,6},{6,4},{5,7},{7,5},{8,10},{10,8},{9,1... | collective-permute-start | bytes 614408 | tf_op jit(solution)/shard_map/ppermute | solution.py:235
  81.8 14.3 %collective-permute-start.10 = (bf16[1024,768]{1,0:T(8,128)(2,1)S(1)}, bf16[1024,768]{1,0:T(8,128)(2,1)S(1)}, u32[]{:S(2)}, u32[]{:S(2)}) collective-permute-start(bf16[1024,768]{1,0:T(8,128)(2,1)S(1)} %get-tuple-element.172.refs_1_), channel_id=1, source_target_pairs={{0,1},{1,0},{2,3},{3,2},{4,5},{5,4},{6,7},{7,6},{8,9},{9,8},{10,11... | collective-permute-start | bytes 4718600 | tf_op jit(solution)/shard_map/ppermute | solution.py:235
  94.2 31.9 %collective-permute-start.21 = (bf16[3072,128]{1,0:T(8,128)(2,1)}, bf16[3072,128]{1,0:T(8,128)(2,1)}, u32[]{:S(2)}, u32[]{:S(2)}) collective-permute-start(bf16[3072,128]{1,0:T(8,128)(2,1)} %get-tuple-element.275.refs_5_), channel_id=1, source_target_pairs={{0,4},{4,0},{1,5},{5,1},{2,6},{6,2},{3,7},{7,3},{8,12},{12,8},{9,1... | collective-permute-start | bytes 2359304 | tf_op jit(solution)/shard_map/ppermute | solution.py:235
  95.7 30.4 %collective-permute-start.22 = (bf16[3072,128]{1,0:T(8,128)(2,1)}, bf16[3072,128]{1,0:T(8,128)(2,1)}, u32[]{:S(2)}, u32[]{:S(2)}) collective-permute-start(bf16[3072,128]{1,0:T(8,128)(2,1)} %get-tuple-element.275.refs_5_), channel_id=1, source_target_pairs={{0,2},{2,0},{1,3},{3,1},{4,6},{6,4},{5,7},{7,5},{8,10},{10,8},{9,1... | collective-permute-start | bytes 2359304 | tf_op jit(solution)/shard_map/ppermute | solution.py:235
  105.4 3.5 %collective-permute-start.17 = (bf16[1024,768]{1,0:T(8,128)(2,1)S(1)}, bf16[1024,768]{1,0:T(8,128)(2,1)S(1)}, u32[]{:S(2)}, u32[]{:S(2)}) collective-permute-start(bf16[1024,768]{1,0:T(8,128)(2,1)S(1)} %get-tuple-element.181.refs_2_), channel_id=1, source_target_pairs={{0,1},{1,0},{2,3},{3,2},{4,5},{5,4},{6,7},{7,6},{8,9},{9,8},{10,11... | collective-permute-start | bytes 4718600 | tf_op jit(solution)/shard_map/ppermute | solution.py:235
  106.6 25.4 %collective-permute-start.23 = (bf16[3072,128]{1,0:T(8,128)(2,1)}, bf16[3072,128]{1,0:T(8,128)(2,1)S(1)}, u32[]{:S(2)}, u32[]{:S(2)}) collective-permute-start(bf16[3072,128]{1,0:T(8,128)(2,1)} %get-tuple-element.275.refs_5_), channel_id=1, source_target_pairs={{0,6},{2,4},{4,2},{6,0},{1,7},{3,5},{5,3},{7,1},{8,14},{10,12},{12... | collective-permute-start | bytes 2359304 | tf_op jit(solution)/shard_map/ppermute | solution.py:255
  125.9 6.0 %collective-permute-start.20 = (bf16[1024,512]{1,0:T(8,128)(2,1)S(1)}, bf16[1024,512]{1,0:T(8,128)(2,1)S(1)}, u32[]{:S(2)}, u32[]{:S(2)}) collective-permute-start(bf16[1024,512]{1,0:T(8,128)(2,1)S(1)} %get-tuple-element.189.refs_2_), channel_id=1, source_target_pairs={{0,1},{1,0},{2,3},{3,2},{4,5},{5,4},{6,7},{7,6},{8,9},{9,8},{10,11... | collective-permute-start | bytes 3145736 | tf_op jit(solution)/shard_map/ppermute | solution.py:235
  140.3 4.9 %collective-permute-start.24 = (bf16[1024,512]{1,0:T(8,128)(2,1)S(1)}, bf16[1024,512]{1,0:T(8,128)(2,1)S(1)}, u32[]{:S(2)}, u32[]{:S(2)}) collective-permute-start(bf16[1024,512]{1,0:T(8,128)(2,1)S(1)} %get-tuple-element.204.refs_1_), channel_id=1, source_target_pairs={{0,1},{1,0},{2,3},{3,2},{4,5},{5,4},{6,7},{7,6},{8,9},{9,8},{10,11... | collective-permute-start | bytes 3145736 | tf_op jit(solution)/shard_map/ppermute | solution.py:235
  141.6 15.6 %collective-permute-start.25 = (bf16[2048,128]{1,0:T(8,128)(2,1)S(1)}, bf16[2048,128]{1,0:T(8,128)(2,1)S(1)}, u32[]{:S(2)}, u32[]{:S(2)}) collective-permute-start(bf16[2048,128]{1,0:T(8,128)(2,1)S(1)} %decoder_feed_grads.1), channel_id=1, source_target_pairs={{0,8},{24,16},{1,9},{25,17},{2,10},{26,18},{3,11},{27,19},{4,12},{... | collective-permute-start | bytes 1572872 | tf_op jit(solution)/shard_map/ppermute | solution.py:1033
  157.4 10.3 %collective-permute-start.26 = (bf16[2048,128]{1,0:T(8,128)(2,1)S(1)}, bf16[2048,128]{1,0:T(8,128)(2,1)S(1)}, u32[]{:S(2)}, u32[]{:S(2)}) collective-permute-start(bf16[2048,128]{1,0:T(8,128)(2,1)S(1)} %add_convert_fusion.7), channel_id=1, source_target_pairs={{8,16},{16,8},{9,17},{17,9},{10,18},{18,10},{11,19},{19,11},{12,20... | collective-permute-start | bytes 1572872 | tf_op jit(solution)/shard_map/ppermute | solution.py:1049
  167.9 40.1 %copy-start.50 = (bf16[2048,128]{1,0:T(8,128)(2,1)}, bf16[2048,128]{1,0:T(8,128)(2,1)S(1)}, u32[]{:S(2)}) copy-start(bf16[2048,128]{1,0:T(8,128)(2,1)S(1)} %add_convert_fusion.6) | copy-start | bytes 1572868
  169.1 2.7 collective-permute-start.27
  176.7 21.0 %collective-permute-start.28 = (bf16[768,384]{1,0:T(8,128)(2,1)S(1)}, bf16[768,384]{1,0:T(8,128)(2,1)S(1)}, u32[]{:S(2)}, u32[]{:S(2)}) collective-permute-start(bf16[768,384]{1,0:T(8,128)(2,1)S(1)} %encoder_down_grads.1), channel_id=1, source_target_pairs={{0,8},{24,16},{1,9},{25,17},{2,10},{26,18},{3,11},{27,19},{4,12},{... | collective-permute-start | bytes 1769480 | tf_op jit(solution)/shard_map/ppermute | solution.py:1033
  193.9 15.3 %collective-permute-start.29 = (bf16[1024,768]{1,0:T(8,128)(2,1)S(1)}, bf16[1024,768]{1,0:T(8,128)(2,1)S(1)}, u32[]{:S(2)}, u32[]{:S(2)}) collective-permute-start(bf16[1024,768]{1,0:T(8,128)(2,1)S(1)} %get-tuple-element.236.refs_1_), channel_id=1, source_target_pairs={{0,1},{1,0},{2,3},{3,2},{4,5},{5,4},{6,7},{7,6},{8,9},{9,8},{10,11... | collective-permute-start | bytes 4718600 | tf_op jit(solution)/shard_map/ppermute | solution.py:235
  197.9 11.4 %copy-start.23 = (bf16[384,768]{1,0:T(8,128)(2,1)S(1)}, bf16[384,768]{1,0:T(8,128)(2,1)}, u32[]{:S(2)}) copy-start(bf16[384,768]{1,0:T(8,128)(2,1)} %copy-done.22) | copy-start | bytes 1769476
  197.9 11.4 %copy-start.47 = (f32[4,768]{1,0:T(4,128)S(1)}, f32[4,768]{1,0:T(4,128)}, u32[]{:S(2)}) copy-start(f32[4,768]{1,0:T(4,128)} %copy-done.46) | copy-start | bytes 36868
  198.7 21.3 %collective-permute-start.32 = (bf16[384,768]{1,0:T(8,128)(2,1)S(1)}, bf16[384,768]{1,0:T(8,128)(2,1)S(1)}, u32[]{:S(2)}, u32[]{:S(2)}) collective-permute-start(bf16[384,768]{1,0:T(8,128)(2,1)S(1)} %encoder_up_grads.1), channel_id=1, source_target_pairs={{0,8},{24,16},{1,9},{25,17},{2,10},{26,18},{3,11},{27,19},{4,12},{... | collective-permute-start | bytes 1769480 | tf_op jit(solution)/shard_map/ppermute | solution.py:1033
  203.2 19.7 %collective-permute-start.30 = (bf16[768,384]{1,0:T(8,128)(2,1)S(1)}, bf16[768,384]{1,0:T(8,128)(2,1)S(1)}, u32[]{:S(2)}, u32[]{:S(2)}) collective-permute-start(bf16[768,384]{1,0:T(8,128)(2,1)S(1)} %add_convert_fusion.5), channel_id=1, source_target_pairs={{8,16},{16,8},{9,17},{17,9},{10,18},{18,10},{11,19},{19,11},{12,20... | collective-permute-start | bytes 1769480 | tf_op jit(solution)/shard_map/ppermute | solution.py:1049
  203.9 19.0 %collective-permute-start.31 = (bf16[1408,128]{1,0:T(8,128)(2,1)S(1)}, bf16[1408,128]{1,0:T(8,128)(2,1)S(1)}, u32[]{:S(2)}, u32[]{:S(2)}) collective-permute-start(bf16[1408,128]{1,0:T(8,128)(2,1)S(1)} %decoder_mixing_grads.1), channel_id=1, source_target_pairs={{0,8},{24,16},{1,9},{25,17},{2,10},{26,18},{3,11},{27,19},{4,12},{... | collective-permute-start | bytes 1081352 | tf_op jit(solution)/shard_map/ppermute | solution.py:1033
  207.9 20.5 %collective-permute-start.33 = (bf16[2048,128]{1,0:T(8,128)(2,1)S(1)}, bf16[2048,128]{1,0:T(8,128)(2,1)S(1)}, u32[]{:S(2)}, u32[]{:S(2)}) collective-permute-start(bf16[2048,128]{1,0:T(8,128)(2,1)S(1)} %add_convert_fusion.6), channel_id=1, source_target_pairs={{8,0},{16,24},{9,1},{17,25},{10,2},{18,26},{11,3},{19,27},{12,4},{... | collective-permute-start | bytes 1572872 | tf_op jit(solution)/shard_map/ppermute | solution.py:1049
  214.8 13.6 %copy-start.4 = (f32[1024,384]{1,0:T(8,128)}, f32[1024,384]{1,0:T(8,128)S(1)}, u32[]{:S(2)}) copy-start(f32[1024,384]{1,0:T(8,128)S(1)} %get-tuple-element.255.grad_ref) | copy-start | bytes 4718596
  220.0 14.1 %copy-start.28 = (bf16[1024,128]{1,0:T(8,128)(2,1)}, bf16[1024,128]{1,0:T(8,128)(2,1)S(1)}, u32[]{:S(2)}) copy-start(bf16[1024,128]{1,0:T(8,128)(2,1)S(1)} %get-tuple-element.240.refs_2_) | copy-start | bytes 786436
  220.1 14.1 %copy-start.30 = (bf16[1024,128]{1,0:T(8,128)(2,1)}, bf16[1024,128]{1,0:T(8,128)(2,1)S(1)}, u32[]{:S(2)}) copy-start(bf16[1024,128]{1,0:T(8,128)(2,1)S(1)} %get-tuple-element.241.refs_3_) | copy-start | bytes 786436
  223.8 21.1 %collective-permute-start.36 = (bf16[384,768]{1,0:T(8,128)(2,1)}, bf16[384,768]{1,0:T(8,128)(2,1)}, u32[]{:S(2)}, u32[]{:S(2)}) collective-permute-start(bf16[384,768]{1,0:T(8,128)(2,1)} %add_convert_fusion.3), channel_id=1, source_target_pairs={{8,16},{16,8},{9,17},{17,9},{10,18},{18,10},{11,19},{19,11},{12,20... | collective-permute-start | bytes 1769480 | tf_op jit(solution)/shard_map/ppermute | solution.py:1049
  226.3 20.1 %collective-permute-start.35 = (bf16[768,384]{1,0:T(8,128)(2,1)}, bf16[768,384]{1,0:T(8,128)(2,1)}, u32[]{:S(2)}, u32[]{:S(2)}) collective-permute-start(bf16[768,384]{1,0:T(8,128)(2,1)} %add_convert_fusion.4), channel_id=1, source_target_pairs={{8,0},{16,24},{9,1},{17,25},{10,2},{18,26},{11,3},{19,27},{12,4},{... | collective-permute-start | bytes 1769480 | tf_op jit(solution)/shard_map/ppermute | solution.py:1049
  236.1 18.4 %collective-permute-start.34 = (bf16[2304,128]{1,0:T(8,128)(2,1)}, bf16[2304,128]{1,0:T(8,128)(2,1)}, u32[]{:S(2)}, u32[]{:S(2)}) collective-permute-start(bf16[2304,128]{1,0:T(8,128)(2,1)} %encoder_mixing_grads.1), channel_id=1, source_target_pairs={{0,8},{24,16},{1,9},{25,17},{2,10},{26,18},{3,11},{27,19},{4,12},{... | collective-permute-start | bytes 1769480 | tf_op jit(solution)/shard_map/ppermute | solution.py:1033
  244.2 15.9 %collective-permute-start.38 = (bf16[1408,128]{1,0:T(8,128)(2,1)}, bf16[1408,128]{1,0:T(8,128)(2,1)S(1)}, u32[]{:S(2)}, u32[]{:S(2)}) collective-permute-start(bf16[1408,128]{1,0:T(8,128)(2,1)} %add_convert_fusion.9), channel_id=1, source_target_pairs={{8,16},{16,8},{9,17},{17,9},{10,18},{18,10},{11,19},{19,11},{12,20... | collective-permute-start | bytes 1081352 | tf_op jit(solution)/shard_map/ppermute | solution.py:1049
  255.9 17.2 %collective-permute-start.37 = (bf16[2304,128]{1,0:T(8,128)(2,1)S(1)}, bf16[2304,128]{1,0:T(8,128)(2,1)S(1)}, u32[]{:S(2)}, u32[]{:S(2)}) collective-permute-start(bf16[2304,128]{1,0:T(8,128)(2,1)S(1)} %add_convert_fusion.1), channel_id=1, source_target_pairs={{8,16},{16,8},{9,17},{17,9},{10,18},{18,10},{11,19},{19,11},{12,20... | collective-permute-start | bytes 1769480 | tf_op jit(solution)/shard_map/ppermute | solution.py:1049
  256.6 23.7 %collective-permute-start.47 = (bf16[384,768]{1,0:T(8,128)(2,1)S(1)}, bf16[384,768]{1,0:T(8,128)(2,1)S(1)}, u32[]{:S(2)}, u32[]{:S(2)}) collective-permute-start(bf16[384,768]{1,0:T(8,128)(2,1)S(1)} %add_convert_fusion.2), channel_id=1, source_target_pairs={{8,0},{16,24},{9,1},{17,25},{10,2},{18,26},{11,3},{19,27},{12,4},{... | collective-permute-start | bytes 1769480 | tf_op jit(solution)/shard_map/ppermute | solution.py:1049
  259.9 1.8 collective-permute-start.39
  260.1 21.8 %collective-permute-start.45 = (bf16[1408,128]{1,0:T(8,128)(2,1)S(1)}, bf16[1408,128]{1,0:T(8,128)(2,1)S(1)}, u32[]{:S(2)}, u32[]{:S(2)}) collective-permute-start(bf16[1408,128]{1,0:T(8,128)(2,1)S(1)} %add_convert_fusion.8), channel_id=1, source_target_pairs={{8,0},{16,24},{9,1},{17,25},{10,2},{18,26},{11,3},{19,27},{12,4},{... | collective-permute-start | bytes 1081352 | tf_op jit(solution)/shard_map/ppermute | solution.py:1049
  261.7 11.3 %copy-start.51 = (bf16[2048,128]{1,0:T(8,128)(2,1)S(1)}, bf16[2048,128]{1,0:T(8,128)(2,1)}, u32[]{:S(2)}) copy-start(bf16[2048,128]{1,0:T(8,128)(2,1)} %copy-done.50) | copy-start | bytes 1572868
  261.7 11.3 %copy-start.54 = (bf16[2048,128]{1,0:T(8,128)(2,1)S(1)}, bf16[2048,128]{1,0:T(8,128)(2,1)}, u32[]{:S(2)}) copy-start(bf16[2048,128]{1,0:T(8,128)(2,1)} %copy-done.53) | copy-start | bytes 1572868
  273.3 26.0 %collective-permute-start.44 = (bf16[2304,128]{1,0:T(8,128)(2,1)S(1)}, bf16[2304,128]{1,0:T(8,128)(2,1)S(1)}, u32[]{:S(2)}, u32[]{:S(2)}) collective-permute-start(bf16[2304,128]{1,0:T(8,128)(2,1)S(1)} %add_convert_fusion), channel_id=1, source_target_pairs={{8,0},{16,24},{9,1},{17,25},{10,2},{18,26},{11,3},{19,27},{12,4},{... | collective-permute-start | bytes 1769480 | tf_op jit(solution)/shard_map/ppermute | solution.py:1049
  274.6 19.7 %collective-permute-start.41 = (f32[8,768]{1,0:T(8,128)S(1)}, f32[8,768]{1,0:T(8,128)S(1)}, u32[]{:S(2)}, u32[]{:S(2)}) collective-permute-start(f32[8,768]{1,0:T(8,128)S(1)} %bitcast_reduce_fusion), channel_id=1, source_target_pairs={{0,24},{8,0},{16,8},{24,16},{1,25},{9,1},{17,9},{25,17},{2,26},{10... | collective-permute-start | bytes 73736 | tf_op jit(solution)/shard_map/ppermute | solution.py:1071
  276.0 18.4 %collective-permute-start.42 = (f32[8,768]{1,0:T(8,128)S(1)}, f32[8,768]{1,0:T(8,128)S(1)}, u32[]{:S(2)}, u32[]{:S(2)}) collective-permute-start(f32[8,768]{1,0:T(8,128)S(1)} %bitcast_reduce_fusion), channel_id=1, source_target_pairs={{0,16},{8,24},{16,0},{24,8},{1,17},{9,25},{17,1},{25,9},{2,18},{10... | collective-permute-start | bytes 73736 | tf_op jit(solution)/shard_map/ppermute | solution.py:1071
  280.3 14.1 %collective-permute-start.43 = (f32[8,768]{1,0:T(8,128)S(1)}, f32[8,768]{1,0:T(8,128)S(1)}, u32[]{:S(2)}, u32[]{:S(2)}) collective-permute-start(f32[8,768]{1,0:T(8,128)S(1)} %bitcast_reduce_fusion), channel_id=1, source_target_pairs={{0,8},{8,16},{16,24},{24,0},{1,9},{9,17},{17,25},{25,1},{2,10},{10... | collective-permute-start | bytes 73736 | tf_op jit(solution)/shard_map/ppermute | solution.py:1071
  282.5 14.9 %collective-permute-start.46 = (bf16[1536,128]{1,0:T(8,128)(2,1)S(1)}, bf16[1536,128]{1,0:T(8,128)(2,1)S(1)}, u32[]{:S(2)}, u32[]{:S(2)}) collective-permute-start(bf16[1536,128]{1,0:T(8,128)(2,1)S(1)} %decoder_send.1), channel_id=1, source_target_pairs={{0,1},{1,0},{2,3},{3,2},{4,5},{5,4},{6,7},{7,6},{8,9},{9,8},{10,11... | collective-permute-start | bytes 1179656 | tf_op jit(solution)/shard_map/ppermute | solution.py:235
  294.3 1.4 collective-permute-start.40
  (43 other events, 165.6 us)

commit v2 on v1

--- a/solution.py
+++ b/solution.py
@@ -391,15 +391,16 @@
 
 def pack_mixing_kernel(w_ref, out_ref, v1, v2, v3, v4, pack_ref):
     store_three(pack_ref, A_VEC, (v1, v2, v3, v4))
-    rows = w_ref.shape[1]
-    pack_ref[:rows, :] = w_ref[0, :, :LANES]
-    pack_ref[rows : 2 * rows, :] = w_ref[1, :, :LANES]
-    pack_ref[A_LAST:A_VEC, :HALF] = w_ref[0, :, LANES:]
-    pack_ref[A_LAST:A_VEC, HALF:] = w_ref[1, :, LANES:]
-    pack_ref[A_END : A_END + rows, :] = w_ref[2, :, :LANES]
+    rows = w_ref.shape[2]
+    parts = [w_ref[kind].astype(F32).T.astype(BF16) for kind in range(3)]
+    pack_ref[:rows, :] = parts[0][:, :LANES]
+    pack_ref[rows : 2 * rows, :] = parts[1][:, :LANES]
+    pack_ref[A_LAST:A_VEC, :HALF] = parts[0][:, LANES:]
+    pack_ref[A_LAST:A_VEC, HALF:] = parts[1][:, LANES:]
+    pack_ref[A_END : A_END + rows, :] = parts[2][:, :LANES]
     rest = A_END + B_REST
-    pack_ref[rest : rest + rows // 2, :HALF] = w_ref[2, : rows // 2, LANES:]
-    pack_ref[rest : rest + rows // 2, HALF:] = w_ref[2, rows // 2 :, LANES:]
+    pack_ref[rest : rest + rows // 2, :HALF] = parts[2][: rows // 2, LANES:]
+    pack_ref[rest : rest + rows // 2, HALF:] = parts[2][rows // 2 :, LANES:]
     heads = out_ref.shape[0]
     base = A_END + B_OUT
     for tile in range(3):
@@ -575,22 +576,26 @@
 
     for block in range(length // BLOCK):
 
-        @pl.loop(0, BLOCK // TILE)
+        @pl.loop(0, BLOCK // FEED)
         def _(step):
-            at = pl.ds(block * BLOCK + step * TILE, TILE)
+            at = pl.ds(block * BLOCK + step * FEED, FEED)
             limits = limit_ref[at, :]
-            places = block * BLOCK + lax.broadcasted_iota(jnp.int32, (TILE, BLOCK), 1)
+            places = block * BLOCK + lax.broadcasted_iota(jnp.int32, (FEED, BLOCK), 1)
             visible = places <= limits
 
-            @pl.loop(0, groups)
-            def _(group):
-                queries = mixed_ref[at, pl.ds(group * LANES, LANES)]
-                result = jnp.zeros((TILE, LANES), F32)
-                inverses = jnp.zeros((TILE, LANES), F32)
-                for head in range(heads):
-                    own = head_lanes(head, head_size, TILE)
+            @pl.loop(0, groups * heads // 2)
+            def _(step):
+                group, pair = step // (heads // 2), step % (heads // 2)
+                lanes = pl.ds(pl.multiple_of(group * LANES, LANES), LANES)
+                queries = mixed_ref[at, lanes]
+                result = attended_ref[at, lanes]
+                inverses = inverse_ref[at, lanes]
+                lane = lax.broadcasted_iota(jnp.int32, (FEED, LANES), 1)
+                for number in range(2):
+                    start = (2 * pair + number) * head_size
+                    own = (lane >= start) & (lane < start + head_size)
                     masked = jnp.where(own, queries, jnp.zeros_like(queries))
-                    total = jnp.zeros((TILE, 2 * LANES), F32)
+                    total = jnp.zeros((FEED, 2 * LANES), F32)
                     for part in range(block + 1):
                         span = slice(part * BLOCK, (part + 1) * BLOCK)
                         keys = mixed_ref[span, pl.ds((groups + group) * LANES, LANES)]
@@ -599,10 +604,9 @@
                             weights = jnp.where(visible, weights, 0.0)
                         total = total + mm(weights.astype(BF16), aug_ref[group, span, :])
                     inverse = 1.0 / total[:, LANES:]
-                    result = jnp.where(own, total[:, :LANES] * inverse, result)
+                    result = jnp.where(own, (total[:, :LANES] * inverse).astype(BF16), result)
                     inverses = jnp.where(own, inverse, inverses)
-                lanes = pl.ds(group * LANES, LANES)
-                attended_ref[at, lanes] = result.astype(BF16)
+                attended_ref[at, lanes] = result
                 inverse_ref[at, lanes] = inverses
 
             partial_ref[at, :] = mm(attended_ref[at, :], weight_ref[...]).astype(BF16)
@@ -775,15 +779,17 @@
     gain, bias = vec_ref[0:1, :], vec_ref[1:2, :]
     width = low_ref.shape[1]
 
-    @pl.loop(0, middle_ref.shape[0] // TILE)
+    @pl.loop(0, middle_ref.shape[0] // FEED)
     def _(tile):
-        at = pl.ds(tile * TILE, TILE)
+        at = pl.ds(tile * FEED, FEED)
         total = middle_ref[at, :] + (mine_ref[at, :].astype(F32) + got_ref[at, :].astype(F32))
         low = total.astype(BF16)
 
-        @pl.when(tile == block)
-        def _():
-            out_ref[...] = total[:, :width]
+        for part in range(FEED // TILE):
+
+            @pl.when(tile * (FEED // TILE) + part == block)
+            def _():
+                out_ref[...] = total[part * TILE : (part + 1) * TILE, :width]
 
         low_ref[at, :] = low[:, :width]
         stream = mm(low, weight_ref[...])
@@ -974,13 +980,12 @@
 def encoder_unpack_kernel(pack_ref, mixing_ref, out_ref):
     rows, half = E_ROWS, E_ROWS // 2
     for kind in range(3):
-        mixing_ref[kind, :, :LANES] = pack_ref[kind * rows : (kind + 1) * rows, :].astype(F32)
-    last = pack_ref[G_LAST:G_REST, :].astype(F32)
-    mixing_ref[0, :, LANES:] = last[:, :HALF]
-    mixing_ref[1, :, LANES:] = last[:, HALF:]
-    rest = pack_ref[G_REST:G_OUT, :].astype(F32)
-    mixing_ref[2, :half, LANES:] = rest[:, :HALF]
-    mixing_ref[2, half:, LANES:] = rest[:, HALF:]
+        mixing_ref[kind, :LANES, :] = pack_ref[kind * rows : (kind + 1) * rows, :].astype(F32).T
+    last = pack_ref[G_LAST:G_REST, :].astype(F32).T
+    mixing_ref[0, LANES:, :] = last[:HALF]
+    mixing_ref[1, LANES:, :] = last[HALF:]
+    rest = pack_ref[G_REST:G_OUT, :].astype(F32).T
+    mixing_ref[2, LANES:, :] = jnp.concatenate([rest[:HALF], rest[HALF:]], 1)
     for tile in range(3):
         at = slice(G_OUT + tile * half, G_OUT + (tile + 1) * half)
         out_ref[:, tile * LANES : (tile + 1) * LANES] = pack_ref[at, :].astype(F32)
@@ -1143,7 +1148,7 @@
         "pack_mixing",
         shaped(A_END + B_END, LANES, BF16),
         (
-            jnp.transpose(encoder_query_key_value, (1, 0, 2)),
+            jnp.transpose(encoder_query_key_value, (1, 2, 0)),
             encoder_output_weight,
             row_of(encoder_attention_gain),
             row_of(encoder_attention_bias),
@@ -1359,44 +1364,44 @@
         limit=12,
         cost=3.9,
     )
-    grads_c = call(
-        product_kernel,
-        "encoder_down_grads",
-        shaped(units // 2, width, BF16),
-        (active, down_low),
-        limit=8,
-        cost=1,
-    )
-    sum_c = line_first(grads_c, data_size)
     grads_b = call(
         mixing_grads_kernel,
         "decoder_mixing_grads",
         shaped(GB_END, LANES, BF16),
         (
             place, d_normed_first, *d_lows[:3], d_attended, d_middle_low, encoder_low,
-            after(proj_low, grads_c),
+            proj_low,
         ),
         scalars=1,
         limit=8,
         cost=1.3,
     )
     sum_b = line_first(grads_b, data_size)
+    grads_c = call(
+        product_kernel,
+        "encoder_down_grads",
+        shaped(units // 2, width, BF16),
+        (after(active, grads_b), down_low),
+        limit=8,
+        cost=1,
+    )
+    sum_c = line_first(grads_c, data_size)
     hidden_low, partial = call(
         feed_back_kernel,
         "feed_back",
         (shaped(length, units, BF16), shaped(length, full, BF16)),
-        (after(down_low, grads_b), slope, *e_parts),
+        (after(down_low, grads_c), slope, *e_parts),
         (pltpu.VMEM((FEED, full), F32),),
         limit=16,
         cost=12,
     )
     got = swap(partial, "core")
-    sum_c = line_across(sum_c, data_size, partial)
+    sum_b = line_across(sum_b, data_size, partial)
     grads_e = call(
         product_kernel,
         "encoder_up_grads",
         shaped(width, units // 2, BF16),
-        (normed_second, after(hidden_low, sum_c[0])),
+        (normed_second, after(hidden_low, sum_b[0])),
         limit=8,
         cost=1000,
     )
@@ -1415,17 +1420,17 @@
         limit=12,
         cost=5.5,
     )
+    sum_c = line_across(sum_c, data_size, middle_low)
     first = attention_backward(
-        mixed, attended, inverse, attended_grad, limits_row, HD1, 0, 1
-    )
-    sum_c = line_back(sum_c, data_size, first)
-    sum_b = line_across(sum_b, data_size, first)
+        mixed, attended, inverse, after(attended_grad, sum_c[0]), limits_row, HD1, 0, 1
+    )
+    sum_b = line_back(sum_b, data_size, first)
     sum_e = line_across(sum_e, data_size, first)
     second = attention_backward(
         mixed,
         attended,
         inverse,
-        after(attended_grad, sum_c[0], sum_b[0], sum_e[0], sum_a),
+        after(attended_grad, sum_b[0], sum_e[0], sum_a),
         limits_row,
         HD1,
         1,
@@ -1440,9 +1445,10 @@
         cost=1.1,
     )
     sum_d = line_first(grads_d, data_size)
+    sum_c = line_back(sum_c, data_size, grads_d)
     sum_e = line_back(sum_e, data_size, grads_d)
     third = attention_backward(
-        mixed, attended, inverse, after(attended_grad, grads_d, sum_c, sum_e[0]), limits_row, HD1, 2, 1
+        mixed, attended, inverse, after(attended_grad, grads_d, sum_b, sum_c[0], sum_e[0]), limits_row, HD1, 2, 1
     )
     sum_d = line_across(sum_d, data_size, third)
     lows = (*first, *second, after(third[0], sum_d[0]), *third[1:])
@@ -1456,12 +1462,11 @@
         cost=1.8,
     )
     got = swap(send, "core")
-    sum_b = line_back(sum_b, data_size, send)
     own_input_grad, first_sums = call(
         input_back_kernel,
         "input_back",
         (shaped(own_rows, width, F32), shaped(2, full, F32)),
-        (place, after(keep, sum_b[0]), got, stream, middle_grad, e_vec),
+        (place, after(keep, sum_c), got, stream, middle_grad, e_vec),
         scalars=1,
         limit=8,
         cost=1.8,
@@ -1476,10 +1481,6 @@
     sums = jnp.concatenate([e_sums, jnp.pad(d_sums, ((0, 0), (0, full - low_full)))], 0)
     sums = jnp.sum(lax.all_gather(sums, ("row", "y", "core")), 0)
     sum_d = line_back(sum_d, data_size, sums)
-    sums = dp_sum(after(sums, sum_d[0]), data_size)
-    e_sums = lax.dynamic_slice_in_dim(sums[:4], row * width, width, 1)
-    share = decoder_attention_gain.shape[0]
-    d_sums = lax.dynamic_slice_in_dim(sums[4:], block * share, share, 1)
 
     own, by_row = after(f_parts[:2], sum_d[0])
     out_rows, out_columns = output_cotangent.shape
@@ -1525,12 +1526,16 @@
     )
     grads_c = line_last(sum_c, data_size, sum_d[0]).astype(F32)
     grads_e = line_last(sum_e, data_size, sum_d[0]).astype(F32)
+    sums = dp_sum(after(sums, sum_d[0], d_down_grad, own_decoder_out), data_size)
+    e_sums = lax.dynamic_slice_in_dim(sums[:4], row * width, width, 1)
+    share = decoder_attention_gain.shape[0]
+    d_sums = lax.dynamic_slice_in_dim(sums[4:], block * share, share, 1)
     grads_d = line_last(sum_d, data_size, d_down_grad, grads_c, grads_e)
     mixing_grad, out_grad = call(
         encoder_unpack_kernel,
         "encoder_unpack",
         (
-            jax.ShapeDtypeStruct((3, width, width // 2), F32),
+            jax.ShapeDtypeStruct((3, width // 2, width), F32),
             shaped(width // 2, width, F32),
         ),
         (grads_d,),
@@ -1542,7 +1547,7 @@
         own_input_grad,
         e_sums[0],
         e_sums[1],
-        jnp.transpose(mixing_grad, (1, 0, 2)),
+        jnp.transpose(mixing_grad, (2, 0, 1)),
         out_grad,
         e_sums[2],
         e_sums[3],

time: 306 us -> 296 us (0.967)
  starting transfers between devices: 71.6 us -> 61.6 us
  waiting for transfers between devices: 57.4 us -> 66.9 us
  local copies, waits for them, and re-layouts: 17.4 us -> 14 us
  other arithmetic: 12.2 us -> 8.81 us
    ppermute x10, waiting for transfers between devices: 0.03 us -> 11.1 us  [line_next(): return (total, lax.ppermute(total, 'dp', pairs))]
    ppermute x5, starting transfers between devices: 28.2 us -> 23.6 us  [line_first(): return (value, lax.ppermute(value, 'dp', [(0, 1), (3, 2)]))]
    ppermute x3, starting transfers between devices: 7.3 us -> 3.15 us  [dp_sum(): lax.ppermute(value, 'dp', [(i, (i + step) % size) for i in range(size)])]
    ppermute x29, waiting for transfers between devices: 36.8 us -> 40.5 us  [swap(): return lax.ppermute(value, axis, SWAP)]
    unnamed x127 -> x113, local copies, waits for them, and re-layouts: 11.8 us -> 8.41 us
    convert_element_type x10, other arithmetic: 6.24 us -> 3.03 us  [line_next(): total = (mine.astype(F32) + got.astype(F32)).astype(BF16)]
  transfers between devices with their start and end apart: 48 -> 48, of which waited for: 14 -> 16; matrix products, arithmetic and copies ran while one was open for 7% -> 5% of each run, Pallas kernels for 38% -> 39%
where the time goes in v2:
time: 296 us; the launch traced here: 291 us
  Pallas kernels  128 us (43%)
  waiting for transfers between devices  66.9 us (23%)
  starting transfers between devices  61.6 us (21%)
  local copies, waits for them, and re-layouts  14 us (5%)
  blocking collectives  9.19 us (3%)
  other arithmetic  8.81 us (3%)
    pallas_call x31, Pallas kernels, call(): pl.pallas_call(body, out_shape=outs, in_specs=[SMEM] * scalars + [place]...  93.3 us
    ppermute x29, waiting for transfers between devices, swap(): return lax.ppermute(value, axis, SWAP)  40.5 us
    pallas_call x5, Pallas kernels, attention_backward(): pl.pallas_call(functools.partial(attention_backward_kernel, head_size, pa...  34.7 us
    ppermute x5, starting transfers between devices, line_first(): return (value, lax.ppermute(value, 'dp', [(0, 1), (3, 2)]))  23.6 us
    ppermute x29, starting transfers between devices, swap(): return lax.ppermute(value, axis, SWAP)  23 us
    ppermute x10, waiting for transfers between devices, line_next(): return (total, lax.ppermute(total, 'dp', pairs))  11.1 us
    ppermute x10, starting transfers between devices, line_next(): return (total, lax.ppermute(total, 'dp', pairs))  10.4 us
    all_gather x1, blocking collectives, per_device(): sums = jnp.sum(lax.all_gather(sums, ('row', 'y', 'core')), 0)  9.19 us
  transfers between devices with their start and end apart: 48, of which 16 were waited for; matrix products, arithmetic and copies ran while one was open for 5% of the time, Pallas kernels for 39%

profile of v2, /device:TPU:0, one launch (start us, length us, event | category | flops | bytes accessed | tf_op | source)
XLA Modules:
  0.0 291.2 jit_solution(16549041795991760774)
XLA Ops:
  0.7 3.0 %collective-permute-start = (bf16[256,384]{1,0:T(8,128)(2,1)}, bf16[256,384]{1,0:T(8,128)(2,1)S(1)}, u32[]{:S(2)}, u32[]{:S(2)}) collective-permute-start(bf16[256,384]{1,0:T(8,128)(2,1)} %refs_1_.4), channel_id=1, source_target_pairs={{0,4},{4,0},{1,5},{5,1},{2,6},{6,2},{3,7},{7,3},{8,12},{12,8},{9,1... | collective-permute-start | bytes 589832 | tf_op jit(solution)/shard_map/ppermute | solution.py:235
  3.7 1.5 collective-permute-start.1
  5.8 3.2 %pack_decoder.1 = (bf16[2448,128]{1,0:T(8,128)(2,1)}, bf16[2448,128]{1,0:T(8,128)(2,1)}) custom-call(s32[4]{0:T(128)} %pad_add_fusion.refs_0_, bf16[3,128,256]{2,1,0:T(8,128)(2,1)} %bitcast.47, bf16[256,128]{1,0:T(8,128)(2,1)} %refs_2_.1, bf16[128,1024]{1,0:T(8,128)(2,1)} %refs_3_.1, bf16[1024,128]{1,0:T(8,128)(2,1)} %refs_4_.1, f32[1,128]{1,0:T(1,128)} %bitcast.52, ...), custom_call_target="tpu_custom_call" | custom-call | flops 10000000 | bytes 1 | tf_op jit(solution)/shard_map/pack_decoder/pallas_call | solution.py:315
  10.2 2.3 pack_mixing.1.refs_3_.refs_1_
  13.0 1.7 collective-permute-start.3
  14.7 2.5 pack_encoder.1.refs_4_.refs_2_
  17.3 1.5 join_decoder.1
  19.2 1.6 collective-permute-start.6
  20.8 8.0 %collective-permute-done.2.refs_4_.refs_2_ = bf16[2352,128]{1,0:T(8,128)(2,1)S(1)} collective-permute-done((bf16[2352,128]{1,0:T(8,128)(2,1)}, bf16[2352,128]{1,0:T(8,128)(2,1)S(1)}, u32[]{:S(2)}, u32[]{:S(2)}) %collective-permute-start.2) | collective-permute-done | bytes 602144 | tf_op jit(solution)/shard_map/ppermute | solution.py:235
  31.2 1.3 collective-permute-start.9
  32.7 2.9 join_input.1.refs_1_
  36.4 1.3 collective-permute-start.14
  38.2 1.3 collective-permute-start.11
  39.5 1.4 collective-permute-start.12
  42.2 1.8 first_norm.1
  44.0 4.9 %encoder_mixing.1 = (bf16[1024,1152]{1,0:T(8,128)(2,1)S(1)}, bf16[768,1152]{1,0:T(8,128)(2,1)S(1)}, bf16[384,768]{1,0:T(8,128)(2,1)S(1)}) custom-call(bf16[1024,768]{1,0:T(8,128)(2,1)S(1)} %get-tuple-element.170.refs_0_, bf16[2352,128]{1,0:T(8,128)(2,1)S(1)} %copy-done.11, bf16[2352,128]{1,0:T(8,128)(2,1)S(1)} %collective-permute-done.2.refs_4_.refs_2_, ...), custom_call_target="tpu_custom_call" | custom-call | flops 30000000 | bytes 1 | tf_op jit(solution)/shard_map/encoder_mixing/pallas_call | solution.py:315
  50.2 9.0 %encoder_attend.1 = (bf16[1024,384]{1,0:T(8,128)(2,1)S(1)}, f32[1024,384]{1,0:T(8,128)S(1)}, bf16[1024,768]{1,0:T(8,128)(2,1)S(1)}) custom-call(bf16[1024,1152]{1,0:T(8,128)(2,1)S(1)} %get-tuple-element.171.refs_0_.q_ref.k_ref.v_ref, s32[1024,1]{1,0:T(8,128)S(1)} %copy.42.refs_1_, bf16[384,768]{1,0:T(8,128)(2,1)S(1)} %get-tuple-element.172.refs_2_.refs_6_), custom_call_target="tpu_custom_call" | custom-call | flops 120000000 | bytes 1 | tf_op jit(solution)/shard_map/encoder_attend/pallas_call | solution.py:315
  59.2 14.8 %collective-permute-done.11.refs_5_.refs_3_ = bf16[4608,128]{1,0:T(8,128)(2,1)S(1)} collective-permute-done((bf16[4608,128]{1,0:T(8,128)(2,1)S(1)}, bf16[4608,128]{1,0:T(8,128)(2,1)S(1)}, u32[]{:S(2)}, u32[]{:S(2)}) %collective-permute-start.11) | collective-permute-done | bytes 1179680 | tf_op jit(solution)/shard_map/ppermute | solution.py:235
  74.6 1.3 collective-permute-start.15
  75.9 1.3 collective-permute-start.16
  80.1 10.8 %collective-permute-done.15.refs_7_.refs_5_ = bf16[2304,128]{1,0:T(8,128)(2,1)S(1)} collective-permute-done((bf16[2304,128]{1,0:T(8,128)(2,1)S(1)}, bf16[2304,128]{1,0:T(8,128)(2,1)S(1)}, u32[]{:S(2)}, u32[]{:S(2)}) %collective-permute-start.15) | collective-permute-done | bytes 589856 | tf_op jit(solution)/shard_map/ppermute | solution.py:235
  90.9 1.3 collective-permute-done.16.refs_8_.refs_6_
  92.2 1.3 collective-permute-start.21
  94.3 9.2 %feed_forward.1 = (f32[1024,768]{1,0:T(8,128)S(1)}, bf16[1024,768]{1,0:T(8,128)(2,1)S(1)}, bf16[1024,1536]{1,0:T(8,128)(2,1)S(1)}, bf16[1024,1536]{1,0:T(8,128)(2,1)S(1)}, bf16[1024,768]{1,0:T(8,128)(2,1)S(1)}) custom-call(bf16[1024,768]{1,0:T(8,128)(2,1)S(1)} %get-tuple-element.169.refs_0_.refs_3_, bf16[1024,768]{1,0:T(8,128)(2,1)S(1)} %get-tuple-element.173.refs_1_, ...), custom_call_target="tpu_custom_call" | custom-call | flops 120000000 | bytes 1 | tf_op jit(solution)/shard_map/feed_forward/pallas_call | solution.py:315
  104.7 1.4 collective-permute-start.23
  107.0 5.5 %bridge.1 = (f32[256,384]{1,0:T(8,128)}, bf16[1024,384]{1,0:T(8,128)(2,1)S(1)}, f32[1024,512]{1,0:T(8,128)S(1)}, bf16[1024,512]{1,0:T(8,128)(2,1)S(1)}, bf16[102...) custom-call(s32[4]{0:T(128)S(1)} %copy-done.34, ...), custom_call_target="tpu_custom_call" | custom-call | flops 57000000 | bytes 1 | tf_op jit(solution)/shard_map/bridge/pallas_call | solution.py:315
  112.6 11.1 %decoder_attend.1 = (bf16[1024,256]{1,0:T(8,128)(2,1)S(1)}, f32[1024,256]{1,0:T(8,128)S(1)}, bf16[1024,512]{1,0:T(8,128)(2,1)S(1)}) custom-call(bf16[1024,768]{1,0:T(8,128)(2,1)S(1)} %get-tuple-element.188.refs_0_.q_ref.k_ref.v_ref, s32[1024,1]{1,0:T(8,128)S(1)} %copy.42.refs_1_, bf16[256,512]{1,0:T(8,128)(2,1)S(1)} %get-tuple-element.189.refs_2_.refs_6_), custom_call_target="tpu_custom_call" | custom-call | flops 110000000 | bytes 1 | tf_op jit(solution)/shard_map/decoder_attend/pallas_call | solution.py:315
  123.9 5.8 %collective-permute-done.23.refs_8_ = bf16[3072,128]{1,0:T(8,128)(2,1)S(1)} collective-permute-done((bf16[3072,128]{1,0:T(8,128)(2,1)}, bf16[3072,128]{1,0:T(8,128)(2,1)S(1)}, u32[]{:S(2)}, u32[]{:S(2)}) %collective-permute-start.23) | collective-permute-done | bytes 786464 | tf_op jit(solution)/shard_map/ppermute | solution.py:255
  129.7 8.0 %decoder_feed.1 = (f32[1024,512]{1,0:T(8,128)S(1)}, bf16[1024,512]{1,0:T(8,128)(2,1)S(1)}, bf16[1024,1024]{1,0:T(8,128)(2,1)S(1)}, bf16[1024,1024]{1,0:T(8,128)(...) custom-call(s32[4]{0:T(128)S(1)} %copy-done.34, ...), custom_call_target="tpu_custom_call" | custom-call | flops 80000000 | bytes 1 | tf_op jit(solution)/shard_map/decoder_feed/pallas_call | solution.py:315
  139.0 3.5 %collective-permute-start.25 = (bf16[2048,128]{1,0:T(8,128)(2,1)S(1)}, bf16[2048,128]{1,0:T(8,128)(2,1)S(1)}, u32[]{:S(2)}, u32[]{:S(2)}) collective-permute-start(bf16[2048,128]{1,0:T(8,128)(2,1)S(1)} %decoder_feed_grads.1), channel_id=1, source_target_pairs={{0,8},{24,16},{1,9},{25,17},{2,10},{26,18},{3,11},{27,19},{4,12},{... | collective-permute-start | bytes 1572872 | tf_op jit(solution)/shard_map/ppermute | solution.py:1038
  142.5 2.7 decoder_middle_back.1
  145.2 9.4 %attention_backward.5 = (bf16[1024,128]{1,0:T(8,128)(2,1)S(1)}, bf16[1024,128]{1,0:T(8,128)(2,1)S(1)}, bf16[1024,128]{1,0:T(8,128)(2,1)S(1)}) custom-call(bf16[1024,768]{1,0:T(8,128)(2,1)S(1)} %get-tuple-element.188.refs_0_.q_ref.k_ref.v_ref, bf16[1024,768]{1,0:T(8,128)(2,1)S(1)} %get-tuple-element.188.refs_0_.q_ref.k_ref.v_ref, ...), custom_call_target="tpu_custom_call" | custom-call | flops 96000000 | bytes 1 | tf_op jit(solution)/shard_map/attention_backward/pallas_call | solution.py:202
  155.5 9.6 %attention_backward.6 = (bf16[1024,128]{1,0:T(8,128)(2,1)S(1)}, bf16[1024,128]{1,0:T(8,128)(2,1)S(1)}, bf16[1024,128]{1,0:T(8,128)(2,1)S(1)}) custom-call(bf16[1024,768]{1,0:T(8,128)(2,1)S(1)} %get-tuple-element.188.refs_0_.q_ref.k_ref.v_ref, bf16[1024,768]{1,0:T(8,128)(2,1)S(1)} %get-tuple-element.188.refs_0_.q_ref.k_ref.v_ref, ...), custom_call_target="tpu_custom_call" | custom-call | flops 96000000 | bytes 1 | tf_op jit(solution)/shard_map/attention_backward/pallas_call | solution.py:202
  166.6 2.6 collective-permute-done.27.refs_2_
  169.3 3.9 %bridge_back.1 = (bf16[1024,512]{1,0:T(8,128)(2,1)S(1)}, f32[1024,768]{1,0:T(8,128)S(1)}, bf16[1024,768]{1,0:T(8,128)(2,1)S(1)}, f32[2,512]{1,0:T(2,128)S(1)}) custom-call(s32[4]{0:T(128)S(1)} %copy-done.34, bf16[1024,512]{1,0:T(8,128)(2,1)S(1)} %decoder_mixed_back.1.refs_1_, bf16[1024,512]{1,0:T(8,128)(2,1)S(1)} %collective-permute-done.27.refs_2_, ...), custom_call_target="tpu_custom_call" | custom-call | flops 39000000 | bytes 1 | tf_op jit(solution)/shard_map/bridge_back/pallas_call | solution.py:315
  173.1 1.3 decoder_mixing_grads.1
  174.5 8.2 %collective-permute-start.28 = (bf16[1408,128]{1,0:T(8,128)(2,1)S(1)}, bf16[1408,128]{1,0:T(8,128)(2,1)S(1)}, u32[]{:S(2)}, u32[]{:S(2)}) collective-permute-start(bf16[1408,128]{1,0:T(8,128)(2,1)S(1)} %decoder_mixing_grads.1), channel_id=1, source_target_pairs={{0,8},{24,16},{1,9},{25,17},{2,10},{26,18},{3,11},{27,19},{4,12},{... | collective-permute-start | bytes 1081352 | tf_op jit(solution)/shard_map/ppermute | solution.py:1038
  183.8 1.8 collective-permute-start.30
  185.7 7.3 %feed_back.1 = (bf16[1024,1536]{1,0:T(8,128)(2,1)S(1)}, bf16[1024,768]{1,0:T(8,128)(2,1)S(1)}) custom-call(bf16[1024,768]{1,0:T(8,128)(2,1)S(1)} %get-tuple-element.229.refs_1_.refs_0_, bf16[1024,1536]{1,0:T(8,128)(2,1)S(1)} %get-tuple-element.230.refs_1_, bf16[4608,128]{1,0:T(8,128)(2,1)S(1)} %copy-done.2, bf16[4608,128]{1,0:T(8,128)(2,1)S(1)} %copy-done.4, ...), custom_call_target="tpu_custom_call" | custom-call | flops 120000000 | bytes 1 | tf_op jit(solution)/shard_map/feed_back/pallas_call | solution.py:315
  194.0 2.8 collective-permute-start.32
  196.8 1.3 collective-permute-start.33
  198.9 4.1 %encoder_middle_back.1 = (f32[1024,768]{1,0:T(8,128)S(1)}, bf16[1024,384]{1,0:T(8,128)(2,1)S(1)}, f32[1024,384]{1,0:T(8,128)S(1)}, f32[2,768]{1,0:T(2,128)S(1)}) custom-call(s32[4]{0:T(128)S(1)} %copy-done.34, bf16[1024,768]{1,0:T(8,128)(2,1)S(1)} %get-tuple-element.237.refs_1_, bf16[1024,768]{1,0:T(8,128)(2,1)S(1)} %collective-permute-done.29.refs_2_, ...), custom_call_target="tpu_custom_call" | custom-call | flops 55000000 | bytes 1 | tf_op jit(solution)/shard_map/encoder_middle_back/pallas_call | solution.py:315
  203.0 1.6 copy-done.12
  205.5 5.2 %attention_backward.7 = (bf16[1024,128]{1,0:T(8,128)(2,1)S(1)}, bf16[1024,128]{1,0:T(8,128)(2,1)S(1)}, bf16[1024,128]{1,0:T(8,128)(2,1)S(1)}) custom-call(bf16[1024,1152]{1,0:T(8,128)(2,1)S(1)} %copy-done.1, bf16[1024,1152]{1,0:T(8,128)(2,1)S(1)} %copy-done.1, bf16[1024,1152]{1,0:T(8,128)(2,1)S(1)} %copy-done.1, ...), custom_call_target="tpu_custom_call" | custom-call | flops 52000000 | bytes 1 | tf_op jit(solution)/shard_map/attention_backward/pallas_call | solution.py:202
  210.7 5.2 %collective-permute-done.32 = bf16[384,768]{1,0:T(8,128)(2,1)S(1)} collective-permute-done((bf16[384,768]{1,0:T(8,128)(2,1)S(1)}, bf16[384,768]{1,0:T(8,128)(2,1)S(1)}, u32[]{:S(2)}, u32[]{:S(2)}) %collective-permute-start.32) | collective-permute-done | bytes 589856 | tf_op jit(solution)/shard_map/ppermute | solution.py:1038
  217.1 5.2 %attention_backward.8 = (bf16[1024,128]{1,0:T(8,128)(2,1)S(1)}, bf16[1024,128]{1,0:T(8,128)(2,1)S(1)}, bf16[1024,128]{1,0:T(8,128)(2,1)S(1)}) custom-call(bf16[1024,1152]{1,0:T(8,128)(2,1)S(1)} %copy-done.1, bf16[1024,1152]{1,0:T(8,128)(2,1)S(1)} %copy-done.1, bf16[1024,1152]{1,0:T(8,128)(2,1)S(1)} %copy-done.1, ...), custom_call_target="tpu_custom_call" | custom-call | flops 52000000 | bytes 1 | tf_op jit(solution)/shard_map/attention_backward/pallas_call | solution.py:202
  223.5 7.2 %collective-permute-start.34 = (bf16[2304,128]{1,0:T(8,128)(2,1)S(1)}, bf16[2304,128]{1,0:T(8,128)(2,1)S(1)}, u32[]{:S(2)}, u32[]{:S(2)}) collective-permute-start(bf16[2304,128]{1,0:T(8,128)(2,1)S(1)} %encoder_mixing_grads.1), channel_id=1, source_target_pairs={{0,8},{24,16},{1,9},{25,17},{2,10},{26,18},{3,11},{27,19},{4,12},{... | collective-permute-start | bytes 1769480 | tf_op jit(solution)/shard_map/ppermute | solution.py:1038
  230.7 1.3 collective-permute-start.35
  232.2 1.5 collective-permute-start.39
  234.7 9.3 %collective-permute-done.35 = bf16[1408,128]{1,0:T(8,128)(2,1)S(1)} collective-permute-done((bf16[1408,128]{1,0:T(8,128)(2,1)S(1)}, bf16[1408,128]{1,0:T(8,128)(2,1)S(1)}, u32[]{:S(2)}, u32[]{:S(2)}) %collective-permute-start.35) | collective-permute-done | bytes 360480 | tf_op jit(solution)/shard_map/ppermute | solution.py:1054
  244.0 5.2 %attention_backward.9 = (bf16[1024,128]{1,0:T(8,128)(2,1)S(1)}, bf16[1024,128]{1,0:T(8,128)(2,1)S(1)}, bf16[1024,128]{1,0:T(8,128)(2,1)S(1)}) custom-call(bf16[1024,1152]{1,0:T(8,128)(2,1)S(1)} %copy-done.1, bf16[1024,1152]{1,0:T(8,128)(2,1)S(1)} %copy-done.1, bf16[1024,1152]{1,0:T(8,128)(2,1)S(1)} %copy-done.1, ...), custom_call_target="tpu_custom_call" | custom-call | flops 52000000 | bytes 1 | tf_op jit(solution)/shard_map/attention_backward/pallas_call | solution.py:202
  250.9 1.7 encoder_mixed_back.1
  253.5 1.3 collective-permute-start.47
  254.8 1.9 copy-done.13
  256.7 1.9 input_back.1
  258.6 9.2 %all-gather = f32[64,768]{1,0:T(8,128)S(1)} all-gather(f32[8,768]{1,0:T(8,128)S(1)} %select_maximum_fusion), channel_id=2, replica_groups=mesh['dp'=4,'row'=2,'y'=2,'core'=2] {'row','y','core'}, dimensions={0}, use_global_device_ids=true | all-gather | bytes 221184 | tf_op jit(solution)/shard_map/all_gather | solution.py:1482
  268.0 1.4 collective-permute-start.46
  269.4 1.8 collective-permute-done.47
  275.4 1.7 convert_add_fusion
  277.1 1.9 decoder_unpack.1
  278.9 1.3 collective-permute-start.43
  280.3 2.2 select_convert_fusion.1
  282.7 1.5 collective-permute-start.45
  284.2 2.5 collective-permute-done.43
  (224 shorter events, 37.1 us)
Async XLA Ops:
  0.7 8.4 %collective-permute-start = (bf16[256,384]{1,0:T(8,128)(2,1)}, bf16[256,384]{1,0:T(8,128)(2,1)S(1)}, u32[]{:S(2)}, u32[]{:S(2)}) collective-permute-start(bf16[256,384]{1,0:T(8,128)(2,1)} %refs_1_.4), channel_id=1, source_target_pairs={{0,4},{4,0},{1,5},{5,1},{2,6},{6,2},{3,7},{7,3},{8,12},{12,8},{9,1... | collective-permute-start | bytes 589832 | tf_op jit(solution)/shard_map/ppermute | solution.py:235
  3.7 6.6 %collective-permute-start.1 = (bf16[256,384]{1,0:T(8,128)(2,1)}, bf16[256,384]{1,0:T(8,128)(2,1)S(1)}, u32[]{:S(2)}, u32[]{:S(2)}) collective-permute-start(bf16[256,384]{1,0:T(8,128)(2,1)} %refs_1_.4), channel_id=1, source_target_pairs={{0,2},{2,0},{1,3},{3,1},{4,6},{6,4},{5,7},{7,5},{8,10},{10,8},{9,1... | collective-permute-start | bytes 589832 | tf_op jit(solution)/shard_map/ppermute | solution.py:235
  9.0 8.3 %collective-permute-start.4 = (bf16[2448,128]{1,0:T(8,128)(2,1)}, bf16[2448,128]{1,0:T(8,128)(2,1)S(1)}, u32[]{:S(2)}, u32[]{:S(2)}) collective-permute-start(bf16[2448,128]{1,0:T(8,128)(2,1)} %get-tuple-element.162), channel_id=1, source_target_pairs={{0,1},{1,0},{2,3},{3,2},{4,5},{5,4},{6,7},{7,6},{8,9},{9,8},{10,11... | collective-permute-start | bytes 1880072 | tf_op jit(solution)/shard_map/ppermute | solution.py:235
  9.1 8.1 %copy-start.47 = (bf16[256,384]{1,0:T(8,128)(2,1)}, bf16[256,384]{1,0:T(8,128)(2,1)S(1)}, u32[]{:S(2)}) copy-start(bf16[256,384]{1,0:T(8,128)(2,1)S(1)} %collective-permute-done.refs_2_) | copy-start | bytes 589828
  12.6 16.2 %collective-permute-start.2 = (bf16[2352,128]{1,0:T(8,128)(2,1)}, bf16[2352,128]{1,0:T(8,128)(2,1)S(1)}, u32[]{:S(2)}, u32[]{:S(2)}) collective-permute-start(bf16[2352,128]{1,0:T(8,128)(2,1)} %pack_mixing.1.refs_3_.refs_1_), channel_id=1, source_target_pairs={{0,4},{4,0},{1,5},{5,1},{2,6},{6,2},{3,7},{7,3},{8,12},{12,8},{9,1... | collective-permute-start | bytes 1806344 | tf_op jit(solution)/shard_map/ppermute | solution.py:235
  13.0 16.5 %collective-permute-start.3 = (bf16[2352,128]{1,0:T(8,128)(2,1)}, bf16[2352,128]{1,0:T(8,128)(2,1)S(1)}, u32[]{:S(2)}, u32[]{:S(2)}) collective-permute-start(bf16[2352,128]{1,0:T(8,128)(2,1)} %pack_mixing.1.refs_3_.refs_1_), channel_id=1, source_target_pairs={{0,2},{2,0},{1,3},{3,1},{4,6},{6,4},{5,7},{7,5},{8,10},{10,8},{9,1... | collective-permute-start | bytes 1806344 | tf_op jit(solution)/shard_map/ppermute | solution.py:235
  17.2 15.3 %copy-start.31 = (s32[1024]{0:T(1024)S(1)}, s32[1024]{0:T(1024)}, u32[]{:S(2)}) copy-start(s32[1024]{0:T(1024)} %param.21) | copy-start | bytes 12292
  18.8 19.4 %copy-start.2 = (bf16[4608,128]{1,0:T(8,128)(2,1)S(1)}, bf16[4608,128]{1,0:T(8,128)(2,1)}, u32[]{:S(2)}) copy-start(bf16[4608,128]{1,0:T(8,128)(2,1)} %pack_encoder.1.refs_4_.refs_2_) | copy-start | bytes 3538948
  18.8 11.5 %collective-permute-start.5 = (bf16[128,384]{1,0:T(8,128)(2,1)S(1)}, bf16[128,384]{1,0:T(8,128)(2,1)S(1)}, u32[]{:S(2)}, u32[]{:S(2)}) collective-permute-start(bf16[128,384]{1,0:T(8,128)(2,1)S(1)} %slice.104), channel_id=1, source_target_pairs={{0,2},{2,0},{1,3},{3,1},{4,6},{6,4},{5,7},{7,5},{8,10},{10,8},{9,1... | collective-permute-start | bytes 294920 | tf_op jit(solution)/shard_map/ppermute | solution.py:235
  19.2 11.2 %collective-permute-start.6 = (bf16[128,384]{1,0:T(8,128)(2,1)S(1)}, bf16[128,384]{1,0:T(8,128)(2,1)S(1)}, u32[]{:S(2)}, u32[]{:S(2)}) collective-permute-start(bf16[128,384]{1,0:T(8,128)(2,1)S(1)} %slice.105), channel_id=1, source_target_pairs={{0,4},{4,0},{1,5},{5,1},{2,6},{6,2},{3,7},{7,3},{8,12},{12,8},{9,1... | collective-permute-start | bytes 294920 | tf_op jit(solution)/shard_map/ppermute | solution.py:235
  30.3 9.2 %collective-permute-start.8 = (bf16[1200,128]{1,0:T(8,128)(2,1)}, bf16[1200,128]{1,0:T(8,128)(2,1)}, u32[]{:S(2)}, u32[]{:S(2)}) collective-permute-start(bf16[1200,128]{1,0:T(8,128)(2,1)} %slice.106), channel_id=1, source_target_pairs={{0,2},{2,0},{1,3},{3,1},{4,6},{6,4},{5,7},{7,5},{8,10},{10,8},{9,1... | collective-permute-start | bytes 921608 | tf_op jit(solution)/shard_map/ppermute | solution.py:235
  31.2 7.0 %collective-permute-start.9 = (bf16[1152,128]{1,0:T(8,128)(2,1)}, bf16[1152,128]{1,0:T(8,128)(2,1)}, u32[]{:S(2)}, u32[]{:S(2)}) collective-permute-start(bf16[1152,128]{1,0:T(8,128)(2,1)} %slice.107), channel_id=1, source_target_pairs={{0,4},{4,0},{1,5},{5,1},{2,6},{6,2},{3,7},{7,3},{8,12},{12,8},{9,1... | collective-permute-start | bytes 884744 | tf_op jit(solution)/shard_map/ppermute | solution.py:235
  35.6 5.4 %collective-permute-start.7 = (bf16[512,768]{1,0:T(8,128)(2,1)}, bf16[512,768]{1,0:T(8,128)(2,1)S(1)}, u32[]{:S(2)}, u32[]{:S(2)}) collective-permute-start(bf16[512,768]{1,0:T(8,128)(2,1)} %join_input.1.refs_1_), channel_id=1, source_target_pairs={{0,1},{1,0},{2,3},{3,2},{4,5},{5,4},{6,7},{7,6},{8,9},{9,8},{10,11... | collective-permute-start | bytes 2359304 | tf_op jit(solution)/shard_map/ppermute | solution.py:235
  35.7 38.9 %collective-permute-start.13 = (bf16[1824,128]{1,0:T(8,128)(2,1)S(1)}, bf16[1824,128]{1,0:T(8,128)(2,1)S(1)}, u32[]{:S(2)}, u32[]{:S(2)}) collective-permute-start(bf16[1824,128]{1,0:T(8,128)(2,1)S(1)} %get-tuple-element.177.refs_4_), channel_id=1, source_target_pairs={{0,4},{4,0},{1,5},{5,1},{2,6},{6,2},{3,7},{7,3},{8,12},{12,8},{9,1... | collective-permute-start | bytes 1400840 | tf_op jit(solution)/shard_map/ppermute | solution.py:235
  36.4 38.1 %collective-permute-start.14 = (bf16[1824,128]{1,0:T(8,128)(2,1)S(1)}, bf16[1824,128]{1,0:T(8,128)(2,1)S(1)}, u32[]{:S(2)}, u32[]{:S(2)}) collective-permute-start(bf16[1824,128]{1,0:T(8,128)(2,1)S(1)} %get-tuple-element.177.refs_4_), channel_id=1, source_target_pairs={{0,2},{2,0},{1,3},{3,1},{4,6},{6,4},{5,7},{7,5},{8,10},{10,8},{9,1... | collective-permute-start | bytes 1400840 | tf_op jit(solution)/shard_map/ppermute | solution.py:235
  38.2 35.9 %collective-permute-start.11 = (bf16[4608,128]{1,0:T(8,128)(2,1)S(1)}, bf16[4608,128]{1,0:T(8,128)(2,1)S(1)}, u32[]{:S(2)}, u32[]{:S(2)}) collective-permute-start(bf16[4608,128]{1,0:T(8,128)(2,1)S(1)} %copy-done.2), channel_id=1, source_target_pairs={{0,4},{4,0},{1,5},{5,1},{2,6},{6,2},{3,7},{7,3},{8,12},{12,8},{9,1... | collective-permute-start | bytes 3538952 | tf_op jit(solution)/shard_map/ppermute | solution.py:235
  39.5 35.0 %collective-permute-start.12 = (bf16[4608,128]{1,0:T(8,128)(2,1)S(1)}, bf16[4608,128]{1,0:T(8,128)(2,1)S(1)}, u32[]{:S(2)}, u32[]{:S(2)}) collective-permute-start(bf16[4608,128]{1,0:T(8,128)(2,1)S(1)} %copy-done.2), channel_id=1, source_target_pairs={{0,2},{2,0},{1,3},{3,1},{4,6},{6,4},{5,7},{7,5},{8,10},{10,8},{9,1... | collective-permute-start | bytes 3538952 | tf_op jit(solution)/shard_map/ppermute | solution.py:235
  44.0 50.2 %copy-start.7 = (bf16[1024,768]{1,0:T(8,128)(2,1)}, bf16[1024,768]{1,0:T(8,128)(2,1)S(1)}, u32[]{:S(2)}) copy-start(bf16[1024,768]{1,0:T(8,128)(2,1)S(1)} %get-tuple-element.169.refs_0_.refs_3_) | copy-start | bytes 4718596
  44.0 50.2 %copy-start.35 = (f32[4,768]{1,0:T(4,128)}, f32[4,768]{1,0:T(4,128)S(1)}, u32[]{:S(2)}) copy-start(f32[4,768]{1,0:T(4,128)S(1)} %get-tuple-element.174.refs_3_.refs_5_) | copy-start | bytes 36868
  50.2 9.0 %copy-start = (bf16[1024,1152]{1,0:T(8,128)(2,1)}, bf16[1024,1152]{1,0:T(8,128)(2,1)S(1)}, u32[]{:S(2)}) copy-start(bf16[1024,1152]{1,0:T(8,128)(2,1)S(1)} %get-tuple-element.171.refs_0_.q_ref.k_ref.v_ref) | copy-start | bytes 7077892
  50.2 9.0 %copy-start.20 = (bf16[384,768]{1,0:T(8,128)(2,1)}, bf16[384,768]{1,0:T(8,128)(2,1)S(1)}, u32[]{:S(2)}) copy-start(bf16[384,768]{1,0:T(8,128)(2,1)S(1)} %get-tuple-element.172.refs_2_.refs_6_) | copy-start | bytes 1769476
  74.0 20.2 %copy-start.3 = (bf16[4608,128]{1,0:T(8,128)(2,1)}, bf16[4608,128]{1,0:T(8,128)(2,1)S(1)}, u32[]{:S(2)}) copy-start(bf16[4608,128]{1,0:T(8,128)(2,1)S(1)} %collective-permute-done.11.refs_5_.refs_3_) | copy-start | bytes 3538948
  74.5 19.8 %copy-start.5 = (bf16[4608,128]{1,0:T(8,128)(2,1)}, bf16[4608,128]{1,0:T(8,128)(2,1)S(1)}, u32[]{:S(2)}) copy-start(bf16[4608,128]{1,0:T(8,128)(2,1)S(1)} %collective-permute-done.12.refs_6_.refs_4_) | copy-start | bytes 3538948
  74.5 19.7 %copy-start.28 = (bf16[1824,128]{1,0:T(8,128)(2,1)}, bf16[1824,128]{1,0:T(8,128)(2,1)S(1)}, u32[]{:S(2)}) copy-start(bf16[1824,128]{1,0:T(8,128)(2,1)S(1)} %collective-permute-done.13.refs_5_) | copy-start | bytes 1400836
  74.6 19.7 %copy-start.26 = (bf16[1824,128]{1,0:T(8,128)(2,1)}, bf16[1824,128]{1,0:T(8,128)(2,1)S(1)}, u32[]{:S(2)}) copy-start(bf16[1824,128]{1,0:T(8,128)(2,1)S(1)} %collective-permute-done.14.refs_6_) | copy-start | bytes 1400836
  74.6 16.3 %collective-permute-start.15 = (bf16[2304,128]{1,0:T(8,128)(2,1)S(1)}, bf16[2304,128]{1,0:T(8,128)(2,1)S(1)}, u32[]{:S(2)}, u32[]{:S(2)}) collective-permute-start(bf16[2304,128]{1,0:T(8,128)(2,1)S(1)} %slice.108), channel_id=1, source_target_pairs={{0,2},{2,0},{1,3},{3,1},{4,6},{6,4},{5,7},{7,5},{8,10},{10,8},{9,1... | collective-permute-start | bytes 1769480 | tf_op jit(solution)/shard_map/ppermute | solution.py:235
  75.9 16.3 %collective-permute-start.16 = (bf16[2304,128]{1,0:T(8,128)(2,1)S(1)}, bf16[2304,128]{1,0:T(8,128)(2,1)S(1)}, u32[]{:S(2)}, u32[]{:S(2)}) collective-permute-start(bf16[2304,128]{1,0:T(8,128)(2,1)S(1)} %slice.109), channel_id=1, source_target_pairs={{0,4},{4,0},{1,5},{5,1},{2,6},{6,2},{3,7},{7,3},{8,12},{12,8},{9,1... | collective-permute-start | bytes 1769480 | tf_op jit(solution)/shard_map/ppermute | solution.py:235
  78.7 27.5 %collective-permute-start.19 = (bf16[1024,128]{1,0:T(8,128)(2,1)}, bf16[1024,128]{1,0:T(8,128)(2,1)}, u32[]{:S(2)}, u32[]{:S(2)}) collective-permute-start(bf16[1024,128]{1,0:T(8,128)(2,1)} %slice.111), channel_id=1, source_target_pairs={{0,4},{4,0},{1,5},{5,1},{2,6},{6,2},{3,7},{7,3},{8,12},{12,8},{9,1... | collective-permute-start | bytes 786440 | tf_op jit(solution)/shard_map/ppermute | solution.py:235
  79.4 25.3 %collective-permute-start.18 = (bf16[800,128]{1,0:T(8,128)(2,1)}, bf16[800,128]{1,0:T(8,128)(2,1)}, u32[]{:S(2)}, u32[]{:S(2)}) collective-permute-start(bf16[800,128]{1,0:T(8,128)(2,1)} %slice.110), channel_id=1, source_target_pairs={{0,2},{2,0},{1,3},{3,1},{4,6},{6,4},{5,7},{7,5},{8,10},{10,8},{9,1... | collective-permute-start | bytes 614408 | tf_op jit(solution)/shard_map/ppermute | solution.py:235
  80.1 14.1 %collective-permute-start.10 = (bf16[1024,768]{1,0:T(8,128)(2,1)S(1)}, bf16[1024,768]{1,0:T(8,128)(2,1)S(1)}, u32[]{:S(2)}, u32[]{:S(2)}) collective-permute-start(bf16[1024,768]{1,0:T(8,128)(2,1)S(1)} %get-tuple-element.173.refs_1_), channel_id=1, source_target_pairs={{0,1},{1,0},{2,3},{3,2},{4,5},{5,4},{6,7},{7,6},{8,9},{9,8},{10,11... | collective-permute-start | bytes 4718600 | tf_op jit(solution)/shard_map/ppermute | solution.py:235
  92.2 31.7 %collective-permute-start.21 = (bf16[3072,128]{1,0:T(8,128)(2,1)}, bf16[3072,128]{1,0:T(8,128)(2,1)}, u32[]{:S(2)}, u32[]{:S(2)}) collective-permute-start(bf16[3072,128]{1,0:T(8,128)(2,1)} %get-tuple-element.277.refs_5_), channel_id=1, source_target_pairs={{0,4},{4,0},{1,5},{5,1},{2,6},{6,2},{3,7},{7,3},{8,12},{12,8},{9,1... | collective-permute-start | bytes 2359304 | tf_op jit(solution)/shard_map/ppermute | solution.py:235
  93.5 30.4 %collective-permute-start.22 = (bf16[3072,128]{1,0:T(8,128)(2,1)}, bf16[3072,128]{1,0:T(8,128)(2,1)}, u32[]{:S(2)}, u32[]{:S(2)}) collective-permute-start(bf16[3072,128]{1,0:T(8,128)(2,1)} %get-tuple-element.277.refs_5_), channel_id=1, source_target_pairs={{0,2},{2,0},{1,3},{3,1},{4,6},{6,4},{5,7},{7,5},{8,10},{10,8},{9,1... | collective-permute-start | bytes 2359304 | tf_op jit(solution)/shard_map/ppermute | solution.py:235
  103.6 3.5 %collective-permute-start.17 = (bf16[1024,768]{1,0:T(8,128)(2,1)S(1)}, bf16[1024,768]{1,0:T(8,128)(2,1)S(1)}, u32[]{:S(2)}, u32[]{:S(2)}) collective-permute-start(bf16[1024,768]{1,0:T(8,128)(2,1)S(1)} %get-tuple-element.182.refs_2_), channel_id=1, source_target_pairs={{0,1},{1,0},{2,3},{3,2},{4,5},{5,4},{6,7},{7,6},{8,9},{9,8},{10,11... | collective-permute-start | bytes 4718600 | tf_op jit(solution)/shard_map/ppermute | solution.py:235
  104.7 25.0 %collective-permute-start.23 = (bf16[3072,128]{1,0:T(8,128)(2,1)}, bf16[3072,128]{1,0:T(8,128)(2,1)S(1)}, u32[]{:S(2)}, u32[]{:S(2)}) collective-permute-start(bf16[3072,128]{1,0:T(8,128)(2,1)} %get-tuple-element.277.refs_5_), channel_id=1, source_target_pairs={{0,6},{2,4},{4,2},{6,0},{1,7},{3,5},{5,3},{7,1},{8,14},{10,12},{12... | collective-permute-start | bytes 2359304 | tf_op jit(solution)/shard_map/ppermute | solution.py:255
  123.7 6.0 %collective-permute-start.20 = (bf16[1024,512]{1,0:T(8,128)(2,1)S(1)}, bf16[1024,512]{1,0:T(8,128)(2,1)S(1)}, u32[]{:S(2)}, u32[]{:S(2)}) collective-permute-start(bf16[1024,512]{1,0:T(8,128)(2,1)S(1)} %get-tuple-element.190.refs_2_), channel_id=1, source_target_pairs={{0,1},{1,0},{2,3},{3,2},{4,5},{5,4},{6,7},{7,6},{8,9},{9,8},{10,11... | collective-permute-start | bytes 3145736 | tf_op jit(solution)/shard_map/ppermute | solution.py:235
  137.7 4.8 %collective-permute-start.24 = (bf16[1024,512]{1,0:T(8,128)(2,1)S(1)}, bf16[1024,512]{1,0:T(8,128)(2,1)S(1)}, u32[]{:S(2)}, u32[]{:S(2)}) collective-permute-start(bf16[1024,512]{1,0:T(8,128)(2,1)S(1)} %get-tuple-element.205.refs_1_), channel_id=1, source_target_pairs={{0,1},{1,0},{2,3},{3,2},{4,5},{5,4},{6,7},{7,6},{8,9},{9,8},{10,11... | collective-permute-start | bytes 3145736 | tf_op jit(solution)/shard_map/ppermute | solution.py:235
  139.0 15.6 %collective-permute-start.25 = (bf16[2048,128]{1,0:T(8,128)(2,1)S(1)}, bf16[2048,128]{1,0:T(8,128)(2,1)S(1)}, u32[]{:S(2)}, u32[]{:S(2)}) collective-permute-start(bf16[2048,128]{1,0:T(8,128)(2,1)S(1)} %decoder_feed_grads.1), channel_id=1, source_target_pairs={{0,8},{24,16},{1,9},{25,17},{2,10},{26,18},{3,11},{27,19},{4,12},{... | collective-permute-start | bytes 1572872 | tf_op jit(solution)/shard_map/ppermute | solution.py:1038
  154.8 10.3 %collective-permute-start.26 = (bf16[2048,128]{1,0:T(8,128)(2,1)S(1)}, bf16[2048,128]{1,0:T(8,128)(2,1)S(1)}, u32[]{:S(2)}, u32[]{:S(2)}) collective-permute-start(bf16[2048,128]{1,0:T(8,128)(2,1)S(1)} %add_convert_fusion.7), channel_id=1, source_target_pairs={{8,16},{16,8},{9,17},{17,9},{10,18},{18,10},{11,19},{19,11},{12,20... | collective-permute-start | bytes 1572872 | tf_op jit(solution)/shard_map/ppermute | solution.py:1054
  165.3 31.5 %copy-start.41 = (bf16[2048,128]{1,0:T(8,128)(2,1)}, bf16[2048,128]{1,0:T(8,128)(2,1)S(1)}, u32[]{:S(2)}) copy-start(bf16[2048,128]{1,0:T(8,128)(2,1)S(1)} %add_convert_fusion.6) | copy-start | bytes 1572868
  166.5 2.7 collective-permute-start.27
  174.5 18.6 %collective-permute-start.28 = (bf16[1408,128]{1,0:T(8,128)(2,1)S(1)}, bf16[1408,128]{1,0:T(8,128)(2,1)S(1)}, u32[]{:S(2)}, u32[]{:S(2)}) collective-permute-start(bf16[1408,128]{1,0:T(8,128)(2,1)S(1)} %decoder_mixing_grads.1), channel_id=1, source_target_pairs={{0,8},{24,16},{1,9},{25,17},{2,10},{26,18},{3,11},{27,19},{4,12},{... | collective-permute-start | bytes 1081352 | tf_op jit(solution)/shard_map/ppermute | solution.py:1038
  183.8 20.8 %collective-permute-start.30 = (bf16[768,384]{1,0:T(8,128)(2,1)S(1)}, bf16[768,384]{1,0:T(8,128)(2,1)S(1)}, u32[]{:S(2)}, u32[]{:S(2)}) collective-permute-start(bf16[768,384]{1,0:T(8,128)(2,1)S(1)} %encoder_down_grads.1), channel_id=1, source_target_pairs={{0,8},{24,16},{1,9},{25,17},{2,10},{26,18},{3,11},{27,19},{4,12},{... | collective-permute-start | bytes 1769480 | tf_op jit(solution)/shard_map/ppermute | solution.py:1038
  193.0 5.9 %collective-permute-start.29 = (bf16[1024,768]{1,0:T(8,128)(2,1)S(1)}, bf16[1024,768]{1,0:T(8,128)(2,1)S(1)}, u32[]{:S(2)}, u32[]{:S(2)}) collective-permute-start(bf16[1024,768]{1,0:T(8,128)(2,1)S(1)} %get-tuple-element.237.refs_1_), channel_id=1, source_target_pairs={{0,1},{1,0},{2,3},{3,2},{4,5},{5,4},{6,7},{7,6},{8,9},{9,8},{10,11... | collective-permute-start | bytes 4718600 | tf_op jit(solution)/shard_map/ppermute | solution.py:235
  194.0 21.9 %collective-permute-start.32 = (bf16[384,768]{1,0:T(8,128)(2,1)S(1)}, bf16[384,768]{1,0:T(8,128)(2,1)S(1)}, u32[]{:S(2)}, u32[]{:S(2)}) collective-permute-start(bf16[384,768]{1,0:T(8,128)(2,1)S(1)} %encoder_up_grads.1), channel_id=1, source_target_pairs={{0,8},{24,16},{1,9},{25,17},{2,10},{26,18},{3,11},{27,19},{4,12},{... | collective-permute-start | bytes 1769480 | tf_op jit(solution)/shard_map/ppermute | solution.py:1038
  196.8 20.3 %collective-permute-start.33 = (bf16[2048,128]{1,0:T(8,128)(2,1)S(1)}, bf16[2048,128]{1,0:T(8,128)(2,1)S(1)}, u32[]{:S(2)}, u32[]{:S(2)}) collective-permute-start(bf16[2048,128]{1,0:T(8,128)(2,1)S(1)} %add_convert_fusion.6), channel_id=1, source_target_pairs={{8,0},{16,24},{9,1},{17,25},{10,2},{18,26},{11,3},{19,27},{12,4},{... | collective-permute-start | bytes 1572872 | tf_op jit(solution)/shard_map/ppermute | solution.py:1054
  198.1 17.9 %collective-permute-start.31 = (bf16[1408,128]{1,0:T(8,128)(2,1)S(1)}, bf16[1408,128]{1,0:T(8,128)(2,1)S(1)}, u32[]{:S(2)}, u32[]{:S(2)}) collective-permute-start(bf16[1408,128]{1,0:T(8,128)(2,1)S(1)} %add_convert_fusion.9), channel_id=1, source_target_pairs={{8,16},{16,8},{9,17},{17,9},{10,18},{18,10},{11,19},{19,11},{12,20... | collective-permute-start | bytes 1081352 | tf_op jit(solution)/shard_map/ppermute | solution.py:1054
  204.7 27.3 %collective-permute-start.36 = (bf16[768,384]{1,0:T(8,128)(2,1)S(1)}, bf16[768,384]{1,0:T(8,128)(2,1)S(1)}, u32[]{:S(2)}, u32[]{:S(2)}) collective-permute-start(bf16[768,384]{1,0:T(8,128)(2,1)S(1)} %add_convert_fusion.5), channel_id=1, source_target_pairs={{8,16},{16,8},{9,17},{17,9},{10,18},{18,10},{11,19},{19,11},{12,20... | collective-permute-start | bytes 1769480 | tf_op jit(solution)/shard_map/ppermute | solution.py:1054
  216.1 16.1 %collective-permute-start.37 = (bf16[384,768]{1,0:T(8,128)(2,1)S(1)}, bf16[384,768]{1,0:T(8,128)(2,1)S(1)}, u32[]{:S(2)}, u32[]{:S(2)}) collective-permute-start(bf16[384,768]{1,0:T(8,128)(2,1)S(1)} %add_convert_fusion.4), channel_id=1, source_target_pairs={{8,16},{16,8},{9,17},{17,9},{10,18},{18,10},{11,19},{19,11},{12,20... | collective-permute-start | bytes 1769480 | tf_op jit(solution)/shard_map/ppermute | solution.py:1054
  217.1 13.6 %copy-start.43 = (bf16[1408,128]{1,0:T(8,128)(2,1)}, bf16[1408,128]{1,0:T(8,128)(2,1)S(1)}, u32[]{:S(2)}) copy-start(bf16[1408,128]{1,0:T(8,128)(2,1)S(1)} %add_convert_fusion.8) | copy-start | bytes 1081348
  223.5 25.7 %collective-permute-start.34 = (bf16[2304,128]{1,0:T(8,128)(2,1)S(1)}, bf16[2304,128]{1,0:T(8,128)(2,1)S(1)}, u32[]{:S(2)}, u32[]{:S(2)}) collective-permute-start(bf16[2304,128]{1,0:T(8,128)(2,1)S(1)} %encoder_mixing_grads.1), channel_id=1, source_target_pairs={{0,8},{24,16},{1,9},{25,17},{2,10},{26,18},{3,11},{27,19},{4,12},{... | collective-permute-start | bytes 1769480 | tf_op jit(solution)/shard_map/ppermute | solution.py:1038
  230.7 13.2 %collective-permute-start.35 = (bf16[1408,128]{1,0:T(8,128)(2,1)S(1)}, bf16[1408,128]{1,0:T(8,128)(2,1)S(1)}, u32[]{:S(2)}, u32[]{:S(2)}) collective-permute-start(bf16[1408,128]{1,0:T(8,128)(2,1)S(1)} %add_convert_fusion.8), channel_id=1, source_target_pairs={{8,0},{16,24},{9,1},{17,25},{10,2},{18,26},{11,3},{19,27},{12,4},{... | collective-permute-start | bytes 1081352 | tf_op jit(solution)/shard_map/ppermute | solution.py:1054
  232.2 22.6 %collective-permute-start.39 = (bf16[768,384]{1,0:T(8,128)(2,1)S(1)}, bf16[768,384]{1,0:T(8,128)(2,1)}, u32[]{:S(2)}, u32[]{:S(2)}) collective-permute-start(bf16[768,384]{1,0:T(8,128)(2,1)S(1)} %add_convert_fusion.3), channel_id=1, source_target_pairs={{8,0},{16,24},{9,1},{17,25},{10,2},{18,26},{11,3},{19,27},{12,4},{... | collective-permute-start | bytes 1769480 | tf_op jit(solution)/shard_map/ppermute | solution.py:1054
  252.6 2.2 collective-permute-start.40
  252.7 15.1 %collective-permute-start.38 = (bf16[2304,128]{1,0:T(8,128)(2,1)}, bf16[2304,128]{1,0:T(8,128)(2,1)S(1)}, u32[]{:S(2)}, u32[]{:S(2)}) collective-permute-start(bf16[2304,128]{1,0:T(8,128)(2,1)} %add_convert_fusion.1), channel_id=1, source_target_pairs={{8,16},{16,8},{9,17},{17,9},{10,18},{18,10},{11,19},{19,11},{12,20... | collective-permute-start | bytes 1769480 | tf_op jit(solution)/shard_map/ppermute | solution.py:1054
  253.5 17.8 %collective-permute-start.47 = (bf16[384,768]{1,0:T(8,128)(2,1)}, bf16[384,768]{1,0:T(8,128)(2,1)S(1)}, u32[]{:S(2)}, u32[]{:S(2)}) collective-permute-start(bf16[384,768]{1,0:T(8,128)(2,1)} %add_convert_fusion.2), channel_id=1, source_target_pairs={{8,0},{16,24},{9,1},{17,25},{10,2},{18,26},{11,3},{19,27},{12,4},{... | collective-permute-start | bytes 1769480 | tf_op jit(solution)/shard_map/ppermute | solution.py:1054
  256.7 11.1 %copy-start.40 = (bf16[2304,128]{1,0:T(8,128)(2,1)S(1)}, bf16[2304,128]{1,0:T(8,128)(2,1)}, u32[]{:S(2)}) copy-start(bf16[2304,128]{1,0:T(8,128)(2,1)} %add_convert_fusion.1) | copy-start | bytes 1769476
  258.6 12.7 %copy-start.44 = (bf16[1408,128]{1,0:T(8,128)(2,1)S(1)}, bf16[1408,128]{1,0:T(8,128)(2,1)}, u32[]{:S(2)}) copy-start(bf16[1408,128]{1,0:T(8,128)(2,1)} %copy-done.43) | copy-start | bytes 1081348
  258.6 12.7 %copy-start.50 = (bf16[1408,128]{1,0:T(8,128)(2,1)S(1)}, bf16[1408,128]{1,0:T(8,128)(2,1)}, u32[]{:S(2)}) copy-start(bf16[1408,128]{1,0:T(8,128)(2,1)} %copy-done.49) | copy-start | bytes 1081348
  268.0 21.7 %collective-permute-start.46 = (bf16[2304,128]{1,0:T(8,128)(2,1)S(1)}, bf16[2304,128]{1,0:T(8,128)(2,1)S(1)}, u32[]{:S(2)}, u32[]{:S(2)}) collective-permute-start(bf16[2304,128]{1,0:T(8,128)(2,1)S(1)} %add_convert_fusion), channel_id=1, source_target_pairs={{8,0},{16,24},{9,1},{17,25},{10,2},{18,26},{11,3},{19,27},{12,4},{... | collective-permute-start | bytes 1769480 | tf_op jit(solution)/shard_map/ppermute | solution.py:1054
  272.0 5.1 %collective-permute-start.42 = (bf16[1536,128]{1,0:T(8,128)(2,1)S(1)}, bf16[1536,128]{1,0:T(8,128)(2,1)S(1)}, u32[]{:S(2)}, u32[]{:S(2)}) collective-permute-start(bf16[1536,128]{1,0:T(8,128)(2,1)S(1)} %decoder_send.1), channel_id=1, source_target_pairs={{0,1},{1,0},{2,3},{3,2},{4,5},{5,4},{6,7},{7,6},{8,9},{9,8},{10,11... | collective-permute-start | bytes 1179656 | tf_op jit(solution)/shard_map/ppermute | solution.py:235
  273.7 1.7 collective-permute-start.41
  278.9 7.8 %collective-permute-start.43 = (f32[8,768]{1,0:T(8,128)S(1)}, f32[8,768]{1,0:T(8,128)S(1)}, u32[]{:S(2)}, u32[]{:S(2)}) collective-permute-start(f32[8,768]{1,0:T(8,128)S(1)} %bitcast_reduce_fusion), channel_id=1, source_target_pairs={{0,24},{8,0},{16,8},{24,16},{1,25},{9,1},{17,9},{25,17},{2,26},{10... | collective-permute-start | bytes 73736 | tf_op jit(solution)/shard_map/ppermute | solution.py:1076
  282.4 5.0 %collective-permute-start.44 = (f32[8,768]{1,0:T(8,128)S(1)}, f32[8,768]{1,0:T(8,128)S(1)}, u32[]{:S(2)}, u32[]{:S(2)}) collective-permute-start(f32[8,768]{1,0:T(8,128)S(1)} %bitcast_reduce_fusion), channel_id=1, source_target_pairs={{0,16},{8,24},{16,0},{24,8},{1,17},{9,25},{17,1},{25,9},{2,18},{10... | collective-permute-start | bytes 73736 | tf_op jit(solution)/shard_map/ppermute | solution.py:1076
  282.7 5.6 %collective-permute-start.45 = (f32[8,768]{1,0:T(8,128)S(1)}, f32[8,768]{1,0:T(8,128)S(1)}, u32[]{:S(2)}, u32[]{:S(2)}) collective-permute-start(f32[8,768]{1,0:T(8,128)S(1)} %bitcast_reduce_fusion), channel_id=1, source_target_pairs={{0,8},{8,16},{16,24},{24,0},{1,9},{9,17},{17,25},{25,1},{2,10},{10... | collective-permute-start | bytes 73736 | tf_op jit(solution)/shard_map/ppermute | solution.py:1076
  (37 other events, 125.7 us)

commit v3 on v2

--- a/solution.py
+++ b/solution.py
@@ -38,82 +38,14 @@
     return (lane >= head * head_size) & (lane < (head + 1) * head_size)
 
 
-def attention_forward_kernel(head_size, q_ref, k_ref, v_ref, limit_ref, out_ref, inv_ref, aug_ref):
-    tile = pl.program_id(1)
-    rows = q_ref.shape[0]
-    heads = LANES // head_size
-    per_block = BLOCK // rows
-    scale = head_size ** (-0.5) * LOG2E
-
-    @pl.when(tile == 0)
-    def _():
-        aug_ref[:, :LANES] = v_ref[...]
-        aug_ref[:, LANES:] = jnp.ones_like(v_ref)
-
-    def run(block):
-        queries = q_ref[...]
-        limits = limit_ref[...]
-        places = block * BLOCK + lax.broadcasted_iota(jnp.int32, (rows, BLOCK), 1)
-        visible = places <= limits
-        result = jnp.zeros((rows, LANES), F32)
-        inverses = jnp.zeros((rows, LANES), F32)
-        for head in range(heads):
-            own = head_lanes(head, head_size, rows)
-            masked = jnp.where(own, queries, jnp.zeros_like(queries))
-            total = jnp.zeros((rows, 2 * LANES), F32)
-            for part in range(block + 1):
-                span = slice(part * BLOCK, (part + 1) * BLOCK)
-                weights = jnp.exp2(mm_nt(masked, k_ref[span, :]) * scale)
-                if part == block:
-                    weights = jnp.where(visible, weights, 0.0)
-                total = total + mm(weights.astype(BF16), aug_ref[span, :])
-            inverse = 1.0 / total[:, LANES:]
-            result = jnp.where(own, total[:, :LANES] * inverse, result)
-            inverses = jnp.where(own, inverse, inverses)
-        out_ref[...] = result.astype(BF16)
-        inv_ref[...] = inverses
-
-    for block in range(k_ref.shape[0] // BLOCK):
-        pl.when(tile // per_block == block)(functools.partial(run, block))
-
-
-def attention_forward(mixed, limits, head_size):
-    length, width = mixed.shape[0], mixed.shape[1] // 3
-    groups = width // LANES
-    rows = 256
-    return pl.pallas_call(
-        functools.partial(attention_forward_kernel, head_size),
-        out_shape=(
-            jax.ShapeDtypeStruct((length, width), BF16),
-            jax.ShapeDtypeStruct((length, width), F32),
-        ),
-        grid=(groups, length // rows),
-        in_specs=[
-            pl.BlockSpec((rows, LANES), lambda g, t: (t, g)),
-            pl.BlockSpec((length, LANES), lambda g, t: (0, groups + g)),
-            pl.BlockSpec((length, LANES), lambda g, t: (0, 2 * groups + g)),
-            pl.BlockSpec((rows, 1), lambda g, t: (t, 0)),
-        ],
-        out_specs=[
-            pl.BlockSpec((rows, LANES), lambda g, t: (t, g)),
-            pl.BlockSpec((rows, LANES), lambda g, t: (t, g)),
-        ],
-        scratch_shapes=[pltpu.VMEM((length, 2 * LANES), BF16)],
-        compiler_params=pltpu.CompilerParams(vmem_limit_bytes=24 << 20),
-        cost_estimate=pl.CostEstimate(flops=int(10.5 * COST), bytes_accessed=1, transcendentals=0),
-        name="attention_forward",
-    )(mixed, mixed, mixed, limits)
-
-
 def attention_backward_kernel(
     head_size,
     pairs,
-    q_ref,
-    k_ref,
-    v_ref,
-    att_ref,
-    inv_ref,
-    grad_ref,
+    lanes,
+    mixed_ref,
+    att_all_ref,
+    inv_all_ref,
+    grad_all_ref,
     limit_ref,
     dq_ref,
     dk_ref,
@@ -124,31 +56,32 @@
     dk_acc,
     dv_acc,
 ):
-    step = pl.program_id(1)
+    q_ref, k_ref, v_ref = (mixed_ref.at[:, pl.ds(start, LANES)] for start in lanes)
+    att_ref, inv_ref, grad_ref = (
+        ref.at[:, pl.ds(lanes[0], LANES)] for ref in (att_all_ref, inv_all_ref, grad_all_ref)
+    )
     length = q_ref.shape[0]
     heads = LANES // head_size
     scaling = head_size ** (-0.5)
 
-    @pl.when(step == 0)
-    def _():
-        lane = lax.broadcasted_iota(jnp.int32, (length, LANES), 1)
-        vaug_ref[:, :LANES] = v_ref[...]
-        vaug_ref[:, LANES:] = jnp.where(lane < 2, 1.0, 0.0).astype(BF16)
-        scaled = grad_ref[...] * inv_ref[...]
-        terms = scaled * att_ref[...].astype(F32)
-        low = scaled.astype(BF16)
-        for head in range(heads):
-            own = head_lanes(head, head_size, length)
-            total = -jnp.sum(jnp.where(own, terms, 0.0), 1, keepdims=True)
-            high = total.astype(BF16).astype(F32)
-            rest = total - high
-            naug_ref[head, :, :LANES] = jnp.where(own, low, jnp.zeros_like(low))
-            naug_ref[head, :, LANES:] = jnp.where(
-                lane == 0, high, jnp.where(lane == 1, rest, 0.0)
-            ).astype(BF16)
-        dq_acc[...] = jnp.zeros_like(dq_acc)
-        dk_acc[...] = jnp.zeros_like(dk_acc)
-        dv_acc[...] = jnp.zeros_like(dv_acc)
+    lane = lax.broadcasted_iota(jnp.int32, (length, LANES), 1)
+    vaug_ref[:, :LANES] = v_ref[...]
+    vaug_ref[:, LANES:] = jnp.where(lane < 2, 1.0, 0.0).astype(BF16)
+    scaled = grad_ref[...] * inv_ref[...]
+    terms = scaled * att_ref[...].astype(F32)
+    low = scaled.astype(BF16)
+    for head in range(heads):
+        own = head_lanes(head, head_size, length)
+        total = -jnp.sum(jnp.where(own, terms, 0.0), 1, keepdims=True)
+        high = total.astype(BF16).astype(F32)
+        rest = total - high
+        naug_ref[head, :, :LANES] = jnp.where(own, low, jnp.zeros_like(low))
+        naug_ref[head, :, LANES:] = jnp.where(
+            lane == 0, high, jnp.where(lane == 1, rest, 0.0)
+        ).astype(BF16)
+    dq_acc[...] = jnp.zeros_like(dq_acc)
+    dk_acc[...] = jnp.zeros_like(dk_acc)
+    dv_acc[...] = jnp.zeros_like(dv_acc)
 
     def run(key_block, query_block):
         keys = slice(key_block * BLOCK, (key_block + 1) * BLOCK)
@@ -180,14 +113,11 @@
         dk_acc[keys, :] += dk
         dv_acc[keys, :] += dv
 
-    for number, (key_block, query_block) in enumerate(pairs):
-        pl.when(step == number)(functools.partial(run, key_block, query_block))
-
-    @pl.when(step == len(pairs) - 1)
-    def _():
-        dq_ref[...] = (dq_acc[...].T * scaling).astype(BF16)
-        dk_ref[...] = (dk_acc[...] * scaling).astype(BF16)
-        dv_ref[...] = dv_acc[...].astype(BF16)
+    for key_block, query_block in pairs:
+        run(key_block, query_block)
+    dq_ref[...] = (dq_acc[...].T * scaling).astype(BF16)
+    dk_ref[...] = (dk_acc[...] * scaling).astype(BF16)
+    dv_ref[...] = dv_acc[...].astype(BF16)
 
 
 def attention_backward(
@@ -198,21 +128,13 @@
     count = groups if count is None else count
     blocks = length // BLOCK
     pairs = [(k, q) for q in range(blocks) for k in range(q + 1)]
-    whole = lambda offset: pl.BlockSpec((length, LANES), lambda g, s: (0, offset + g))
+    lanes = tuple((kind * groups + start) * LANES for kind in range(3))
+    memory = pl.BlockSpec(memory_space=pltpu.VMEM)
     results = pl.pallas_call(
-        functools.partial(attention_backward_kernel, head_size, pairs),
-        out_shape=(jax.ShapeDtypeStruct((length, count * LANES), BF16),) * 3,
-        grid=(count, len(pairs)),
-        in_specs=[
-            whole(start),
-            whole(groups + start),
-            whole(2 * groups + start),
-            whole(start),
-            whole(start),
-            whole(start),
-            pl.BlockSpec((1, length), lambda g, s: (0, 0)),
-        ],
-        out_specs=[whole(0), whole(0), whole(0)],
+        functools.partial(attention_backward_kernel, head_size, pairs, lanes),
+        out_shape=(jax.ShapeDtypeStruct((length, LANES), BF16),) * 3,
+        in_specs=[memory] * 5,
+        out_specs=[memory] * 3,
         scratch_shapes=[
             pltpu.VMEM((length, 2 * LANES), BF16),
             pltpu.VMEM((LANES // head_size, length, 2 * LANES), BF16),
@@ -220,15 +142,13 @@
             pltpu.VMEM((length, LANES), F32),
             pltpu.VMEM((length, LANES), F32),
         ],
-        compiler_params=pltpu.CompilerParams(vmem_limit_bytes=32 << 20),
+        compiler_params=pltpu.CompilerParams(vmem_limit_bytes=16 << 20),
         cost_estimate=pl.CostEstimate(
             flops=int(count * (5.2 if head_size == HD1 else 9.6) * COST), bytes_accessed=1, transcendentals=0
         ),
         name="attention_backward",
-    )(mixed, mixed, mixed, attended, inverse, grad, limits_row)
-    if count == 1:
-        return tuple(results)
-    return tuple(r[:, g * LANES : (g + 1) * LANES] for g in range(count) for r in results)
+    )(mixed, attended, inverse, grad, limits_row)
+    return tuple(results)
 
 
 def swap(value, axis):
@@ -838,7 +758,13 @@
         incoming = mine_ref[at, :].astype(F32) + got_ref[at, :].astype(F32)
         centred, inverse = norm_rows(middle_ref[at, :])
         total = grad_ref[at, :].astype(F32) + norm_back(incoming, centred, inverse, gain)
-        total_ref[at, :] = total
+        if total_ref.shape[0] == TILE:
+
+            @pl.when(tile == place_ref[1])
+            def _():
+                total_ref[...] = total
+        else:
+            total_ref[at, :] = total
         low = total.astype(BF16)
         low_ref[at, :] = low[:, :width]
         attended_ref[at, :] = mm_nt(low, weight_ref[...])
@@ -916,7 +842,7 @@
     at = pl.ds(place_ref[1] * TILE, TILE)
     incoming = mine_ref[...].astype(F32) + got_ref[...].astype(F32)
     centred, inverse = norm_rows(x_ref[at, :].astype(F32))
-    total = grad_ref[at, :] + norm_back(incoming, centred, inverse, vec_ref[0:1, :])
+    total = grad_ref[...] + norm_back(incoming, centred, inverse, vec_ref[0:1, :])
     out_ref[...] = total[:, : out_ref.shape[1]]
     own_sums(place_ref, place_ref[1], sums_ref, incoming, centred)
 
@@ -1410,7 +1336,7 @@
         middle_back_kernel,
         "encoder_middle_back",
         (
-            shaped(length, full, F32),
+            shaped(own_rows, full, F32),
             shaped(length, width, BF16),
             shaped(length, 3 * LANES, F32),
             shaped(2, full, F32),

time: 296 us -> 294 us (level)
  waiting for transfers between devices: 66.9 us -> 73.6 us
  local copies, waits for them, and re-layouts: 14 us -> 7.59 us
  Pallas kernels: 128 us -> 125 us
    unnamed x113 -> x97, local copies, waits for them, and re-layouts: 8.41 us -> 1.99 us
    pallas_call x5, Pallas kernels: 34.7 us -> 30.3 us  [attention_backward(): pl.pallas_call(functools.partial(attention_backward_kernel, head_size, pa...]
  transfers between devices with their start and end apart: 48 -> 48, of which waited for: 16 -> 19; matrix products, arithmetic and copies ran while one was open for 5% -> 5% of each run, Pallas kernels for 39% -> 38%
where the time goes in v3:
time: 294 us; the launch traced here: 290 us
  Pallas kernels  125 us (43%)
  waiting for transfers between devices  73.6 us (25%)
  starting transfers between devices  62.4 us (21%)
  other arithmetic  9.64 us (3%)
  blocking collectives  9.18 us (3%)
  local copies, waits for them, and re-layouts  7.59 us (3%)
    pallas_call x31, Pallas kernels, call(): pl.pallas_call(body, out_shape=outs, in_specs=[SMEM] * scalars + [place]...  94.3 us
    ppermute x29, waiting for transfers between devices, swap(): return lax.ppermute(value, axis, SWAP)  43 us
    pallas_call x5, Pallas kernels, attention_backward(): pl.pallas_call(functools.partial(attention_backward_kernel, head_size, pa...  30.3 us
    ppermute x5, starting transfers between devices, line_first(): return (value, lax.ppermute(value, 'dp', [(0, 1), (3, 2)]))  25.2 us
    ppermute x29, starting transfers between devices, swap(): return lax.ppermute(value, axis, SWAP)  23 us
    ppermute x10, waiting for transfers between devices, line_next(): return (total, lax.ppermute(total, 'dp', pairs))  12.2 us
    ppermute x10, starting transfers between devices, line_next(): return (total, lax.ppermute(total, 'dp', pairs))  10.5 us
    all_gather x1, blocking collectives, per_device(): sums = jnp.sum(lax.all_gather(sums, ('row', 'y', 'core')), 0)  9.18 us
  transfers between devices with their start and end apart: 48, of which 19 were waited for; matrix products, arithmetic and copies ran while one was open for 5% of the time, Pallas kernels for 38%

profile of v3, /device:TPU:0, one launch (start us, length us, event | category | flops | bytes accessed | tf_op | source)
XLA Modules:
  0.0 289.9 jit_solution(9469763415255430944)
XLA Ops:
  0.7 3.0 %collective-permute-start = (bf16[256,384]{1,0:T(8,128)(2,1)}, bf16[256,384]{1,0:T(8,128)(2,1)S(1)}, u32[]{:S(2)}, u32[]{:S(2)}) collective-permute-start(bf16[256,384]{1,0:T(8,128)(2,1)} %refs_1_.4), channel_id=1, source_target_pairs={{0,4},{4,0},{1,5},{5,1},{2,6},{6,2},{3,7},{7,3},{8,12},{12,8},{9,1... | collective-permute-start | bytes 589832 | tf_op jit(solution)/shard_map/ppermute | solution.py:155
  3.7 1.5 collective-permute-start.1
  5.8 3.2 %pack_decoder.1 = (bf16[2448,128]{1,0:T(8,128)(2,1)}, bf16[2448,128]{1,0:T(8,128)(2,1)}) custom-call(s32[4]{0:T(128)} %pad_add_fusion.refs_0_, bf16[3,128,256]{2,1,0:T(8,128)(2,1)} %bitcast.47, bf16[256,128]{1,0:T(8,128)(2,1)} %refs_2_.1, bf16[128,1024]{1,0:T(8,128)(2,1)} %refs_3_.1, bf16[1024,128]{1,0:T(8,128)(2,1)} %refs_4_.1, f32[1,128]{1,0:T(1,128)} %bitcast.52, ...), custom_call_target="tpu_custom_call" | custom-call | flops 10000000 | bytes 1 | tf_op jit(solution)/shard_map/pack_decoder/pallas_call | solution.py:235
  10.2 2.3 pack_mixing.1.refs_3_.refs_1_
  13.0 1.7 collective-permute-start.3
  14.7 2.5 pack_encoder.1.refs_4_.refs_2_
  17.3 1.5 join_decoder.1
  19.1 1.6 collective-permute-start.6
  20.8 8.0 %collective-permute-done.2.refs_4_.refs_2_ = bf16[2352,128]{1,0:T(8,128)(2,1)S(1)} collective-permute-done((bf16[2352,128]{1,0:T(8,128)(2,1)}, bf16[2352,128]{1,0:T(8,128)(2,1)S(1)}, u32[]{:S(2)}, u32[]{:S(2)}) %collective-permute-start.2) | collective-permute-done | bytes 602144 | tf_op jit(solution)/shard_map/ppermute | solution.py:155
  31.1 1.3 collective-permute-start.9
  32.7 2.9 join_input.1.refs_1_
  36.4 1.3 collective-permute-start.14
  38.2 1.3 collective-permute-start.11
  39.5 1.4 collective-permute-start.12
  42.2 1.8 first_norm.1
  44.0 4.6 %encoder_mixing.1 = (bf16[1024,1152]{1,0:T(8,128)(2,1)S(1)}, bf16[768,1152]{1,0:T(8,128)(2,1)S(1)}, bf16[384,768]{1,0:T(8,128)(2,1)S(1)}) custom-call(bf16[1024,768]{1,0:T(8,128)(2,1)S(1)} %get-tuple-element.170.refs_0_, bf16[2352,128]{1,0:T(8,128)(2,1)S(1)} %copy-done.11, bf16[2352,128]{1,0:T(8,128)(2,1)S(1)} %collective-permute-done.2.refs_4_.refs_2_, ...), custom_call_target="tpu_custom_call" | custom-call | flops 30000000 | bytes 1 | tf_op jit(solution)/shard_map/encoder_mixing/pallas_call | solution.py:235
  48.7 9.0 %encoder_attend.1 = (bf16[1024,384]{1,0:T(8,128)(2,1)S(1)}, f32[1024,384]{1,0:T(8,128)S(1)}, bf16[1024,768]{1,0:T(8,128)(2,1)S(1)}) custom-call(bf16[1024,1152]{1,0:T(8,128)(2,1)S(1)} %get-tuple-element.171.refs_0_.mixed_ref, s32[1024,1]{1,0:T(8,128)S(1)} %copy.42.refs_1_, bf16[384,768]{1,0:T(8,128)(2,1)S(1)} %get-tuple-element.172.refs_2_.refs_6_), custom_call_target="tpu_custom_call" | custom-call | flops 120000000 | bytes 1 | tf_op jit(solution)/shard_map/encoder_attend/pallas_call | solution.py:235
  57.7 16.3 %collective-permute-done.11.refs_5_.refs_3_ = bf16[4608,128]{1,0:T(8,128)(2,1)S(1)} collective-permute-done((bf16[4608,128]{1,0:T(8,128)(2,1)S(1)}, bf16[4608,128]{1,0:T(8,128)(2,1)S(1)}, u32[]{:S(2)}, u32[]{:S(2)}) %collective-permute-start.11) | collective-permute-done | bytes 1179680 | tf_op jit(solution)/shard_map/ppermute | solution.py:155
  74.6 1.3 collective-permute-start.15
  75.9 1.3 collective-permute-start.16
  80.1 10.8 %collective-permute-done.15.refs_7_.refs_5_ = bf16[2304,128]{1,0:T(8,128)(2,1)S(1)} collective-permute-done((bf16[2304,128]{1,0:T(8,128)(2,1)S(1)}, bf16[2304,128]{1,0:T(8,128)(2,1)S(1)}, u32[]{:S(2)}, u32[]{:S(2)}) %collective-permute-start.15) | collective-permute-done | bytes 589856 | tf_op jit(solution)/shard_map/ppermute | solution.py:155
  90.9 1.3 collective-permute-done.16.refs_8_.refs_6_
  92.2 1.3 collective-permute-start.21
  94.3 9.2 %feed_forward.1 = (f32[1024,768]{1,0:T(8,128)S(1)}, bf16[1024,768]{1,0:T(8,128)(2,1)S(1)}, bf16[1024,1536]{1,0:T(8,128)(2,1)S(1)}, bf16[1024,1536]{1,0:T(8,128)(2,1)S(1)}, bf16[1024,768]{1,0:T(8,128)(2,1)S(1)}) custom-call(bf16[1024,768]{1,0:T(8,128)(2,1)S(1)} %get-tuple-element.169.refs_0_.refs_3_, bf16[1024,768]{1,0:T(8,128)(2,1)S(1)} %get-tuple-element.173.refs_1_, ...), custom_call_target="tpu_custom_call" | custom-call | flops 120000000 | bytes 1 | tf_op jit(solution)/shard_map/feed_forward/pallas_call | solution.py:235
  103.6 1.5 collective-permute-start.23
  105.1 1.8 collective-permute-done.17.refs_3_
  106.9 5.3 %bridge.1 = (f32[256,384]{1,0:T(8,128)}, bf16[1024,384]{1,0:T(8,128)(2,1)S(1)}, f32[1024,512]{1,0:T(8,128)S(1)}, bf16[1024,512]{1,0:T(8,128)(2,1)S(1)}, bf16[102...) custom-call(s32[4]{0:T(128)S(1)} %copy-done.28, ...), custom_call_target="tpu_custom_call" | custom-call | flops 57000000 | bytes 1 | tf_op jit(solution)/shard_map/bridge/pallas_call | solution.py:235
  112.3 11.3 %decoder_attend.1 = (bf16[1024,256]{1,0:T(8,128)(2,1)S(1)}, f32[1024,256]{1,0:T(8,128)S(1)}, bf16[1024,512]{1,0:T(8,128)(2,1)S(1)}) custom-call(bf16[1024,768]{1,0:T(8,128)(2,1)S(1)} %get-tuple-element.188.refs_0_.mixed_ref, s32[1024,1]{1,0:T(8,128)S(1)} %copy.42.refs_1_, bf16[256,512]{1,0:T(8,128)(2,1)S(1)} %get-tuple-element.189.refs_2_.refs_6_), custom_call_target="tpu_custom_call" | custom-call | flops 110000000 | bytes 1 | tf_op jit(solution)/shard_map/decoder_attend/pallas_call | solution.py:235
  123.8 5.9 %collective-permute-done.23.refs_8_ = bf16[3072,128]{1,0:T(8,128)(2,1)S(1)} collective-permute-done((bf16[3072,128]{1,0:T(8,128)(2,1)}, bf16[3072,128]{1,0:T(8,128)(2,1)S(1)}, u32[]{:S(2)}, u32[]{:S(2)}) %collective-permute-start.23) | collective-permute-done | bytes 786464 | tf_op jit(solution)/shard_map/ppermute | solution.py:175
  129.7 7.9 %decoder_feed.1 = (f32[1024,512]{1,0:T(8,128)S(1)}, bf16[1024,512]{1,0:T(8,128)(2,1)S(1)}, bf16[1024,1024]{1,0:T(8,128)(2,1)S(1)}, bf16[1024,1024]{1,0:T(8,128)(...) custom-call(s32[4]{0:T(128)S(1)} %copy-done.28, ...), custom_call_target="tpu_custom_call" | custom-call | flops 80000000 | bytes 1 | tf_op jit(solution)/shard_map/decoder_feed/pallas_call | solution.py:235
  138.9 3.5 %collective-permute-start.25 = (bf16[2048,128]{1,0:T(8,128)(2,1)S(1)}, bf16[2048,128]{1,0:T(8,128)(2,1)S(1)}, u32[]{:S(2)}, u32[]{:S(2)}) collective-permute-start(bf16[2048,128]{1,0:T(8,128)(2,1)S(1)} %decoder_feed_grads.1), channel_id=1, source_target_pairs={{0,8},{24,16},{1,9},{25,17},{2,10},{26,18},{3,11},{27,19},{4,12},{... | collective-permute-start | bytes 1572872 | tf_op jit(solution)/shard_map/ppermute | solution.py:964
  142.5 2.7 decoder_middle_back.1
  145.1 8.5 %attention_backward.5 = (bf16[1024,128]{1,0:T(8,128)(2,1)S(1)}, bf16[1024,128]{1,0:T(8,128)(2,1)S(1)}, bf16[1024,128]{1,0:T(8,128)(2,1)S(1)}) custom-call(bf16[1024,768]{1,0:T(8,128)(2,1)S(1)} %get-tuple-element.188.refs_0_.mixed_ref, bf16[1024,256]{1,0:T(8,128)(2,1)S(1)} %get-tuple-element.198.att_all_ref.refs_5_, ...), custom_call_target="tpu_custom_call" | custom-call | flops 96000000 | bytes 1 | tf_op jit(solution)/shard_map/attention_backward/pallas_call | solution.py:133
  154.8 8.5 %attention_backward.6 = (bf16[1024,128]{1,0:T(8,128)(2,1)S(1)}, bf16[1024,128]{1,0:T(8,128)(2,1)S(1)}, bf16[1024,128]{1,0:T(8,128)(2,1)S(1)}) custom-call(bf16[1024,768]{1,0:T(8,128)(2,1)S(1)} %get-tuple-element.188.refs_0_.mixed_ref, bf16[1024,256]{1,0:T(8,128)(2,1)S(1)} %get-tuple-element.198.att_all_ref.refs_5_, ...), custom_call_target="tpu_custom_call" | custom-call | flops 96000000 | bytes 1 | tf_op jit(solution)/shard_map/attention_backward/pallas_call | solution.py:133
  164.8 2.6 collective-permute-done.27.refs_2_
  167.4 3.8 %bridge_back.1 = (bf16[1024,512]{1,0:T(8,128)(2,1)S(1)}, f32[1024,768]{1,0:T(8,128)S(1)}, bf16[1024,768]{1,0:T(8,128)(2,1)S(1)}, f32[2,512]{1,0:T(2,128)S(1)}) custom-call(s32[4]{0:T(128)S(1)} %copy-done.28, bf16[1024,512]{1,0:T(8,128)(2,1)S(1)} %decoder_mixed_back.1.refs_1_, bf16[1024,512]{1,0:T(8,128)(2,1)S(1)} %collective-permute-done.27.refs_2_, ...), custom_call_target="tpu_custom_call" | custom-call | flops 39000000 | bytes 1 | tf_op jit(solution)/shard_map/bridge_back/pallas_call | solution.py:235
  171.3 1.3 decoder_mixing_grads.1
  172.6 9.9 %collective-permute-start.28 = (bf16[1408,128]{1,0:T(8,128)(2,1)S(1)}, bf16[1408,128]{1,0:T(8,128)(2,1)S(1)}, u32[]{:S(2)}, u32[]{:S(2)}) collective-permute-start(bf16[1408,128]{1,0:T(8,128)(2,1)S(1)} %decoder_mixing_grads.1), channel_id=1, source_target_pairs={{0,8},{24,16},{1,9},{25,17},{2,10},{26,18},{3,11},{27,19},{4,12},{... | collective-permute-start | bytes 1081352 | tf_op jit(solution)/shard_map/ppermute | solution.py:964
  183.6 1.5 collective-permute-start.30
  185.2 7.3 %feed_back.1 = (bf16[1024,1536]{1,0:T(8,128)(2,1)S(1)}, bf16[1024,768]{1,0:T(8,128)(2,1)S(1)}) custom-call(bf16[1024,768]{1,0:T(8,128)(2,1)S(1)} %get-tuple-element.229.refs_1_.refs_0_, bf16[1024,1536]{1,0:T(8,128)(2,1)S(1)} %get-tuple-element.230.refs_1_, bf16[4608,128]{1,0:T(8,128)(2,1)S(1)} %copy-done.2, bf16[4608,128]{1,0:T(8,128)(2,1)S(1)} %copy-done.4, ...), custom_call_target="tpu_custom_call" | custom-call | flops 120000000 | bytes 1 | tf_op jit(solution)/shard_map/feed_back/pallas_call | solution.py:235
  193.5 3.1 %collective-permute-start.32 = (bf16[384,768]{1,0:T(8,128)(2,1)S(1)}, bf16[384,768]{1,0:T(8,128)(2,1)S(1)}, u32[]{:S(2)}, u32[]{:S(2)}) collective-permute-start(bf16[384,768]{1,0:T(8,128)(2,1)S(1)} %encoder_up_grads.1), channel_id=1, source_target_pairs={{0,8},{24,16},{1,9},{25,17},{2,10},{26,18},{3,11},{27,19},{4,12},{... | collective-permute-start | bytes 1769480 | tf_op jit(solution)/shard_map/ppermute | solution.py:964
  196.6 1.3 collective-permute-start.33
  198.7 4.5 %encoder_middle_back.1 = (f32[256,768]{1,0:T(8,128)S(1)}, bf16[1024,384]{1,0:T(8,128)(2,1)S(1)}, f32[1024,384]{1,0:T(8,128)S(1)}, f32[2,768]{1,0:T(2,128)S(1)}) custom-call(s32[4]{0:T(128)S(1)} %copy-done.28, bf16[1024,768]{1,0:T(8,128)(2,1)S(1)} %get-tuple-element.237.refs_1_, bf16[1024,768]{1,0:T(8,128)(2,1)S(1)} %collective-permute-done.29.refs_2_, ...), custom_call_target="tpu_custom_call" | custom-call | flops 55000000 | bytes 1 | tf_op jit(solution)/shard_map/encoder_middle_back/pallas_call | solution.py:235
  204.8 4.4 %attention_backward.7 = (bf16[1024,128]{1,0:T(8,128)(2,1)S(1)}, bf16[1024,128]{1,0:T(8,128)(2,1)S(1)}, bf16[1024,128]{1,0:T(8,128)(2,1)S(1)}) custom-call(bf16[1024,1152]{1,0:T(8,128)(2,1)S(1)} %copy-done.1, bf16[1024,384]{1,0:T(8,128)(2,1)S(1)} %get-tuple-element.176.att_all_ref.refs_7_, f32[1024,384]{1,0:T(8,128)S(1)} %get-tuple-element.197.inv_all_ref, ...), custom_call_target="tpu_custom_call" | custom-call | flops 52000000 | bytes 1 | tf_op jit(solution)/shard_map/attention_backward/pallas_call | solution.py:133
  209.2 6.6 %collective-permute-done.32 = bf16[384,768]{1,0:T(8,128)(2,1)S(1)} collective-permute-done((bf16[384,768]{1,0:T(8,128)(2,1)S(1)}, bf16[384,768]{1,0:T(8,128)(2,1)S(1)}, u32[]{:S(2)}, u32[]{:S(2)}) %collective-permute-start.32) | collective-permute-done | bytes 589856 | tf_op jit(solution)/shard_map/ppermute | solution.py:964
  217.0 4.4 %attention_backward.8 = (bf16[1024,128]{1,0:T(8,128)(2,1)S(1)}, bf16[1024,128]{1,0:T(8,128)(2,1)S(1)}, bf16[1024,128]{1,0:T(8,128)(2,1)S(1)}) custom-call(bf16[1024,1152]{1,0:T(8,128)(2,1)S(1)} %copy-done.1, bf16[1024,384]{1,0:T(8,128)(2,1)S(1)} %get-tuple-element.176.att_all_ref.refs_7_, f32[1024,384]{1,0:T(8,128)S(1)} %get-tuple-element.197.inv_all_ref, ...), custom_call_target="tpu_custom_call" | custom-call | flops 52000000 | bytes 1 | tf_op jit(solution)/shard_map/attention_backward/pallas_call | solution.py:133
  222.6 7.2 %collective-permute-start.34 = (bf16[2304,128]{1,0:T(8,128)(2,1)S(1)}, bf16[2304,128]{1,0:T(8,128)(2,1)S(1)}, u32[]{:S(2)}, u32[]{:S(2)}) collective-permute-start(bf16[2304,128]{1,0:T(8,128)(2,1)S(1)} %encoder_mixing_grads.1), channel_id=1, source_target_pairs={{0,8},{24,16},{1,9},{25,17},{2,10},{26,18},{3,11},{27,19},{4,12},{... | collective-permute-start | bytes 1769480 | tf_op jit(solution)/shard_map/ppermute | solution.py:964
  229.8 1.3 collective-permute-start.35
  232.1 1.3 collective-permute-start.39
  234.4 8.7 %collective-permute-done.35 = bf16[1408,128]{1,0:T(8,128)(2,1)S(1)} collective-permute-done((bf16[1408,128]{1,0:T(8,128)(2,1)S(1)}, bf16[1408,128]{1,0:T(8,128)(2,1)S(1)}, u32[]{:S(2)}, u32[]{:S(2)}) %collective-permute-start.35) | collective-permute-done | bytes 360480 | tf_op jit(solution)/shard_map/ppermute | solution.py:980
  243.1 4.4 %attention_backward.9 = (bf16[1024,128]{1,0:T(8,128)(2,1)S(1)}, bf16[1024,128]{1,0:T(8,128)(2,1)S(1)}, bf16[1024,128]{1,0:T(8,128)(2,1)S(1)}) custom-call(bf16[1024,1152]{1,0:T(8,128)(2,1)S(1)} %copy-done.1, bf16[1024,384]{1,0:T(8,128)(2,1)S(1)} %get-tuple-element.176.att_all_ref.refs_7_, f32[1024,384]{1,0:T(8,128)S(1)} %get-tuple-element.197.inv_all_ref, ...), custom_call_target="tpu_custom_call" | custom-call | flops 52000000 | bytes 1 | tf_op jit(solution)/shard_map/attention_backward/pallas_call | solution.py:133
  248.5 2.5 encoder_mixed_back.1
  251.7 1.3 collective-permute-start.47
  253.5 2.1 input_back.1
  255.8 9.2 %all-gather = f32[64,768]{1,0:T(8,128)S(1)} all-gather(f32[8,768]{1,0:T(8,128)S(1)} %select_maximum_fusion), channel_id=2, replica_groups=mesh['dp'=4,'row'=2,'y'=2,'core'=2] {'row','y','core'}, dimensions={0}, use_global_device_ids=true | all-gather | bytes 221184 | tf_op jit(solution)/shard_map/all_gather | solution.py:1408
  265.1 1.4 collective-permute-start.46
  266.6 3.0 %collective-permute-done.47 = bf16[384,768]{1,0:T(8,128)(2,1)S(1)} collective-permute-done((bf16[384,768]{1,0:T(8,128)(2,1)}, bf16[384,768]{1,0:T(8,128)(2,1)S(1)}, u32[]{:S(2)}, u32[]{:S(2)}) %collective-permute-start.47) | collective-permute-done | bytes 589856 | tf_op jit(solution)/shard_map/ppermute | solution.py:980
  273.7 1.7 convert_add_fusion
  275.4 1.9 decoder_unpack.1
  277.2 1.4 collective-permute-start.43
  278.6 2.2 select_convert_fusion.1
  281.7 1.9 collective-permute-done.43
  283.6 2.4 collective-permute-done.44
  288.2 1.2 encoder_unpack.1
  (208 shorter events, 34.2 us)
Async XLA Ops:
  0.7 8.4 %collective-permute-start = (bf16[256,384]{1,0:T(8,128)(2,1)}, bf16[256,384]{1,0:T(8,128)(2,1)S(1)}, u32[]{:S(2)}, u32[]{:S(2)}) collective-permute-start(bf16[256,384]{1,0:T(8,128)(2,1)} %refs_1_.4), channel_id=1, source_target_pairs={{0,4},{4,0},{1,5},{5,1},{2,6},{6,2},{3,7},{7,3},{8,12},{12,8},{9,1... | collective-permute-start | bytes 589832 | tf_op jit(solution)/shard_map/ppermute | solution.py:155
  3.7 6.6 %collective-permute-start.1 = (bf16[256,384]{1,0:T(8,128)(2,1)}, bf16[256,384]{1,0:T(8,128)(2,1)S(1)}, u32[]{:S(2)}, u32[]{:S(2)}) collective-permute-start(bf16[256,384]{1,0:T(8,128)(2,1)} %refs_1_.4), channel_id=1, source_target_pairs={{0,2},{2,0},{1,3},{3,1},{4,6},{6,4},{5,7},{7,5},{8,10},{10,8},{9,1... | collective-permute-start | bytes 589832 | tf_op jit(solution)/shard_map/ppermute | solution.py:155
  9.0 8.3 %collective-permute-start.4 = (bf16[2448,128]{1,0:T(8,128)(2,1)}, bf16[2448,128]{1,0:T(8,128)(2,1)S(1)}, u32[]{:S(2)}, u32[]{:S(2)}) collective-permute-start(bf16[2448,128]{1,0:T(8,128)(2,1)} %get-tuple-element.162), channel_id=1, source_target_pairs={{0,1},{1,0},{2,3},{3,2},{4,5},{5,4},{6,7},{7,6},{8,9},{9,8},{10,11... | collective-permute-start | bytes 1880072 | tf_op jit(solution)/shard_map/ppermute | solution.py:155
  9.1 8.1 %copy-start.39 = (bf16[256,384]{1,0:T(8,128)(2,1)}, bf16[256,384]{1,0:T(8,128)(2,1)S(1)}, u32[]{:S(2)}) copy-start(bf16[256,384]{1,0:T(8,128)(2,1)S(1)} %collective-permute-done.refs_2_) | copy-start | bytes 589828
  10.2 7.0 %copy-start.40 = (bf16[256,384]{1,0:T(8,128)(2,1)}, bf16[256,384]{1,0:T(8,128)(2,1)S(1)}, u32[]{:S(2)}) copy-start(bf16[256,384]{1,0:T(8,128)(2,1)S(1)} %collective-permute-done.1.refs_3_) | copy-start | bytes 589828
  12.6 16.2 %collective-permute-start.2 = (bf16[2352,128]{1,0:T(8,128)(2,1)}, bf16[2352,128]{1,0:T(8,128)(2,1)S(1)}, u32[]{:S(2)}, u32[]{:S(2)}) collective-permute-start(bf16[2352,128]{1,0:T(8,128)(2,1)} %pack_mixing.1.refs_3_.refs_1_), channel_id=1, source_target_pairs={{0,4},{4,0},{1,5},{5,1},{2,6},{6,2},{3,7},{7,3},{8,12},{12,8},{9,1... | collective-permute-start | bytes 1806344 | tf_op jit(solution)/shard_map/ppermute | solution.py:155
  13.0 16.5 %collective-permute-start.3 = (bf16[2352,128]{1,0:T(8,128)(2,1)}, bf16[2352,128]{1,0:T(8,128)(2,1)S(1)}, u32[]{:S(2)}, u32[]{:S(2)}) collective-permute-start(bf16[2352,128]{1,0:T(8,128)(2,1)} %pack_mixing.1.refs_3_.refs_1_), channel_id=1, source_target_pairs={{0,2},{2,0},{1,3},{3,1},{4,6},{6,4},{5,7},{7,5},{8,10},{10,8},{9,1... | collective-permute-start | bytes 1806344 | tf_op jit(solution)/shard_map/ppermute | solution.py:155
  17.2 15.3 %copy-start.25 = (s32[1024]{0:T(1024)S(1)}, s32[1024]{0:T(1024)}, u32[]{:S(2)}) copy-start(s32[1024]{0:T(1024)} %param.21) | copy-start | bytes 12292
  18.8 19.4 %copy-start.2 = (bf16[4608,128]{1,0:T(8,128)(2,1)S(1)}, bf16[4608,128]{1,0:T(8,128)(2,1)}, u32[]{:S(2)}) copy-start(bf16[4608,128]{1,0:T(8,128)(2,1)} %pack_encoder.1.refs_4_.refs_2_) | copy-start | bytes 3538948
  18.8 11.5 %collective-permute-start.5 = (bf16[128,384]{1,0:T(8,128)(2,1)S(1)}, bf16[128,384]{1,0:T(8,128)(2,1)S(1)}, u32[]{:S(2)}, u32[]{:S(2)}) collective-permute-start(bf16[128,384]{1,0:T(8,128)(2,1)S(1)} %slice.104), channel_id=1, source_target_pairs={{0,2},{2,0},{1,3},{3,1},{4,6},{6,4},{5,7},{7,5},{8,10},{10,8},{9,1... | collective-permute-start | bytes 294920 | tf_op jit(solution)/shard_map/ppermute | solution.py:155
  19.1 11.2 %collective-permute-start.6 = (bf16[128,384]{1,0:T(8,128)(2,1)S(1)}, bf16[128,384]{1,0:T(8,128)(2,1)S(1)}, u32[]{:S(2)}, u32[]{:S(2)}) collective-permute-start(bf16[128,384]{1,0:T(8,128)(2,1)S(1)} %slice.105), channel_id=1, source_target_pairs={{0,4},{4,0},{1,5},{5,1},{2,6},{6,2},{3,7},{7,3},{8,12},{12,8},{9,1... | collective-permute-start | bytes 294920 | tf_op jit(solution)/shard_map/ppermute | solution.py:155
  30.3 9.2 %collective-permute-start.8 = (bf16[1200,128]{1,0:T(8,128)(2,1)}, bf16[1200,128]{1,0:T(8,128)(2,1)}, u32[]{:S(2)}, u32[]{:S(2)}) collective-permute-start(bf16[1200,128]{1,0:T(8,128)(2,1)} %slice.106), channel_id=1, source_target_pairs={{0,2},{2,0},{1,3},{3,1},{4,6},{6,4},{5,7},{7,5},{8,10},{10,8},{9,1... | collective-permute-start | bytes 921608 | tf_op jit(solution)/shard_map/ppermute | solution.py:155
  31.1 7.0 %collective-permute-start.9 = (bf16[1152,128]{1,0:T(8,128)(2,1)}, bf16[1152,128]{1,0:T(8,128)(2,1)}, u32[]{:S(2)}, u32[]{:S(2)}) collective-permute-start(bf16[1152,128]{1,0:T(8,128)(2,1)} %slice.107), channel_id=1, source_target_pairs={{0,4},{4,0},{1,5},{5,1},{2,6},{6,2},{3,7},{7,3},{8,12},{12,8},{9,1... | collective-permute-start | bytes 884744 | tf_op jit(solution)/shard_map/ppermute | solution.py:155
  35.6 5.4 %collective-permute-start.7 = (bf16[512,768]{1,0:T(8,128)(2,1)}, bf16[512,768]{1,0:T(8,128)(2,1)S(1)}, u32[]{:S(2)}, u32[]{:S(2)}) collective-permute-start(bf16[512,768]{1,0:T(8,128)(2,1)} %join_input.1.refs_1_), channel_id=1, source_target_pairs={{0,1},{1,0},{2,3},{3,2},{4,5},{5,4},{6,7},{7,6},{8,9},{9,8},{10,11... | collective-permute-start | bytes 2359304 | tf_op jit(solution)/shard_map/ppermute | solution.py:155
  35.6 38.9 %collective-permute-start.13 = (bf16[1824,128]{1,0:T(8,128)(2,1)S(1)}, bf16[1824,128]{1,0:T(8,128)(2,1)S(1)}, u32[]{:S(2)}, u32[]{:S(2)}) collective-permute-start(bf16[1824,128]{1,0:T(8,128)(2,1)S(1)} %get-tuple-element.177.refs_4_), channel_id=1, source_target_pairs={{0,4},{4,0},{1,5},{5,1},{2,6},{6,2},{3,7},{7,3},{8,12},{12,8},{9,1... | collective-permute-start | bytes 1400840 | tf_op jit(solution)/shard_map/ppermute | solution.py:155
  36.4 38.1 %collective-permute-start.14 = (bf16[1824,128]{1,0:T(8,128)(2,1)S(1)}, bf16[1824,128]{1,0:T(8,128)(2,1)S(1)}, u32[]{:S(2)}, u32[]{:S(2)}) collective-permute-start(bf16[1824,128]{1,0:T(8,128)(2,1)S(1)} %get-tuple-element.177.refs_4_), channel_id=1, source_target_pairs={{0,2},{2,0},{1,3},{3,1},{4,6},{6,4},{5,7},{7,5},{8,10},{10,8},{9,1... | collective-permute-start | bytes 1400840 | tf_op jit(solution)/shard_map/ppermute | solution.py:155
  38.2 35.9 %collective-permute-start.11 = (bf16[4608,128]{1,0:T(8,128)(2,1)S(1)}, bf16[4608,128]{1,0:T(8,128)(2,1)S(1)}, u32[]{:S(2)}, u32[]{:S(2)}) collective-permute-start(bf16[4608,128]{1,0:T(8,128)(2,1)S(1)} %copy-done.2), channel_id=1, source_target_pairs={{0,4},{4,0},{1,5},{5,1},{2,6},{6,2},{3,7},{7,3},{8,12},{12,8},{9,1... | collective-permute-start | bytes 3538952 | tf_op jit(solution)/shard_map/ppermute | solution.py:155
  39.5 35.0 %collective-permute-start.12 = (bf16[4608,128]{1,0:T(8,128)(2,1)S(1)}, bf16[4608,128]{1,0:T(8,128)(2,1)S(1)}, u32[]{:S(2)}, u32[]{:S(2)}) collective-permute-start(bf16[4608,128]{1,0:T(8,128)(2,1)S(1)} %copy-done.2), channel_id=1, source_target_pairs={{0,2},{2,0},{1,3},{3,1},{4,6},{6,4},{5,7},{7,5},{8,10},{10,8},{9,1... | collective-permute-start | bytes 3538952 | tf_op jit(solution)/shard_map/ppermute | solution.py:155
  44.0 50.2 %copy-start.7 = (bf16[1024,768]{1,0:T(8,128)(2,1)}, bf16[1024,768]{1,0:T(8,128)(2,1)S(1)}, u32[]{:S(2)}) copy-start(bf16[1024,768]{1,0:T(8,128)(2,1)S(1)} %get-tuple-element.169.refs_0_.refs_3_) | copy-start | bytes 4718596
  44.0 154.6 %copy-start.29 = (f32[4,768]{1,0:T(4,128)}, f32[4,768]{1,0:T(4,128)S(1)}, u32[]{:S(2)}) copy-start(f32[4,768]{1,0:T(4,128)S(1)} %get-tuple-element.174.refs_3_.refs_5_) | copy-start | bytes 36868
  48.7 9.0 %copy-start = (bf16[1024,1152]{1,0:T(8,128)(2,1)}, bf16[1024,1152]{1,0:T(8,128)(2,1)S(1)}, u32[]{:S(2)}) copy-start(bf16[1024,1152]{1,0:T(8,128)(2,1)S(1)} %get-tuple-element.171.refs_0_.mixed_ref) | copy-start | bytes 7077892
  48.7 9.0 %copy-start.18 = (bf16[384,768]{1,0:T(8,128)(2,1)}, bf16[384,768]{1,0:T(8,128)(2,1)S(1)}, u32[]{:S(2)}) copy-start(bf16[384,768]{1,0:T(8,128)(2,1)S(1)} %get-tuple-element.172.refs_2_.refs_6_) | copy-start | bytes 1769476
  74.0 20.2 %copy-start.3 = (bf16[4608,128]{1,0:T(8,128)(2,1)}, bf16[4608,128]{1,0:T(8,128)(2,1)S(1)}, u32[]{:S(2)}) copy-start(bf16[4608,128]{1,0:T(8,128)(2,1)S(1)} %collective-permute-done.11.refs_5_.refs_3_) | copy-start | bytes 3538948
  74.5 19.8 %copy-start.5 = (bf16[4608,128]{1,0:T(8,128)(2,1)}, bf16[4608,128]{1,0:T(8,128)(2,1)S(1)}, u32[]{:S(2)}) copy-start(bf16[4608,128]{1,0:T(8,128)(2,1)S(1)} %collective-permute-done.12.refs_6_.refs_4_) | copy-start | bytes 3538948
  74.6 16.3 %collective-permute-start.15 = (bf16[2304,128]{1,0:T(8,128)(2,1)S(1)}, bf16[2304,128]{1,0:T(8,128)(2,1)S(1)}, u32[]{:S(2)}, u32[]{:S(2)}) collective-permute-start(bf16[2304,128]{1,0:T(8,128)(2,1)S(1)} %slice.108), channel_id=1, source_target_pairs={{0,2},{2,0},{1,3},{3,1},{4,6},{6,4},{5,7},{7,5},{8,10},{10,8},{9,1... | collective-permute-start | bytes 1769480 | tf_op jit(solution)/shard_map/ppermute | solution.py:155
  75.9 16.3 %collective-permute-start.16 = (bf16[2304,128]{1,0:T(8,128)(2,1)S(1)}, bf16[2304,128]{1,0:T(8,128)(2,1)S(1)}, u32[]{:S(2)}, u32[]{:S(2)}) collective-permute-start(bf16[2304,128]{1,0:T(8,128)(2,1)S(1)} %slice.109), channel_id=1, source_target_pairs={{0,4},{4,0},{1,5},{5,1},{2,6},{6,2},{3,7},{7,3},{8,12},{12,8},{9,1... | collective-permute-start | bytes 1769480 | tf_op jit(solution)/shard_map/ppermute | solution.py:155
  78.6 26.5 %collective-permute-start.19 = (bf16[1024,128]{1,0:T(8,128)(2,1)}, bf16[1024,128]{1,0:T(8,128)(2,1)}, u32[]{:S(2)}, u32[]{:S(2)}) collective-permute-start(bf16[1024,128]{1,0:T(8,128)(2,1)} %slice.111), channel_id=1, source_target_pairs={{0,4},{4,0},{1,5},{5,1},{2,6},{6,2},{3,7},{7,3},{8,12},{12,8},{9,1... | collective-permute-start | bytes 786440 | tf_op jit(solution)/shard_map/ppermute | solution.py:155
  79.3 24.2 %collective-permute-start.18 = (bf16[800,128]{1,0:T(8,128)(2,1)}, bf16[800,128]{1,0:T(8,128)(2,1)}, u32[]{:S(2)}, u32[]{:S(2)}) collective-permute-start(bf16[800,128]{1,0:T(8,128)(2,1)} %slice.110), channel_id=1, source_target_pairs={{0,2},{2,0},{1,3},{3,1},{4,6},{6,4},{5,7},{7,5},{8,10},{10,8},{9,1... | collective-permute-start | bytes 614408 | tf_op jit(solution)/shard_map/ppermute | solution.py:155
  80.1 14.1 %collective-permute-start.10 = (bf16[1024,768]{1,0:T(8,128)(2,1)S(1)}, bf16[1024,768]{1,0:T(8,128)(2,1)S(1)}, u32[]{:S(2)}, u32[]{:S(2)}) collective-permute-start(bf16[1024,768]{1,0:T(8,128)(2,1)S(1)} %get-tuple-element.173.refs_1_), channel_id=1, source_target_pairs={{0,1},{1,0},{2,3},{3,2},{4,5},{5,4},{6,7},{7,6},{8,9},{9,8},{10,11... | collective-permute-start | bytes 4718600 | tf_op jit(solution)/shard_map/ppermute | solution.py:155
  92.2 31.6 %collective-permute-start.21 = (bf16[3072,128]{1,0:T(8,128)(2,1)}, bf16[3072,128]{1,0:T(8,128)(2,1)}, u32[]{:S(2)}, u32[]{:S(2)}) collective-permute-start(bf16[3072,128]{1,0:T(8,128)(2,1)} %get-tuple-element.277.refs_5_), channel_id=1, source_target_pairs={{0,4},{4,0},{1,5},{5,1},{2,6},{6,2},{3,7},{7,3},{8,12},{12,8},{9,1... | collective-permute-start | bytes 2359304 | tf_op jit(solution)/shard_map/ppermute | solution.py:155
  93.5 30.3 %collective-permute-start.22 = (bf16[3072,128]{1,0:T(8,128)(2,1)}, bf16[3072,128]{1,0:T(8,128)(2,1)}, u32[]{:S(2)}, u32[]{:S(2)}) collective-permute-start(bf16[3072,128]{1,0:T(8,128)(2,1)} %get-tuple-element.277.refs_5_), channel_id=1, source_target_pairs={{0,2},{2,0},{1,3},{3,1},{4,6},{6,4},{5,7},{7,5},{8,10},{10,8},{9,1... | collective-permute-start | bytes 2359304 | tf_op jit(solution)/shard_map/ppermute | solution.py:155
  103.5 3.5 %collective-permute-start.17 = (bf16[1024,768]{1,0:T(8,128)(2,1)S(1)}, bf16[1024,768]{1,0:T(8,128)(2,1)S(1)}, u32[]{:S(2)}, u32[]{:S(2)}) collective-permute-start(bf16[1024,768]{1,0:T(8,128)(2,1)S(1)} %get-tuple-element.182.refs_2_), channel_id=1, source_target_pairs={{0,1},{1,0},{2,3},{3,2},{4,5},{5,4},{6,7},{7,6},{8,9},{9,8},{10,11... | collective-permute-start | bytes 4718600 | tf_op jit(solution)/shard_map/ppermute | solution.py:155
  103.6 26.1 %collective-permute-start.23 = (bf16[3072,128]{1,0:T(8,128)(2,1)}, bf16[3072,128]{1,0:T(8,128)(2,1)S(1)}, u32[]{:S(2)}, u32[]{:S(2)}) collective-permute-start(bf16[3072,128]{1,0:T(8,128)(2,1)} %get-tuple-element.277.refs_5_), channel_id=1, source_target_pairs={{0,6},{2,4},{4,2},{6,0},{1,7},{3,5},{5,3},{7,1},{8,14},{10,12},{12... | collective-permute-start | bytes 2359304 | tf_op jit(solution)/shard_map/ppermute | solution.py:175
  123.6 6.1 %collective-permute-start.20 = (bf16[1024,512]{1,0:T(8,128)(2,1)S(1)}, bf16[1024,512]{1,0:T(8,128)(2,1)S(1)}, u32[]{:S(2)}, u32[]{:S(2)}) collective-permute-start(bf16[1024,512]{1,0:T(8,128)(2,1)S(1)} %get-tuple-element.190.refs_2_), channel_id=1, source_target_pairs={{0,1},{1,0},{2,3},{3,2},{4,5},{5,4},{6,7},{7,6},{8,9},{9,8},{10,11... | collective-permute-start | bytes 3145736 | tf_op jit(solution)/shard_map/ppermute | solution.py:155
  137.6 4.8 %collective-permute-start.24 = (bf16[1024,512]{1,0:T(8,128)(2,1)S(1)}, bf16[1024,512]{1,0:T(8,128)(2,1)S(1)}, u32[]{:S(2)}, u32[]{:S(2)}) collective-permute-start(bf16[1024,512]{1,0:T(8,128)(2,1)S(1)} %get-tuple-element.205.refs_1_), channel_id=1, source_target_pairs={{0,1},{1,0},{2,3},{3,2},{4,5},{5,4},{6,7},{7,6},{8,9},{9,8},{10,11... | collective-permute-start | bytes 3145736 | tf_op jit(solution)/shard_map/ppermute | solution.py:155
  138.9 14.8 %collective-permute-start.25 = (bf16[2048,128]{1,0:T(8,128)(2,1)S(1)}, bf16[2048,128]{1,0:T(8,128)(2,1)S(1)}, u32[]{:S(2)}, u32[]{:S(2)}) collective-permute-start(bf16[2048,128]{1,0:T(8,128)(2,1)S(1)} %decoder_feed_grads.1), channel_id=1, source_target_pairs={{0,8},{24,16},{1,9},{25,17},{2,10},{26,18},{3,11},{27,19},{4,12},{... | collective-permute-start | bytes 1572872 | tf_op jit(solution)/shard_map/ppermute | solution.py:964
  153.9 9.4 %collective-permute-start.26 = (bf16[2048,128]{1,0:T(8,128)(2,1)S(1)}, bf16[2048,128]{1,0:T(8,128)(2,1)S(1)}, u32[]{:S(2)}, u32[]{:S(2)}) collective-permute-start(bf16[2048,128]{1,0:T(8,128)(2,1)S(1)} %add_convert_fusion.7), channel_id=1, source_target_pairs={{8,16},{16,8},{9,17},{17,9},{10,18},{18,10},{11,19},{19,11},{12,20... | collective-permute-start | bytes 1572872 | tf_op jit(solution)/shard_map/ppermute | solution.py:980
  163.5 33.1 %copy-start.33 = (bf16[2048,128]{1,0:T(8,128)(2,1)}, bf16[2048,128]{1,0:T(8,128)(2,1)S(1)}, u32[]{:S(2)}) copy-start(bf16[2048,128]{1,0:T(8,128)(2,1)S(1)} %add_convert_fusion.6) | copy-start | bytes 1572868
  164.7 2.7 collective-permute-start.27
  172.6 20.0 %collective-permute-start.28 = (bf16[1408,128]{1,0:T(8,128)(2,1)S(1)}, bf16[1408,128]{1,0:T(8,128)(2,1)S(1)}, u32[]{:S(2)}, u32[]{:S(2)}) collective-permute-start(bf16[1408,128]{1,0:T(8,128)(2,1)S(1)} %decoder_mixing_grads.1), channel_id=1, source_target_pairs={{0,8},{24,16},{1,9},{25,17},{2,10},{26,18},{3,11},{27,19},{4,12},{... | collective-permute-start | bytes 1081352 | tf_op jit(solution)/shard_map/ppermute | solution.py:964
  183.6 20.3 %collective-permute-start.30 = (bf16[768,384]{1,0:T(8,128)(2,1)S(1)}, bf16[768,384]{1,0:T(8,128)(2,1)S(1)}, u32[]{:S(2)}, u32[]{:S(2)}) collective-permute-start(bf16[768,384]{1,0:T(8,128)(2,1)S(1)} %encoder_down_grads.1), channel_id=1, source_target_pairs={{0,8},{24,16},{1,9},{25,17},{2,10},{26,18},{3,11},{27,19},{4,12},{... | collective-permute-start | bytes 1769480 | tf_op jit(solution)/shard_map/ppermute | solution.py:964
  192.5 6.1 %collective-permute-start.29 = (bf16[1024,768]{1,0:T(8,128)(2,1)S(1)}, bf16[1024,768]{1,0:T(8,128)(2,1)S(1)}, u32[]{:S(2)}, u32[]{:S(2)}) collective-permute-start(bf16[1024,768]{1,0:T(8,128)(2,1)S(1)} %get-tuple-element.237.refs_1_), channel_id=1, source_target_pairs={{0,1},{1,0},{2,3},{3,2},{4,5},{5,4},{6,7},{7,6},{8,9},{9,8},{10,11... | collective-permute-start | bytes 4718600 | tf_op jit(solution)/shard_map/ppermute | solution.py:155
  193.5 22.2 %collective-permute-start.32 = (bf16[384,768]{1,0:T(8,128)(2,1)S(1)}, bf16[384,768]{1,0:T(8,128)(2,1)S(1)}, u32[]{:S(2)}, u32[]{:S(2)}) collective-permute-start(bf16[384,768]{1,0:T(8,128)(2,1)S(1)} %encoder_up_grads.1), channel_id=1, source_target_pairs={{0,8},{24,16},{1,9},{25,17},{2,10},{26,18},{3,11},{27,19},{4,12},{... | collective-permute-start | bytes 1769480 | tf_op jit(solution)/shard_map/ppermute | solution.py:964
  196.6 20.4 %collective-permute-start.33 = (bf16[2048,128]{1,0:T(8,128)(2,1)S(1)}, bf16[2048,128]{1,0:T(8,128)(2,1)S(1)}, u32[]{:S(2)}, u32[]{:S(2)}) collective-permute-start(bf16[2048,128]{1,0:T(8,128)(2,1)S(1)} %add_convert_fusion.6), channel_id=1, source_target_pairs={{8,0},{16,24},{9,1},{17,25},{10,2},{18,26},{11,3},{19,27},{12,4},{... | collective-permute-start | bytes 1572872 | tf_op jit(solution)/shard_map/ppermute | solution.py:980
  197.9 18.0 %collective-permute-start.31 = (bf16[1408,128]{1,0:T(8,128)(2,1)S(1)}, bf16[1408,128]{1,0:T(8,128)(2,1)S(1)}, u32[]{:S(2)}, u32[]{:S(2)}) collective-permute-start(bf16[1408,128]{1,0:T(8,128)(2,1)S(1)} %add_convert_fusion.9), channel_id=1, source_target_pairs={{8,16},{16,8},{9,17},{17,9},{10,18},{18,10},{11,19},{19,11},{12,20... | collective-permute-start | bytes 1081352 | tf_op jit(solution)/shard_map/ppermute | solution.py:980
  198.7 6.1 %copy-start.1 = (bf16[1024,1152]{1,0:T(8,128)(2,1)S(1)}, bf16[1024,1152]{1,0:T(8,128)(2,1)}, u32[]{:S(2)}) copy-start(bf16[1024,1152]{1,0:T(8,128)(2,1)} %copy-done) | copy-start | bytes 7077892
  204.0 27.1 %collective-permute-start.36 = (bf16[768,384]{1,0:T(8,128)(2,1)S(1)}, bf16[768,384]{1,0:T(8,128)(2,1)S(1)}, u32[]{:S(2)}, u32[]{:S(2)}) collective-permute-start(bf16[768,384]{1,0:T(8,128)(2,1)S(1)} %add_convert_fusion.5), channel_id=1, source_target_pairs={{8,16},{16,8},{9,17},{17,9},{10,18},{18,10},{11,19},{19,11},{12,20... | collective-permute-start | bytes 1769480 | tf_op jit(solution)/shard_map/ppermute | solution.py:980
  215.9 16.2 %collective-permute-start.37 = (bf16[384,768]{1,0:T(8,128)(2,1)S(1)}, bf16[384,768]{1,0:T(8,128)(2,1)S(1)}, u32[]{:S(2)}, u32[]{:S(2)}) collective-permute-start(bf16[384,768]{1,0:T(8,128)(2,1)S(1)} %add_convert_fusion.4), channel_id=1, source_target_pairs={{8,16},{16,8},{9,17},{17,9},{10,18},{18,10},{11,19},{19,11},{12,20... | collective-permute-start | bytes 1769480 | tf_op jit(solution)/shard_map/ppermute | solution.py:980
  217.0 12.8 %copy-start.35 = (bf16[1408,128]{1,0:T(8,128)(2,1)}, bf16[1408,128]{1,0:T(8,128)(2,1)S(1)}, u32[]{:S(2)}) copy-start(bf16[1408,128]{1,0:T(8,128)(2,1)S(1)} %add_convert_fusion.8) | copy-start | bytes 1081348
  222.6 24.9 %collective-permute-start.34 = (bf16[2304,128]{1,0:T(8,128)(2,1)S(1)}, bf16[2304,128]{1,0:T(8,128)(2,1)S(1)}, u32[]{:S(2)}, u32[]{:S(2)}) collective-permute-start(bf16[2304,128]{1,0:T(8,128)(2,1)S(1)} %encoder_mixing_grads.1), channel_id=1, source_target_pairs={{0,8},{24,16},{1,9},{25,17},{2,10},{26,18},{3,11},{27,19},{4,12},{... | collective-permute-start | bytes 1769480 | tf_op jit(solution)/shard_map/ppermute | solution.py:964
  229.8 13.2 %collective-permute-start.35 = (bf16[1408,128]{1,0:T(8,128)(2,1)S(1)}, bf16[1408,128]{1,0:T(8,128)(2,1)S(1)}, u32[]{:S(2)}, u32[]{:S(2)}) collective-permute-start(bf16[1408,128]{1,0:T(8,128)(2,1)S(1)} %add_convert_fusion.8), channel_id=1, source_target_pairs={{8,0},{16,24},{9,1},{17,25},{10,2},{18,26},{11,3},{19,27},{12,4},{... | collective-permute-start | bytes 1081352 | tf_op jit(solution)/shard_map/ppermute | solution.py:980
  232.1 21.4 %collective-permute-start.39 = (bf16[768,384]{1,0:T(8,128)(2,1)}, bf16[768,384]{1,0:T(8,128)(2,1)}, u32[]{:S(2)}, u32[]{:S(2)}) collective-permute-start(bf16[768,384]{1,0:T(8,128)(2,1)} %add_convert_fusion.3), channel_id=1, source_target_pairs={{8,0},{16,24},{9,1},{17,25},{10,2},{18,26},{11,3},{19,27},{12,4},{... | collective-permute-start | bytes 1769480 | tf_op jit(solution)/shard_map/ppermute | solution.py:980
  251.0 2.5 collective-permute-start.40
  251.0 14.0 %collective-permute-start.38 = (bf16[2304,128]{1,0:T(8,128)(2,1)}, bf16[2304,128]{1,0:T(8,128)(2,1)S(1)}, u32[]{:S(2)}, u32[]{:S(2)}) collective-permute-start(bf16[2304,128]{1,0:T(8,128)(2,1)} %add_convert_fusion.1), channel_id=1, source_target_pairs={{8,16},{16,8},{9,17},{17,9},{10,18},{18,10},{11,19},{19,11},{12,20... | collective-permute-start | bytes 1769480 | tf_op jit(solution)/shard_map/ppermute | solution.py:980
  251.7 17.8 %collective-permute-start.47 = (bf16[384,768]{1,0:T(8,128)(2,1)}, bf16[384,768]{1,0:T(8,128)(2,1)S(1)}, u32[]{:S(2)}, u32[]{:S(2)}) collective-permute-start(bf16[384,768]{1,0:T(8,128)(2,1)} %add_convert_fusion.2), channel_id=1, source_target_pairs={{8,0},{16,24},{9,1},{17,25},{10,2},{18,26},{11,3},{19,27},{12,4},{... | collective-permute-start | bytes 1769480 | tf_op jit(solution)/shard_map/ppermute | solution.py:980
  253.5 11.4 %copy-start.32 = (bf16[2304,128]{1,0:T(8,128)(2,1)S(1)}, bf16[2304,128]{1,0:T(8,128)(2,1)}, u32[]{:S(2)}) copy-start(bf16[2304,128]{1,0:T(8,128)(2,1)} %add_convert_fusion.1) | copy-start | bytes 1769476
  255.7 13.9 %copy-start.36 = (bf16[1408,128]{1,0:T(8,128)(2,1)S(1)}, bf16[1408,128]{1,0:T(8,128)(2,1)}, u32[]{:S(2)}) copy-start(bf16[1408,128]{1,0:T(8,128)(2,1)} %copy-done.35) | copy-start | bytes 1081348
  255.7 13.9 %copy-start.42 = (bf16[1408,128]{1,0:T(8,128)(2,1)S(1)}, bf16[1408,128]{1,0:T(8,128)(2,1)}, u32[]{:S(2)}) copy-start(bf16[1408,128]{1,0:T(8,128)(2,1)} %copy-done.41) | copy-start | bytes 1081348
  265.1 23.0 %collective-permute-start.46 = (bf16[2304,128]{1,0:T(8,128)(2,1)S(1)}, bf16[2304,128]{1,0:T(8,128)(2,1)S(1)}, u32[]{:S(2)}, u32[]{:S(2)}) collective-permute-start(bf16[2304,128]{1,0:T(8,128)(2,1)S(1)} %add_convert_fusion), channel_id=1, source_target_pairs={{8,0},{16,24},{9,1},{17,25},{10,2},{18,26},{11,3},{19,27},{12,4},{... | collective-permute-start | bytes 1769480 | tf_op jit(solution)/shard_map/ppermute | solution.py:980
  270.3 5.1 %collective-permute-start.42 = (bf16[1536,128]{1,0:T(8,128)(2,1)S(1)}, bf16[1536,128]{1,0:T(8,128)(2,1)S(1)}, u32[]{:S(2)}, u32[]{:S(2)}) collective-permute-start(bf16[1536,128]{1,0:T(8,128)(2,1)S(1)} %decoder_send.1), channel_id=1, source_target_pairs={{0,1},{1,0},{2,3},{3,2},{4,5},{5,4},{6,7},{7,6},{8,9},{9,8},{10,11... | collective-permute-start | bytes 1179656 | tf_op jit(solution)/shard_map/ppermute | solution.py:155
  272.0 1.7 collective-permute-start.41
  277.2 6.3 %collective-permute-start.43 = (f32[8,768]{1,0:T(8,128)S(1)}, f32[8,768]{1,0:T(8,128)S(1)}, u32[]{:S(2)}, u32[]{:S(2)}) collective-permute-start(f32[8,768]{1,0:T(8,128)S(1)} %bitcast_reduce_fusion), channel_id=1, source_target_pairs={{0,24},{8,0},{16,8},{24,16},{1,25},{9,1},{17,9},{25,17},{2,26},{10... | collective-permute-start | bytes 73736 | tf_op jit(solution)/shard_map/ppermute | solution.py:1002
  280.7 5.3 %collective-permute-start.44 = (f32[8,768]{1,0:T(8,128)S(1)}, f32[8,768]{1,0:T(8,128)S(1)}, u32[]{:S(2)}, u32[]{:S(2)}) collective-permute-start(f32[8,768]{1,0:T(8,128)S(1)} %bitcast_reduce_fusion), channel_id=1, source_target_pairs={{0,16},{8,24},{16,0},{24,8},{1,17},{9,25},{17,1},{25,9},{2,18},{10... | collective-permute-start | bytes 73736 | tf_op jit(solution)/shard_map/ppermute | solution.py:1002
  281.2 5.6 %collective-permute-start.45 = (f32[8,768]{1,0:T(8,128)S(1)}, f32[8,768]{1,0:T(8,128)S(1)}, u32[]{:S(2)}, u32[]{:S(2)}) collective-permute-start(f32[8,768]{1,0:T(8,128)S(1)} %bitcast_reduce_fusion), channel_id=1, source_target_pairs={{0,8},{8,16},{16,24},{24,0},{1,9},{9,17},{17,25},{25,1},{2,10},{10... | collective-permute-start | bytes 73736 | tf_op jit(solution)/shard_map/ppermute | solution.py:1002
  (29 other events, 98.4 us)
